TPU v7x, 128 devices: a whole 4x4x4 slice. The times are simulated.
128 devices in a mesh: grp: 4 (over y), tile: 32 (over z, x, core).
Axes of the slice: x: 4, y: 4, z: 4, core: 2. Of those that a mesh axis runs over, the one named last changes fastest.
Arguments:
- screens: bfloat16 [3, 131072, 256], P(None, ('grp', 'tile')), may hold values from -4 to 4
- interp_weights: bfloat16 [3, 4, 256, 256], replicated, may hold values from -0.375 to 0.375
- footprint: int32 [32768, 3, 4], P(('grp', 'tile')), may hold values from 0 to 131071, as said below
- illumination: float32 [32768, 256], P(('grp', 'tile')), may hold values from 0.3 to 1
- cm_values: bfloat16 [896, 16, 16, 2, 128], P('tile', 'grp'), may hold values from -0.09375 to 0.09375
- cm_columns: int32 [896, 16], P('tile', 'grp'), may hold values from 0 to 255, as said below
- prev_commands: float32 [14336], P('tile'), may hold values from 0 to 5
- owner_map: int32 [14336], P('tile'), may hold values from 0 to 2, as said below
- dm_gain: float32 [3], replicated, may hold values from 0.2 to 1
Outputs:
- slopes: float32 [2, 32768], P(None, ('grp', 'tile'))
- commands: float32 [14336], P('tile')
Inputs may be any that keep to these rules, and one draw needn't show every extreme that they name: `footprint`: the blocks of subaperture s lie among the 1024 blocks of the device holding s and the 256 blocks on either side of them, counted cyclically over all 131072 blocks; some subaperture reaches each end. `cm_columns`: nonzero block n names a column block from (n // 4) * 64 up to that plus 64 - 1. `owner_map`: every mirror owns some actuator.
All inputs are finite; a program needn't handle non-finite values.
Results may differ from a plain program's by a relative error of at most 0.0024.
Values may be sent and summed in bfloat16 or wider, within the bound.
No kernel may reach another device: no remote copies, remote signals or barrier semaphores. Data moves between devices by JAX's collectives and lax.ppermute only.
A program may use at most 64 MiB of HBM per device.

v0:
```python
import math

import jax
import jax.numpy as jnp
from jax import lax
from jax.sharding import PartitionSpec as P

SIDE = 16


def from_behind(block, axis, distance):
    devices = range(lax.axis_size(axis))
    route = [((i - distance) % len(devices), i) for i in devices]
    return lax.ppermute(block, axis, route)


def spectrum_tables(side):
    pixels = side * side
    index = jnp.arange(pixels, dtype=jnp.int32)
    row_ids = index // side
    col_ids = index % side
    turns = (row_ids[:, None] * row_ids[None, :] + col_ids[:, None] * col_ids[None, :]) % side
    angle = turns.astype(jnp.float32) * (2.0 * math.pi / side)
    cosine = jnp.cos(angle)
    sine = jnp.sin(angle)
    table = jnp.concatenate(
        [jnp.concatenate([cosine, -sine], 1), jnp.concatenate([sine, cosine], 1)], 0
    )
    half = side // 2
    centre_v = (col_ids - side * (col_ids >= half).astype(jnp.int32)).astype(jnp.float32)
    centre_u = (row_ids - side * (row_ids >= half).astype(jnp.int32)).astype(jnp.float32)
    return (table.astype(jnp.bfloat16), centre_v, centre_u)


def mirror_update(recon, prev_part, owner_part, dm_gain):
    mirrors = dm_gain.shape[0]
    onehot = (owner_part[:, None] == jnp.arange(mirrors, dtype=jnp.int32)[None, :]).astype(
        jnp.float32
    )
    gains = jnp.sum(onehot * dm_gain[None, :], axis=1)
    updated = prev_part - gains * recon
    sums = jnp.sum(onehot * updated[:, None], axis=0)
    counts = jnp.sum(onehot, axis=0)
    return (onehot, updated, sums, counts)


def on_device(
    screens,
    interp_weights,
    footprint,
    illumination,
    cm_values,
    cm_columns,
    prev_commands,
    owner_map,
    dm_gain,
):
    layers, blk_dev, pixels = screens.shape
    sub_dev = footprint.shape[0]
    foot = footprint.shape[2]
    devices = lax.axis_size(("grp", "tile"))
    here = lax.axis_index(("grp", "tile"))
    before = from_behind(screens, ("grp", "tile"), 1)
    after = from_behind(screens, ("grp", "tile"), -1)
    extended = jnp.concatenate([before, screens, after], axis=1)
    start = here * blk_dev - blk_dev
    local_ids = jnp.mod(footprint - start, blk_dev * devices)
    picked = jnp.stack(
        [jnp.take(extended[layer], local_ids[:, layer, :], axis=0) for layer in range(layers)],
        axis=1,
    )
    picked = picked.reshape(sub_dev, layers * foot * pixels)
    weights_flat = interp_weights.reshape(layers * foot * pixels, pixels)
    phase = jnp.dot(picked, weights_flat, preferred_element_type=jnp.float32)
    side = SIDE
    table, centre_v, centre_u = spectrum_tables(side)
    field = jnp.concatenate(
        [illumination * jnp.cos(phase), illumination * jnp.sin(phase)], 1
    ).astype(jnp.bfloat16)
    spectrum = jnp.dot(field, table, preferred_element_type=jnp.float32)
    real_part = spectrum[:, :pixels]
    imag_part = spectrum[:, pixels:]
    intensity = real_part * real_part + imag_part * imag_part
    total = jnp.sum(intensity, axis=1)
    slope_x = jnp.sum(intensity * centre_v[None, :], axis=1) / total
    slope_y = jnp.sum(intensity * centre_u[None, :], axis=1) / total
    slopes = jnp.stack([slope_x, slope_y], 0)
    slope_words = slopes.astype(jnp.bfloat16)
    block_width = cm_values.shape[4]
    gathered = lax.all_gather(slope_words, "tile", axis=1, tiled=True)
    column_base = lax.axis_index("grp") * (gathered.shape[1] // block_width)
    blocks = gathered.reshape(2, gathered.shape[1] // block_width, block_width)
    chosen = jnp.take(blocks, cm_columns - column_base, axis=1)
    partial_value = jnp.einsum(
        "rjics,crjs->ri", cm_values, chosen, preferred_element_type=jnp.float32
    ).reshape(-1)
    recon = lax.psum(partial_value, "grp")
    onehot, updated, sums, counts = mirror_update(recon, prev_commands, owner_map, dm_gain)
    total_sums, total_counts = lax.psum((sums, counts), "tile")
    piston = total_sums / total_counts
    commands = updated - jnp.sum(onehot * piston[None, :], axis=1)
    return (slopes, commands)


def solution(mesh):
    in_specs = (
        P(None, ("grp", "tile"), None),
        P(),
        P(("grp", "tile"), None, None),
        P(("grp", "tile"), None),
        P("tile", "grp", None, None, None),
        P("tile", "grp"),
        P("tile"),
        P("tile"),
        P(),
    )
    out_specs = (P(None, ("grp", "tile")), P("tile"))
    return jax.shard_map(
        on_device, mesh=mesh, in_specs=in_specs, out_specs=out_specs, check_vma=False
    )
```

profile of v0, /device:TPU:1, one launch (start us, length us, event | category | flops | bytes accessed | tf_op | source)
XLA Modules:
  0.0 156.8 jit_solution(6138320368479981204)
XLA Ops:
  0.6 2.7 %collective-permute-start = (bf16[3,1024,256]{2,1,0:T(8,128)(2,1)}, bf16[3,1024,256]{2,1,0:T(8,128)(2,1)}, u32[]{:S(2)}, u32[]{:S(2)}) collective-permute-start(bf16[3,1024,256]{2,1,0:T(8,128)(2,1)} %param.11), channel_id=1, source_target_pairs={{127,0},{0,1},{1,2},{2,3},{3,4},{4,5},{5,6},{6,7},{7,8},{8,9},{9,1... | collective-permute-start | bytes 4718600 | tf_op jit(solution)/shard_map/ppermute | solution.py:14
  3.3 0.7 add_select_fusion.1
  4.0 0.7 compare_and_fusion.3
  4.7 0.6 and_select_fusion
  6.1 1.1 copy.34
  7.4 0.7 copy.36
  8.7 1.4 select_reduce_fusion.2
  10.7 2.7 %negate_convert_fusion = (bf16[256,256]{1,0:T(8,128)(2,1)S(1)}, bf16[256,256]{1,0:T(8,128)(2,1)}, bf16[256,256]{1,0:T(8,128)(2,1)}) fusion(s32[256]{0:T(256)} %get-tuple-element.30, s32[256]{0:T(256)} %get-tuple-element.31), kind=kLoop, calls=%fused_computation.44 | loop fusion | flops 1310720 | bytes 395264 | tf_op jit(solution)/shard_map/convert.5
  13.4 7.6 %collective-permute-done = bf16[3,1024,256]{2,1,0:T(8,128)(2,1)} collective-permute-done((bf16[3,1024,256]{2,1,0:T(8,128)(2,1)}, bf16[3,1024,256]{2,1,0:T(8,128)(2,1)}, u32[]{:S(2)}, u32[]{:S(2)}) %collective-permute-start) | collective-permute-done | bytes 1572896 | tf_op jit(solution)/shard_map/ppermute | solution.py:14
  21.0 1.5 constant_dynamic-update-slice_fusion.2
  22.6 1.1 collective-permute-done.1
  23.9 2.0 %slice_bitcast_fusion.2 = (bf16[3072,256]{1,0:T(8,128)(2,1)S(1)}, bf16[3072,256]{1,0:T(8,128)(2,1)}, bf16[3072,256]{1,0:T(8,128)(2,1)}) fusion(bf16[3,3072,256]{2,1,0:T(8,128)(2,1)S(1)} %constant_dynamic-update-slice_fusion), kind=kLoop, calls=%fused_computation.6 | loop fusion | bytes 9437184 | tf_op jit(solution)/shard_map/squeeze | solution.py:69
  25.8 6.2 %gather_fusion.3 = bf16[1024,256]{1,0:T(8,128)(2,1)} fusion(bf16[3072,256]{1,0:T(8,128)(2,1)} %get-tuple-element.15, s32[1024]{0:T(1024)S(1)} %get-tuple-element.32), kind=kCustom, calls=%fused_computation.2.clone | custom fusion | bytes 1052672 | tf_op jit(solution)/shard_map/jit(_take)/gather | solution.py:69
  32.0 2.0 %reshape.159 = bf16[256,4,256]{2,1,0:T(4,128)(2,1)} reshape(bf16[1024,256]{1,0:T(8,128)(2,1)} %gather_fusion.3) | data formatting | bytes 1048576 | tf_op jit(solution)/shard_map/jit(_take)/gather | solution.py:69
  34.0 6.2 %gather_fusion.2 = bf16[1024,256]{1,0:T(8,128)(2,1)} fusion(bf16[3072,256]{1,0:T(8,128)(2,1)} %get-tuple-element.16, s32[1024]{0:T(1024)S(1)} %get-tuple-element.33), kind=kCustom, calls=%fused_computation.1.clone | custom fusion | bytes 1052672 | tf_op jit(solution)/shard_map/jit(_take)/gather | solution.py:69
  40.1 2.0 %reshape.155 = bf16[256,4,256]{2,1,0:T(4,128)(2,1)} reshape(bf16[1024,256]{1,0:T(8,128)(2,1)} %gather_fusion.2) | data formatting | bytes 1048576 | tf_op jit(solution)/shard_map/jit(_take)/gather | solution.py:69
  42.1 4.9 %gather_fusion.1 = bf16[1024,256]{1,0:T(8,128)(2,1)} fusion(bf16[3072,256]{1,0:T(8,128)(2,1)S(1)} %get-tuple-element.14, s32[1024]{0:T(1024)S(1)} %broadcast_clamp_fusion.2), kind=kCustom, calls=%fused_computation.clone | custom fusion | bytes 1052672 | tf_op jit(solution)/shard_map/jit(_take)/gather | solution.py:69
  47.0 1.2 reshape.151
  48.2 1.2 fusion.19
  50.0 1.6 %multiply_convert_fusion.1 = (bf16[256,256]{0,1:T(8,128)(2,1)S(1)}, bf16[256,256]{0,1:T(8,128)(2,1)S(1)}) fusion(f32[256,256]{0,1:T(8,128)S(1)} %copy.34, bf16[3,4,256,256]{3,2,1,0:T(8,128)(2,1)S(1)} %copy-done, bf16[256,1,4,256]{3,0,2,1:T(8,128)(2,1)S(1)} %fusion.19, bf16[256,1,4,256]{3,0,2,1:T(8,128)(2,1)S(1)} %fusion.20, ...), kind=kOutput, calls=%fused_computation.47 | convolution fusion | flops 404488192 | bytes 3670016 | tf_op jit(solution)/shard_map/dot_general | solution.py:74
  53.1 27.5 %all_gather.3 = bf16[2,8192]{1,0:T(2,128)(2,1)S(1)} all-gather(bf16[2,256]{1,0:T(2,128)(2,1)S(1)} %get-tuple-element.12), channel_id=1, replica_groups=mesh['grp'=4,'tile'=32] {'tile'}, dimensions={1}, use_global_device_ids=true | all-gather | bytes 33792 | tf_op jit(solution)/shard_map/all_gather | solution.py:90
  80.6 0.7 gather_fusion
  82.1 9.6 %psum.21 = f32[448]{0:T(512)S(1)} all-reduce(f32[448]{0:T(512)S(1)} %reshape.107), channel_id=1, replica_groups=mesh['grp'=4,'tile'=32] {'grp'}, use_global_device_ids=true, to_apply=%region_4.6 | all-reduce | flops 448 | bytes 3584 | tf_op jit(solution)/shard_map/psum | solution.py:97
  91.9 64.2 %all-reduce = (f32[3]{0:T(128)S(1)}, f32[3]{0:T(128)S(1)}) all-reduce(f32[3]{0:T(128)S(1)} %get-tuple-element.7, f32[3]{0:T(128)S(1)} %get-tuple-element.6), channel_id=1, replica_groups=mesh['grp'=4,'tile'=32] {'tile'}, use_global_device_ids=true, to_apply=%region_6.8 | all-reduce | flops 6 | bytes 48 | tf_op jit(solution)/shard_map/psum | solution.py:99
  (60 shorter events, 5.8 us)
Async XLA Ops:
  0.6 49.3 %copy-start = (bf16[3,4,256,256]{3,2,1,0:T(8,128)(2,1)S(1)}, bf16[3,4,256,256]{3,2,1,0:T(8,128)(2,1)}, u32[]{:S(2)}) copy-start(bf16[3,4,256,256]{3,2,1,0:T(8,128)(2,1)} %param.12) | copy-start | bytes 4718596
  0.6 20.3 %collective-permute-start = (bf16[3,1024,256]{2,1,0:T(8,128)(2,1)}, bf16[3,1024,256]{2,1,0:T(8,128)(2,1)}, u32[]{:S(2)}, u32[]{:S(2)}) collective-permute-start(bf16[3,1024,256]{2,1,0:T(8,128)(2,1)} %param.11), channel_id=1, source_target_pairs={{127,0},{0,1},{1,2},{2,3},{3,4},{4,5},{5,6},{6,7},{7,8},{8,9},{9,1... | collective-permute-start | bytes 4718600 | tf_op jit(solution)/shard_map/ppermute | solution.py:14
  3.3 20.5 %collective-permute-start.1 = (bf16[3,1024,256]{2,1,0:T(8,128)(2,1)}, bf16[3,1024,256]{2,1,0:T(8,128)(2,1)S(1)}, u32[]{:S(2)}, u32[]{:S(2)}) collective-permute-start(bf16[3,1024,256]{2,1,0:T(8,128)(2,1)} %param.11), channel_id=1, source_target_pairs={{1,0},{2,1},{3,2},{4,3},{5,4},{6,5},{7,6},{8,7},{9,8},{10,9},{11,1... | collective-permute-start | bytes 4718600 | tf_op jit(solution)/shard_map/ppermute | solution.py:14
  13.4 9.1 %copy-start.2 = (bf16[3,1024,256]{2,1,0:T(8,128)(2,1)S(1)}, bf16[3,1024,256]{2,1,0:T(8,128)(2,1)}, u32[]{:S(2)}) copy-start(bf16[3,1024,256]{2,1,0:T(8,128)(2,1)} %param.11) | copy-start | bytes 4718596
  47.0 2.5 %copy-start.1 = (bf16[256,4,256]{2,1,0:T(4,128)(2,1)S(1)}, bf16[256,4,256]{2,1,0:T(4,128)(2,1)}, u32[]{:S(2)}) copy-start(bf16[256,4,256]{2,1,0:T(4,128)(2,1)} %reshape.155) | copy-start | bytes 1572868
  47.0 2.5 %copy-start.11 = (pred[256,4]{0,1:T(4,128)(4,1)S(1)}, pred[256,4]{0,1:T(4,128)(4,1)}, u32[]{:S(2)}) copy-start(pred[256,4]{0,1:T(4,128)(4,1)} %get-tuple-element.21) | copy-start | bytes 3076
  47.0 2.7 %copy-start.10 = (pred[256,4]{0,1:T(4,128)(4,1)S(1)}, pred[256,4]{0,1:T(4,128)(4,1)}, u32[]{:S(2)}) copy-start(pred[256,4]{0,1:T(4,128)(4,1)} %get-tuple-element.19) | copy-start | bytes 3076
  50.0 1.7 %copy-start.3 = (bf16[256,256]{1,0:T(8,128)(2,1)S(1)}, bf16[256,256]{1,0:T(8,128)(2,1)}, u32[]{:S(2)}) copy-start(bf16[256,256]{1,0:T(8,128)(2,1)} %get-tuple-element.26) | copy-start | bytes 393220
  50.0 1.7 %copy-start.4 = (bf16[256,256]{1,0:T(8,128)(2,1)S(1)}, bf16[256,256]{1,0:T(8,128)(2,1)}, u32[]{:S(2)}) copy-start(bf16[256,256]{1,0:T(8,128)(2,1)} %get-tuple-element.27) | copy-start | bytes 393220
  51.6 0.7 copy-start.8
  51.6 0.7 copy-start.9
  51.6 29.7 %copy-start.6 = (pred[28,4]{1,0:T(8,128)(4,1)S(1)}, pred[28,4]{1,0:T(8,128)(4,1)}, u32[]{:S(2)}) copy-start(pred[28,4]{1,0:T(8,128)(4,1)} %copy.36) | copy-start | bytes 340
  51.7 29.9 %copy-start.13 = (bf16[28,4,16,2,128]{4,3,2,1,0:T(2,128)(2,1)S(1)}, bf16[28,4,16,2,128]{4,3,2,1,0:T(2,128)(2,1)}, u32[]{:S(2)}) copy-start(bf16[28,4,16,2,128]{4,3,2,1,0:T(2,128)(2,1)} %param.15) | copy-start | bytes 2752516
  52.0 39.7 %copy-start.7 = (f32[448]{0:T(512)S(1)}, f32[448]{0:T(512)}, u32[]{:S(2)}) copy-start(f32[448]{0:T(512)} %select_reduce_fusion.2) | copy-start | bytes 5380
  52.0 39.7 %copy-start.12 = (f32[448]{0:T(512)S(1)}, f32[448]{0:T(512)}, u32[]{:S(2)}) copy-start(f32[448]{0:T(512)} %param.17) | copy-start | bytes 5380
  52.0 39.7 %copy-start.5 = (s32[448]{0:T(512)S(1)}, s32[448]{0:T(512)}, u32[]{:S(2)}) copy-start(s32[448]{0:T(512)} %param.18) | copy-start | bytes 5380
where the time goes:
time: 157 us
  blocking collectives  101 us (64%)
  local copies, waits for them, and re-layouts  29.9 us (19%)
  other arithmetic  10.7 us (7%)
  waiting for transfers between devices  8.73 us (6%)
  starting transfers between devices  2.66 us (2%)
  matrix products  2.42 us (2%)
    psum x1, blocking collectives, on_device(): total_sums, total_counts = lax.psum((sums, counts), 'tile')  64.2 us
    all_gather x1, blocking collectives, on_device(): gathered = lax.all_gather(slope_words, 'tile', axis=1, tiled=True)  27.5 us
    gather x6, local copies, waits for them, and re-layouts, on_device(): jnp.take(extended[layer], local_ids[:, layer, :], axis=0)  22.4 us
    psum x1, blocking collectives, on_device(): recon = lax.psum(partial_value, 'grp')  9.6 us
    ppermute x2, waiting for transfers between devices, from_behind(): return lax.ppermute(block, axis, route)  8.73 us
  transfers between devices with their start and end apart: 2, of which 2 were waited for; matrix products, arithmetic and copies ran while one was open for 7% of the time, Pallas kernels for 0%

commit v1 on v0

v1 whole, which is shorter than its diff:
```python
import math

import jax
import jax.numpy as jnp
import numpy as np
from jax import lax
from jax.experimental import pallas as pl
from jax.experimental.pallas import tpu as pltpu
from jax.sharding import PartitionSpec as P

SIDE = 16
DEVICES = ("grp", "tile")
LANES = 128
TILE_ROWS = 256


def from_behind(block, axis, distance):
    devices = range(lax.axis_size(axis))
    route = [((i - distance) % len(devices), i) for i in devices]
    return lax.ppermute(block, axis, route)


def transform_table(side):
    index = np.arange(side * side)
    rows, cols = index // side, index % side
    turns = (rows[:, None] * rows[None, :] + cols[:, None] * cols[None, :]) % side
    angle = turns.astype(np.float32) * np.float32(2.0 * math.pi / side)
    cosine, sine = np.cos(angle), np.sin(angle)
    table = np.concatenate(
        [np.concatenate([cosine, -sine], 1), np.concatenate([sine, cosine], 1)], 0
    )
    return jnp.asarray(table.T.astype(jnp.bfloat16))


def pick(offsets, block, blocks):
    rows = offsets.shape[0]
    lane = lax.broadcasted_iota(jnp.int32, (rows, TILE_ROWS), 1).astype(jnp.float32)
    hit = jnp.where(lane == offsets - float(block * TILE_ROWS), 1.0, 0.0).astype(jnp.bfloat16)
    return jnp.dot(hit, blocks, preferred_element_type=jnp.float32)


def offsets_of(foot_rows, start, total):
    away = foot_rows - start
    away = jnp.where(away < -(total // 2), away + total, away)
    away = jnp.where(away >= total // 2, away - total, away)
    away = away.astype(jnp.float32)
    foot, subs = away.shape
    filled = jnp.concatenate([away, jnp.zeros((8 - foot, subs), jnp.float32)], 0)
    return filled.T


def sense_own(start_ref, foot_ref, screens_ref, weights_ref, phase_ref, *, total):
    offsets = offsets_of(foot_ref[0], start_ref[0], total)
    foot = foot_ref.shape[1]
    blocks = screens_ref.shape[1] // TILE_ROWS
    phase = jnp.zeros(phase_ref.shape, jnp.float32)
    for k in range(foot):
        column = jnp.broadcast_to(offsets[:, k : k + 1], (offsets.shape[0], TILE_ROWS))
        picked = None
        for b in range(blocks):
            part = pick(column, b, screens_ref[0, b * TILE_ROWS : (b + 1) * TILE_ROWS, :])
            picked = part if picked is None else picked + part
        phase = phase + jnp.dot(
            picked.astype(jnp.bfloat16), weights_ref[0, k], preferred_element_type=jnp.float32
        )

    @pl.when(pl.program_id(0) == 0)
    def _():
        phase_ref[...] = phase

    @pl.when(pl.program_id(0) != 0)
    def _():
        phase_ref[...] = phase_ref[...] + phase


def sense_rest(
    start_ref, foot_ref, before_ref, after_ref, weights_ref, phase_ref, illum_ref, table_ref,
    slopes_ref, words_ref, *, total, own
):
    layers, foot, subs = foot_ref.shape
    phase = phase_ref[...]
    for layer in range(layers):
        offsets = offsets_of(foot_ref[layer], start_ref[0], total)
        for k in range(foot):
            column = jnp.broadcast_to(offsets[:, k : k + 1], (subs, TILE_ROWS))
            picked = pick(column, -1, before_ref[layer]) + pick(column, own, after_ref[layer])
            phase = phase + jnp.dot(
                picked.astype(jnp.bfloat16),
                weights_ref[layer, k],
                preferred_element_type=jnp.float32,
            )
    pixels = phase.shape[1]
    phase = phase.T
    illum = illum_ref[...].T
    field = jnp.concatenate([illum * jnp.cos(phase), illum * jnp.sin(phase)], 0)
    spectrum = jnp.dot(
        table_ref[...], field.astype(jnp.bfloat16), preferred_element_type=jnp.float32
    )
    real_part = spectrum[:pixels]
    imag_part = spectrum[pixels:]
    intensity = real_part * real_part + imag_part * imag_part
    row = lax.broadcasted_iota(jnp.int32, intensity.shape, 0)
    cv = row % SIDE
    cu = row // SIDE
    cv = (cv - SIDE * (cv >= SIDE // 2).astype(jnp.int32)).astype(jnp.float32)
    cu = (cu - SIDE * (cu >= SIDE // 2).astype(jnp.int32)).astype(jnp.float32)
    count = jnp.sum(intensity, axis=0, keepdims=True)
    slope_x = jnp.sum(intensity * cv, axis=0, keepdims=True) / count
    slope_y = jnp.sum(intensity * cu, axis=0, keepdims=True) / count
    slopes = jnp.concatenate([slope_x, slope_y], 0)
    slopes_ref[...] = slopes
    words = slopes.astype(jnp.bfloat16).astype(jnp.float32)
    rows = [words[:, h * LANES : (h + 1) * LANES] for h in range(subs // LANES)]
    words_ref[...] = jnp.broadcast_to(jnp.concatenate(rows, 0)[None], words_ref.shape)


def reconstruct(words_ref, cm_ref, rows_ref, owner_ref, prev_ref, gain_ref, sent_ref, *, share):
    words = words_ref[...].astype(jnp.bfloat16)
    positions = cm_ref.shape[0]
    width = cm_ref.shape[1]
    row = lax.broadcasted_iota(jnp.int32, (words.shape[0], width), 0)
    total = jnp.zeros((words.shape[0], width), jnp.float32)
    for n in range(positions):
        for c in range(2):
            product = lax.dot_general(
                words,
                cm_ref[n, :, c * LANES : (c + 1) * LANES],
                (((1,), (1,)), ((), ())),
                preferred_element_type=jnp.float32,
            )
            total = total + jnp.where(row == rows_ref[n : n + 1, :] * 2 + c, product, 0.0)
    recon = jnp.sum(total, axis=0, keepdims=True)
    owner = owner_ref[...]
    lane = lax.broadcasted_iota(jnp.int32, (1, width), 1)
    mirrors = gain_ref.shape[0]
    line = recon
    for m in range(mirrors):
        mine = owner == m
        part = jnp.where(mine, prev_ref[...] * share - gain_ref[m] * recon, 0.0)
        line = jnp.where(lane == width - 2 * mirrors + m, jnp.sum(part, axis=1, keepdims=True), line)
        held = jnp.where(mine, share, 0.0)
        line = jnp.where(lane == width - mirrors + m, jnp.sum(held, axis=1, keepdims=True), line)
    rows = [line[:, i * LANES : (i + 1) * LANES] for i in range(width // LANES)]
    sent_ref[...] = jnp.broadcast_to(jnp.concatenate(rows, 0)[None], sent_ref.shape)


def settle(tile_ref, got_ref, owner_ref, prev_ref, gain_ref, commands_ref, *, groups):
    tiles = got_ref.shape[0] // groups
    recon = got_ref[tile_ref[0]]
    for g in range(1, groups):
        recon = recon + got_ref[g * tiles + tile_ref[0]]
    sums = jnp.sum(got_ref[...], axis=0)
    last = sums[sums.shape[0] - 1 :, :]
    lane = lax.broadcasted_iota(jnp.int32, last.shape, 1)
    owner = owner_ref[...]
    mirrors = gain_ref.shape[0]
    gains = jnp.zeros(owner.shape, jnp.float32)
    piston = jnp.zeros(owner.shape, jnp.float32)
    for m in range(mirrors):
        mine = owner == m
        total = jnp.sum(jnp.where(lane == LANES - 2 * mirrors + m, last, 0.0), axis=1, keepdims=True)
        count = jnp.sum(jnp.where(lane == LANES - mirrors + m, last, 0.0), axis=1, keepdims=True)
        gains = jnp.where(mine, gain_ref[m], gains)
        piston = jnp.where(mine, total / count, piston)
    commands_ref[...] = prev_ref[...] - gains * recon - piston


def on_device(
    screens,
    interp_weights,
    footprint,
    illumination,
    cm_values,
    cm_columns,
    prev_commands,
    owner_map,
    dm_gain,
):
    layers, blk_dev, pixels = screens.shape
    subs, _, foot = footprint.shape
    groups, tiles = lax.axis_size("grp"), lax.axis_size("tile")
    total = blk_dev * groups * tiles
    here = lax.axis_index(DEVICES)
    reach = TILE_ROWS
    smem = pl.BlockSpec(memory_space=pltpu.SMEM)
    limit = pltpu.CompilerParams(vmem_limit_bytes=24 * 2**20)

    before = from_behind(screens[:, blk_dev - reach :], DEVICES, 1)
    after = from_behind(screens[:, :reach], DEVICES, -1)

    start = (here * blk_dev).astype(jnp.int32).reshape(1)
    foot_rows = jnp.transpose(footprint, (1, 2, 0))
    phase = pl.pallas_call(
        lambda *refs: sense_own(*refs, total=total),
        grid=(layers,),
        in_specs=[
            smem,
            pl.BlockSpec((1, foot, subs), lambda i: (i, 0, 0)),
            pl.BlockSpec((1, blk_dev, pixels), lambda i: (i, 0, 0)),
            pl.BlockSpec((1, foot, pixels, pixels), lambda i: (i, 0, 0, 0)),
        ],
        out_specs=pl.BlockSpec((subs, pixels), lambda i: (0, 0)),
        out_shape=jax.ShapeDtypeStruct((subs, pixels), jnp.float32),
        compiler_params=limit,
        name="sense_own",
    )(start, foot_rows, screens, interp_weights)

    slopes, words = pl.pallas_call(
        lambda *refs: sense_rest(*refs, total=total, own=blk_dev // TILE_ROWS),
        in_specs=[smem] + [pl.BlockSpec(memory_space=pltpu.VMEM)] * 7,
        out_shape=(
            jax.ShapeDtypeStruct((2, subs), jnp.float32),
            jax.ShapeDtypeStruct((tiles, 2 * subs // LANES, LANES), jnp.float32),
        ),
        compiler_params=limit,
        name="sense_rest",
    )(start, foot_rows, before, after, interp_weights, phase, illumination, transform_table(SIDE))

    rowblk, positions, rb, comps, cbs = cm_values.shape
    acts = rowblk * rb
    mirrors = dm_gain.shape[0]
    width = -(-(acts + 2 * mirrors) // LANES) * LANES
    pad = width - acts
    cm = jnp.transpose(cm_values, (1, 0, 2, 3, 4)).reshape(positions, acts, comps * cbs)
    cm = jnp.pad(cm, ((0, 0), (0, pad), (0, 0)))
    column_base = lax.axis_index("grp") * (tiles * subs // cbs)
    rows = jnp.repeat((cm_columns - column_base).T, rb, axis=1)
    rows = jnp.pad(rows, ((0, 0), (0, pad)), constant_values=-1)
    owner = jnp.pad(owner_map, (0, pad), constant_values=-1)
    prev = jnp.pad(prev_commands, (0, pad))

    gathered = lax.all_to_all(words, "tile", 0, 0).reshape(-1, LANES)
    lines = width // LANES
    sent = pl.pallas_call(
        lambda *refs: reconstruct(*refs, share=1.0 / groups),
        in_specs=[pl.BlockSpec(memory_space=pltpu.VMEM)] * 5 + [smem],
        out_shape=jax.ShapeDtypeStruct((groups * tiles, lines, LANES), jnp.float32),
        compiler_params=limit,
        name="reconstruct",
    )(gathered, cm, rows, owner.reshape(1, width), prev.reshape(1, width), dm_gain)
    got = lax.all_to_all(sent, DEVICES, 0, 0)
    tile = lax.axis_index("tile").astype(jnp.int32).reshape(1)
    commands = pl.pallas_call(
        lambda *refs: settle(*refs, groups=groups),
        in_specs=[smem] + [pl.BlockSpec(memory_space=pltpu.VMEM)] * 3 + [smem],
        out_shape=jax.ShapeDtypeStruct((lines, LANES), jnp.float32),
        compiler_params=limit,
        name="settle",
    )(tile, got, owner.reshape(lines, LANES), prev.reshape(lines, LANES), dm_gain)
    return (slopes, commands.reshape(width)[:acts])


def solution(mesh):
    in_specs = (
        P(None, ("grp", "tile"), None),
        P(),
        P(("grp", "tile"), None, None),
        P(("grp", "tile"), None),
        P("tile", "grp", None, None, None),
        P("tile", "grp"),
        P("tile"),
        P("tile"),
        P(),
    )
    out_specs = (P(None, ("grp", "tile")), P("tile"))
    return jax.shard_map(
        on_device, mesh=mesh, in_specs=in_specs, out_specs=out_specs, check_vma=False
    )
```

time: 157 us -> 54.7 us (0.35)
  blocking collectives: 101 us -> 14.4 us
  local copies, waits for them, and re-layouts: 29.9 us -> 7.27 us
  Pallas kernels: 0 us -> 11.3 us
  other arithmetic: 10.7 us -> 0.01 us
  starting transfers between devices: 2.66 us -> 13.1 us
  matrix products: 2.42 us -> 0 us
    psum x2 -> x0, blocking collectives: 73.8 us -> none  [the longest x1 64.2 us: on_device(): total_sums, total_counts = lax.psum((sums, counts), 'tile')]
    all_gather x1 -> x0, blocking collectives: 27.5 us -> none  [on_device(): gathered = lax.all_gather(slope_words, 'tile', axis=1, tiled=True)]
    gather x7 -> x0, local copies, waits for them, and re-layouts: 23.1 us -> none  [the longest x6 22.4 us: on_device(): jnp.take(extended[layer], local_ids[:, layer, :], axis=0)]
    all_to_all x0 -> x1, blocking collectives: none -> 14.4 us  [on_device(): got = lax.all_to_all(sent, DEVICES, 0, 0)]
    pallas_call x0 -> x4, Pallas kernels: none -> 11.3 us  [the longest x1 4.91 us: on_device(): pl.pallas_call(lambda *refs: sense_own(*refs, total=total), grid=(layers,...]
    all_to_all x0 -> x1, starting transfers between devices: none -> 10.5 us  [on_device(): gathered = lax.all_to_all(words, 'tile', 0, 0).reshape(-1, LANES)]
    ppermute x2, waiting for transfers between devices: 8.73 us -> 0.01 us  [from_behind(): return lax.ppermute(block, axis, route)]
    all_to_all x0 -> x1, waiting for transfers between devices: none -> 7.41 us  [on_device(): gathered = lax.all_to_all(words, 'tile', 0, 0).reshape(-1, LANES)]
  transfers between devices with their start and end apart: 2 -> 3, of which waited for: 2 -> 1; matrix products, arithmetic and copies ran while one was open for 7% -> 7% of each run, Pallas kernels for 0% -> 9%
where the time goes in v1:
time: 54.7 us; the launch traced here: 54.4 us
  blocking collectives  14.4 us (26%)
  starting transfers between devices  13.1 us (24%)
  Pallas kernels  11.3 us (21%)
  waiting for transfers between devices  7.42 us (14%)
  local copies, waits for them, and re-layouts  7.27 us (13%)
  between operations  0.81 us (1%)
    all_to_all x1, blocking collectives, on_device(): got = lax.all_to_all(sent, DEVICES, 0, 0)  14.4 us
    all_to_all x1, starting transfers between devices, on_device(): gathered = lax.all_to_all(words, 'tile', 0, 0).reshape(-1, LANES)  10.5 us
    all_to_all x1, waiting for transfers between devices, on_device(): gathered = lax.all_to_all(words, 'tile', 0, 0).reshape(-1, LANES)  7.41 us
    pallas_call x1, Pallas kernels, on_device(): pl.pallas_call(lambda *refs: sense_own(*refs, total=total), grid=(layers,...  4.91 us
    pallas_call x1, Pallas kernels, on_device(): pl.pallas_call(lambda *refs: sense_rest(*refs, total=total, own=blk_dev /...  3.91 us
    ppermute x2, starting transfers between devices, from_behind(): return lax.ppermute(block, axis, route)  2.59 us
    slice x1, local copies, waits for them, and re-layouts, on_device(): after = from_behind(screens[:, :reach], DEVICES, -1)  2.18 us
    reshape x1, local copies, waits for them, and re-layouts, on_device(): jnp.transpose(cm_values, (1, 0, 2, 3, 4))  1.5 us
  transfers between devices with their start and end apart: 3, of which 1 were waited for; matrix products, arithmetic and copies ran while one was open for 7% of the time, Pallas kernels for 9%

profile of v1, /device:TPU:1, one launch (start us, length us, event | category | flops | bytes accessed | tf_op | source)
XLA Modules:
  0.0 54.4 jit_solution(18260838273425635602)
XLA Ops:
  0.6 2.2 %fusion = (bf16[3,256,256]{2,1,0:T(8,128)(2,1)}, bf16[3,256,256]{2,1,0:T(8,128)(2,1)}) fusion(bf16[3,1024,256]{2,1,0:T(8,128)(2,1)} %refs_2_.1), kind=kLoop, calls=%fused_computation.3 | loop fusion | bytes 1572864 | tf_op jit(solution)/shard_map/slice | solution.py:189
  2.8 2.6 %collective-permute-start = (bf16[3,256,256]{2,1,0:T(8,128)(2,1)}, bf16[3,256,256]{2,1,0:T(8,128)(2,1)S(1)}, u32[]{:S(2)}, u32[]{:S(2)}) collective-permute-start(bf16[3,256,256]{2,1,0:T(8,128)(2,1)} %get-tuple-element.7), channel_id=1, source_target_pairs={{127,0},{0,1},{1,2},{2,3},{3,4},{4,5},{5,6},{6,7},{7,8},{8,9},{9,1... | collective-permute-start | bytes 1179656 | tf_op jit(solution)/shard_map/ppermute | solution.py:20
  5.4 0.0 collective-permute-start.1
  5.4 0.7 %copy.13 = bf16[4,28,16,2,128]{4,3,2,1,0:T(2,128)(2,1)S(1)} copy(bf16[4,28,16,2,128]{4,3,2,0,1:T(2,128)(2,1)S(1)} %bitcast.20) | data formatting | bytes 1835008 | tf_op jit(solution)/shard_map/transpose | solution.py:224
  6.1 0.0 copy-start
  6.1 0.0 copy-start.4
  6.1 1.5 %reshape.37 = bf16[4,448,256]{2,1,0:T(8,128)(2,1)} reshape(bf16[4,28,16,2,128]{4,3,2,1,0:T(2,128)(2,1)S(1)} %copy.13) | data formatting | bytes 1835008 | tf_op jit(solution)/shard_map/reshape | solution.py:224
  7.7 0.1 broadcast_in_dim.3
  7.7 0.1 reshape.38
  7.8 1.3 %pad.16.refs_1_ = bf16[4,512,256]{2,1,0:T(8,128)(2,1)S(1)} pad(bf16[4,448,256]{2,1,0:T(8,128)(2,1)} %reshape.37, bf16[]{:T(256)} %constant.20.clone.1), padding=0_0x0_64x0_0 | pad | bytes 1966082 | tf_op jit(solution)/shard_map/jit(_pad)/pad | solution.py:225
  9.1 0.0 copy-start.1
  9.1 1.4 %copy-done.1 = bf16[3,1024,256]{2,1,0:T(8,128)(2,1)S(1)} copy-done((bf16[3,1024,256]{2,1,0:T(8,128)(2,1)S(1)}, bf16[3,1024,256]{2,1,0:T(8,128)(2,1)}, u32[]{:S(2)}) %copy-start.1) | copy-done | bytes 1572888
  10.5 4.9 %sense_own.1.refs_5_ = f32[256,256]{1,0:T(8,128)S(1)} custom-call(s32[1]{0:T(128)} %bitcast.refs_0_, s32[3,4,256]{2,1,0:T(4,128)S(1)} %bitcast.16, bf16[3,1024,256]{2,1,0:T(8,128)(2,1)S(1)} %copy-done.1, bf16[3,4,256,256]{3,2,1,0:T(8,128)(2,1)S(1)} %copy-done), custom_call_target="tpu_custom_call" | custom-call | tf_op jit(solution)/shard_map/sense_own/pallas_call | solution.py:193
  15.5 0.0 copy-start.8
  15.5 0.0 copy-start.5
  15.5 0.0 collective-permute-done.refs_2_
  15.5 0.0 collective-permute-done.1.refs_3_
  15.5 0.0 copy-done.2
  15.5 3.9 %sense_rest.1 = (f32[2,256]{1,0:T(2,128)}, f32[32,4,128]{2,1,0:T(4,128)}) custom-call(s32[1]{0:T(128)} %bitcast.refs_0_, s32[3,4,256]{2,1,0:T(4,128)S(1)} %bitcast.17, bf16[3,256,256]{2,1,0:T(8,128)(2,1)S(1)} %collective-permute-done.refs_2_, bf16[3,256,256]{2,1,0:T(8,128)(2,1)S(1)} %collective-permute-done.1.refs_3_, bf16[3,4,256,256]{3,2,1,0:T(8,128)(2,1)S(1)} %copy-done, ...), custom_call_target="tpu_custom_call" | custom-call | tf_op jit(solution)/shard_map/sense_rest/pallas_call | solution.py:208
  19.5 10.5 %all-to-all-start = ((f32[32,4,128]{2,1,0:T(4,128)}), f32[32,4,128]{2,1,0:T(4,128)S(1)}, u32[]{:S(2)}, u32[]{:S(2)}) async-start(f32[32,4,128]{2,1,0:T(4,128)} %get-tuple-element.5), calls=%async_computation | async-start | bytes 131072 | tf_op jit(solution)/shard_map/all_to_all | solution.py:232
  30.0 7.4 %all-to-all-done = f32[32,4,128]{2,1,0:T(4,128)S(1)} async-done(((f32[32,4,128]{2,1,0:T(4,128)}), f32[32,4,128]{2,1,0:T(4,128)S(1)}, u32[]{:S(2)}, u32[]{:S(2)}) %all-to-all-start) | async-done | bytes 65568 | tf_op jit(solution)/shard_map/all_to_all | solution.py:232
  37.4 1.2 %reconstruct.1 = f32[128,4,128]{2,1,0:T(4,128)S(1)} custom-call(f32[128,128]{1,0:T(8,128)S(1)} %bitcast.15, bf16[4,512,256]{2,1,0:T(8,128)(2,1)S(1)} %pad.16.refs_1_, s32[4,512]{1,0:T(4,128)S(1)} %pad.17.refs_2_, s32[1,512]{1,0:T(1,128)S(1)} %bitcast.18, f32[1,512]{1,0:T(1,128)S(1)} %bitcast.19, f32[3]{0:T(128)S(1)} %copy-done.5), custom_call_target="tpu_custom_call" | custom-call | tf_op jit(solution)/shard_map/reconstruct/pallas_call | solution.py:234
  38.6 14.4 %all_to_all.10.refs_1_ = f32[128,4,128]{2,1,0:T(4,128)S(1)} all-to-all(f32[128,4,128]{2,1,0:T(4,128)S(1)} %reconstruct.1), channel_id=1, replica_groups=mesh['grp'=4,'tile'=32] {'grp','tile'}, dimensions={0} | all-to-all | bytes 524288 | tf_op jit(solution)/shard_map/all_to_all | solution.py:241
  53.0 1.3 %settle.1 = f32[4,128]{1,0:T(4,128)} custom-call(s32[1]{0:T(128)} %bitcast.2.refs_0_, f32[128,4,128]{2,1,0:T(4,128)S(1)} %all_to_all.10.refs_1_, s32[4,128]{1,0:T(4,128)S(1)} %get-tuple-element.10.refs_2_, f32[4,128]{1,0:T(4,128)S(1)} %get-tuple-element.8.refs_3_, f32[3]{0:T(128)S(1)} %copy-done.5), custom_call_target="tpu_custom_call" | custom-call | tf_op jit(solution)/shard_map/settle/pallas_call | solution.py:243
  (17 shorter events, 0.0 us)
Async XLA Ops:
  0.6 4.8 %copy-start.6 = (bf16[28,4,16,2,128]{4,3,2,1,0:T(2,128)(2,1)S(1)}, bf16[28,4,16,2,128]{4,3,2,1,0:T(2,128)(2,1)}, u32[]{:S(2)}) copy-start(bf16[28,4,16,2,128]{4,3,2,1,0:T(2,128)(2,1)} %param.14) | copy-start | bytes 2752516
  2.8 12.7 %collective-permute-start = (bf16[3,256,256]{2,1,0:T(8,128)(2,1)}, bf16[3,256,256]{2,1,0:T(8,128)(2,1)S(1)}, u32[]{:S(2)}, u32[]{:S(2)}) collective-permute-start(bf16[3,256,256]{2,1,0:T(8,128)(2,1)} %get-tuple-element.7), channel_id=1, source_target_pairs={{127,0},{0,1},{1,2},{2,3},{3,4},{4,5},{5,6},{6,7},{7,8},{8,9},{9,1... | collective-permute-start | bytes 1179656 | tf_op jit(solution)/shard_map/ppermute | solution.py:20
  5.4 10.1 %collective-permute-start.1 = (bf16[3,256,256]{2,1,0:T(8,128)(2,1)}, bf16[3,256,256]{2,1,0:T(8,128)(2,1)S(1)}, u32[]{:S(2)}, u32[]{:S(2)}) collective-permute-start(bf16[3,256,256]{2,1,0:T(8,128)(2,1)} %get-tuple-element.6), channel_id=1, source_target_pairs={{1,0},{2,1},{3,2},{4,3},{5,4},{6,5},{7,6},{8,7},{9,8},{10,9},{11,1... | collective-permute-start | bytes 1179656 | tf_op jit(solution)/shard_map/ppermute | solution.py:20
  5.4 2.2 %copy-start.9 = (s32[28,4]{0,1:T(4,128)S(1)}, s32[28,4]{0,1:T(4,128)}, u32[]{:S(2)}) copy-start(s32[28,4]{0,1:T(4,128)} %param.15) | copy-start | bytes 1348
  6.1 3.0 %copy-start = (bf16[3,4,256,256]{3,2,1,0:T(8,128)(2,1)S(1)}, bf16[3,4,256,256]{3,2,1,0:T(8,128)(2,1)}, u32[]{:S(2)}) copy-start(bf16[3,4,256,256]{3,2,1,0:T(8,128)(2,1)} %refs_4_.2) | copy-start | bytes 4718596
  6.1 3.0 %copy-start.4 = (s32[256,3,4]{0,2,1:T(4,128)S(1)}, s32[256,3,4]{0,2,1:T(4,128)}, u32[]{:S(2)}) copy-start(s32[256,3,4]{0,2,1:T(4,128)} %param.12) | copy-start | bytes 36868
  9.1 1.4 %copy-start.1 = (bf16[3,1024,256]{2,1,0:T(8,128)(2,1)S(1)}, bf16[3,1024,256]{2,1,0:T(8,128)(2,1)}, u32[]{:S(2)}) copy-start(bf16[3,1024,256]{2,1,0:T(8,128)(2,1)} %refs_2_.1) | copy-start | bytes 4718596
  10.5 4.9 %copy-start.7 = (s32[448]{0:T(512)S(1)}, s32[448]{0:T(512)}, u32[]{:S(2)}) copy-start(s32[448]{0:T(512)} %param.17) | copy-start | bytes 5380
  10.5 5.0 %copy-start.2 = (bf16[512,512]{1,0:T(8,128)(2,1)S(1)}, bf16[512,512]{1,0:T(8,128)(2,1)}, u32[]{:S(2)}) copy-start(bf16[512,512]{1,0:T(8,128)(2,1)} %constant.24.clone.refs_7_) | copy-start | bytes 1572868
  10.5 5.0 %copy-start.3 = (f32[256,256]{1,0:T(8,128)S(1)}, f32[256,256]{1,0:T(8,128)}, u32[]{:S(2)}) copy-start(f32[256,256]{1,0:T(8,128)} %refs_6_.1) | copy-start | bytes 786436
  15.5 14.5 %copy-start.8 = (f32[448]{0:T(512)S(1)}, f32[448]{0:T(512)}, u32[]{:S(2)}) copy-start(f32[448]{0:T(512)} %param.16) | copy-start | bytes 5380
  15.5 21.9 %copy-start.5 = (f32[3]{0:T(128)S(1)}, f32[3]{0:T(128)}, u32[]{:S(2)}) copy-start(f32[3]{0:T(128)} %refs_4_.3) | copy-start | bytes 40
  19.5 18.0 %all-to-all-start = ((f32[32,4,128]{2,1,0:T(4,128)}), f32[32,4,128]{2,1,0:T(4,128)S(1)}, u32[]{:S(2)}, u32[]{:S(2)}) async-start(f32[32,4,128]{2,1,0:T(4,128)} %get-tuple-element.5), calls=%async_computation | async-start | bytes 131072 | tf_op jit(solution)/shard_map/all_to_all | solution.py:232

commit v2 on v1

v2 whole, which is shorter than its diff:
```python
import math

import jax
import jax.numpy as jnp
import numpy as np
from jax import lax
from jax.experimental import pallas as pl
from jax.experimental.pallas import tpu as pltpu
from jax.sharding import PartitionSpec as P

SIDE = 16
DEVICES = ("grp", "tile")
LANES = 128
EDGE = 256


def from_behind(block, axis, distance):
    devices = range(lax.axis_size(axis))
    route = [((i - distance) % len(devices), i) for i in devices]
    return lax.ppermute(block, axis, route)


def transform_table(side):
    index = np.arange(side * side)
    rows, cols = index // side, index % side
    turns = (rows[:, None] * rows[None, :] + cols[:, None] * cols[None, :]) % side
    angle = turns.astype(np.float32) * np.float32(2.0 * math.pi / side)
    cosine, sine = np.cos(angle), np.sin(angle)
    table = np.concatenate(
        [np.concatenate([cosine, -sine], 1), np.concatenate([sine, cosine], 1)], 0
    )
    return jnp.asarray(table.T.astype(jnp.bfloat16))


def sine_cosine(angle):
    turns = jnp.floor(angle * np.float32(2.0 / math.pi) + 0.5)
    rest = angle - turns * np.float32(1.5703125)
    rest = rest - turns * np.float32(4.837512969970703125e-4)
    rest = rest - turns * np.float32(7.54978995489188216e-8)
    sq = rest * rest
    sine = (np.float32(-1.9515295891e-4) * sq + np.float32(8.3321608736e-3)) * sq
    sine = (sine - np.float32(1.6666654611e-1)) * sq * rest + rest
    cosine = (np.float32(2.443315711809948e-5) * sq - np.float32(1.388731625493765e-3)) * sq
    cosine = (cosine + np.float32(4.166664568298827e-2)) * sq * sq - np.float32(0.5) * sq + 1.0
    quarter = turns.astype(jnp.int32)
    odd = (quarter & 1) == 1
    out_sine = jnp.where(odd, cosine, sine)
    out_cosine = jnp.where(odd, sine, cosine)
    out_sine = jnp.where((quarter & 2) == 2, -out_sine, out_sine)
    out_cosine = jnp.where(((quarter + 1) & 2) == 2, -out_cosine, out_cosine)
    return out_sine, out_cosine


def offsets_of(foot_rows, start, total):
    away = foot_rows - start
    away = jnp.where(away < -(total // 2), away + total, away)
    away = jnp.where(away >= total // 2, away - total, away)
    away = away.astype(jnp.float32)
    foot, subs = away.shape
    filled = jnp.concatenate([away, jnp.zeros((8 - foot, subs), jnp.float32)], 0)
    return filled.T.astype(jnp.int32)


def hits(column, first, count):
    column = jnp.broadcast_to(column, (column.shape[0], LANES)).astype(jnp.int16)
    lane = lax.broadcasted_iota(jnp.int16, column.shape, 1)
    one, zero = jnp.bfloat16(1), jnp.bfloat16(0)
    parts = [
        jnp.where(lane == column - jnp.int16(first + b), one, zero)
        for b in range(0, count, LANES)
    ]
    return jnp.concatenate(parts, 1)


def edges(screens_ref, tail_ref, head_ref, sems):
    layers, blocks, _ = screens_ref.shape
    copies = []
    for layer in range(layers):
        tail = screens_ref.at[layer, pl.ds(blocks - EDGE, EDGE)]
        head = screens_ref.at[layer, pl.ds(0, EDGE)]
        copies.append(pltpu.make_async_copy(tail, tail_ref.at[layer], sems.at[2 * layer]))
        copies.append(pltpu.make_async_copy(head, head_ref.at[layer], sems.at[2 * layer + 1]))
    for copy in copies:
        copy.start()
    for copy in copies:
        copy.wait()


def sense_own(
    start_ref, base_ref, gain_ref, foot_ref, cols_ref, owner_ref, prev_ref, screens_ref,
    weights_ref, phase_ref, spot_ref, state_ref, *, total
):
    layers, foot, _ = foot_ref.shape
    blocks, pixels = screens_ref.shape[1:]
    phase = None
    for layer in range(layers):
        offsets = offsets_of(foot_ref[layer], start_ref[0], total)
        picked = [
            jnp.dot(
                hits(offsets[:, k : k + 1], 0, blocks),
                screens_ref[layer],
                preferred_element_type=jnp.float32,
            ).astype(jnp.bfloat16)
            for k in range(foot)
        ]
        part = jnp.dot(
            jnp.concatenate(picked, 1),
            weights_ref[layer].reshape(foot * pixels, pixels),
            preferred_element_type=jnp.float32,
        )
        phase = part if phase is None else phase + part
    phase_ref[...] = phase

    positions, rowblk = cols_ref.shape
    acts = owner_ref.shape[1]
    rb = acts // rowblk
    cols = (cols_ref[...] - base_ref[0]).astype(jnp.float32)
    lane = lax.broadcasted_iota(jnp.int32, (positions, LANES), 1)
    place = lax.broadcasted_iota(jnp.int32, (positions, LANES), 0)
    spread = jnp.where(lane // (2 * rb) == place, 1.0, 0.0)
    cols = lax.dot_general(
        cols, spread, (((0,), (0,)), ((), ())), preferred_element_type=jnp.float32
    )
    comp = lax.broadcasted_iota(jnp.int32, cols.shape, 1) % 2
    spot = cols.astype(jnp.int32) * 2 + comp
    height = spot_ref.shape[0]
    spot_ref[...] = jnp.concatenate(
        [spot, jnp.full((height - rowblk, LANES), -1, jnp.int32)], 0
    )
    lines = height * rb // LANES
    owner = owner_ref[...]
    gain = jnp.zeros(owner.shape, jnp.float32)
    for m in range(gain_ref.shape[0]):
        gain = jnp.where(owner == m, gain_ref[m], gain)
    missing = lines * LANES - acts
    rows = []
    for values, fill in ((owner.astype(jnp.float32), -1.0), (prev_ref[...], 0.0), (gain, 0.0)):
        values = jnp.concatenate([values, jnp.full((1, missing), fill, jnp.float32)], 1)
        rows += [values[:, i * LANES : (i + 1) * LANES] for i in range(lines)]
    state_ref[...] = jnp.concatenate(rows, 0)


def sense_rest(
    start_ref, foot_ref, before_ref, after_ref, weights_ref, phase_ref, illum_ref, table_ref,
    slopes_ref, words_ref, *, total, own
):
    layers, foot, subs = foot_ref.shape
    pixels = phase_ref.shape[1]
    phase = phase_ref[...]
    for layer in range(layers):
        offsets = offsets_of(foot_ref[layer], start_ref[0], total)
        blocks = jnp.concatenate([before_ref[layer], after_ref[layer]], 0)
        picked = []
        for k in range(foot):
            column = offsets[:, k : k + 1]
            found = jnp.concatenate([hits(column, -EDGE, EDGE), hits(column, own, EDGE)], 1)
            rows = jnp.dot(found, blocks, preferred_element_type=jnp.float32)
            picked.append(rows.astype(jnp.bfloat16))
        phase = phase + jnp.dot(
            jnp.concatenate(picked, 1),
            weights_ref[layer].reshape(foot * pixels, pixels),
            preferred_element_type=jnp.float32,
        )
    phase = phase.T
    illum = illum_ref[...].T
    sine, cosine = sine_cosine(phase)
    field = jnp.concatenate([illum * cosine, illum * sine], 0).astype(jnp.bfloat16)
    spectrum = jnp.dot(table_ref[...], field, preferred_element_type=jnp.float32)
    real_part = spectrum[:pixels]
    imag_part = spectrum[pixels:]
    intensity = real_part * real_part + imag_part * imag_part
    row = lax.broadcasted_iota(jnp.int32, intensity.shape, 0)
    cv = row % SIDE
    cu = row // SIDE
    cv = (cv - SIDE * (cv >= SIDE // 2).astype(jnp.int32)).astype(jnp.float32)
    cu = (cu - SIDE * (cu >= SIDE // 2).astype(jnp.int32)).astype(jnp.float32)
    whole = jnp.sum(intensity, axis=0, keepdims=True)
    slope_x = jnp.sum(intensity * cv, axis=0, keepdims=True) / whole
    slope_y = jnp.sum(intensity * cu, axis=0, keepdims=True) / whole
    slopes = jnp.concatenate([slope_x, slope_y], 0)
    slopes_ref[...] = slopes
    words = slopes.astype(jnp.bfloat16).astype(jnp.float32)
    words = [words[:, h * LANES : (h + 1) * LANES] for h in range(subs // LANES)]
    words_ref[...] = jnp.broadcast_to(jnp.concatenate(words, 0)[None], words_ref.shape)


def reconstruct(words_ref, cm_ref, spot_ref, state_ref, sent_ref, *, rb, share, mirrors):
    words = words_ref[...].astype(jnp.bfloat16)
    rowblk = cm_ref.shape[0] // LANES
    row = lax.broadcasted_iota(jnp.int32, (words.shape[0], LANES), 0)
    parts = []
    for i in range(rowblk):
        product = lax.dot_general(
            words,
            cm_ref[i * LANES : (i + 1) * LANES, :],
            (((1,), (1,)), ((), ())),
            preferred_element_type=jnp.float32,
        )
        chosen = jnp.where(row == spot_ref[i : i + 1, :], product, 0.0)
        parts.append(jnp.sum(chosen, axis=0, keepdims=True))
    height = spot_ref.shape[0]
    if height > rowblk:
        parts.append(jnp.zeros((height - rowblk, LANES), jnp.float32))
    parts = jnp.concatenate(parts, 0)
    source = lax.broadcasted_iota(jnp.int32, (LANES, LANES), 0)
    lane = lax.broadcasted_iota(jnp.int32, (LANES, LANES), 1)
    fold = jnp.where((source % (2 * rb)) // 2 == lane % rb, 1.0, 0.0)
    spread = jnp.dot(
        parts, fold, preferred_element_type=jnp.float32, precision=lax.Precision.HIGHEST
    )
    per = LANES // rb
    block = lax.broadcasted_iota(jnp.int32, spread.shape, 0)
    lane = lax.broadcasted_iota(jnp.int32, spread.shape, 1)
    spread = jnp.where(lane // rb == block % per, spread, 0.0)
    lines = height // per
    recon = jnp.sum(spread.reshape(lines, per, LANES), axis=1)
    owner = state_ref[:lines]
    updated = state_ref[lines : 2 * lines] * share - state_ref[2 * lines :] * recon
    row = lax.broadcasted_iota(jnp.int32, recon.shape, 0)
    lane = lax.broadcasted_iota(jnp.int32, recon.shape, 1)
    last = row == lines - 1
    for m in range(mirrors):
        mine = owner == float(m)
        recon = jnp.where(
            last & (lane == LANES - 2 * mirrors + m),
            jnp.sum(jnp.where(mine, updated, 0.0), keepdims=True),
            recon,
        )
        recon = jnp.where(
            last & (lane == LANES - mirrors + m),
            jnp.sum(jnp.where(mine, share, 0.0), keepdims=True),
            recon,
        )
    sent_ref[...] = jnp.broadcast_to(recon[None], sent_ref.shape)


def settle(tile_ref, got_ref, state_ref, commands_ref, *, groups, mirrors):
    count, lines, _ = got_ref.shape
    tiles = count // groups
    recon = got_ref[tile_ref[0]]
    for g in range(1, groups):
        recon = recon + got_ref[g * tiles + tile_ref[0]]
    last = jnp.sum(got_ref[:, lines - 1, :], axis=0, keepdims=True)
    lane = lax.broadcasted_iota(jnp.int32, last.shape, 1)

    def entry(at):
        return jnp.sum(jnp.where(lane == at, last, 0.0), axis=1, keepdims=True)

    owner = state_ref[:lines]
    piston = jnp.zeros(owner.shape, jnp.float32)
    for m in range(mirrors):
        mean = entry(LANES - 2 * mirrors + m) / entry(LANES - mirrors + m)
        piston = jnp.where(owner == float(m), mean, piston)
    commands = state_ref[lines : 2 * lines] - state_ref[2 * lines :] * recon - piston
    acts = commands_ref.shape[0]
    for i in range(lines):
        some = min(LANES, acts - i * LANES)
        commands_ref[i * LANES : i * LANES + some] = commands[i, :some]


def on_device(
    screens,
    interp_weights,
    footprint,
    illumination,
    cm_values,
    cm_columns,
    prev_commands,
    owner_map,
    dm_gain,
):
    layers, blk_dev, pixels = screens.shape
    subs, _, foot = footprint.shape
    groups, tiles = lax.axis_size("grp"), lax.axis_size("tile")
    total = blk_dev * groups * tiles
    rowblk, positions, rb, comps, cbs = cm_values.shape
    acts = rowblk * rb
    mirrors = dm_gain.shape[0]
    height = -(-(acts + 2 * mirrors) // LANES) * LANES // rb
    lines = height * rb // LANES
    smem = pl.BlockSpec(memory_space=pltpu.SMEM)
    vmem = pl.BlockSpec(memory_space=pltpu.VMEM)
    limit = pltpu.CompilerParams(vmem_limit_bytes=24 * 2**20)
    f32 = jnp.float32

    edge = jax.ShapeDtypeStruct((layers, EDGE, pixels), screens.dtype)
    tail, head = pl.pallas_call(
        edges,
        in_specs=[pl.BlockSpec(memory_space=pltpu.HBM)],
        out_specs=[vmem, vmem],
        out_shape=[edge, edge],
        scratch_shapes=[pltpu.SemaphoreType.DMA((2 * layers,))],
        compiler_params=limit,
        name="edges",
    )(pltpu.with_memory_space_constraint(screens, pltpu.HBM))
    before = from_behind(tail, DEVICES, 1)
    after = from_behind(head, DEVICES, -1)

    start = (lax.axis_index(DEVICES) * blk_dev).astype(jnp.int32).reshape(1)
    base = (lax.axis_index("grp") * (tiles * subs // cbs)).astype(jnp.int32).reshape(1)
    foot_rows = jnp.transpose(footprint, (1, 2, 0))
    phase, spot, state = pl.pallas_call(
        lambda *refs: sense_own(*refs, total=total),
        in_specs=[smem] * 3 + [vmem] * 6,
        out_shape=(
            jax.ShapeDtypeStruct((subs, pixels), f32),
            jax.ShapeDtypeStruct((height, LANES), jnp.int32),
            jax.ShapeDtypeStruct((3 * lines, LANES), f32),
        ),
        compiler_params=limit,
        name="sense_own",
    )(
        start, base, dm_gain, foot_rows, cm_columns.T, owner_map.reshape(1, acts),
        prev_commands.reshape(1, acts), screens, interp_weights,
    )
    slopes, words = pl.pallas_call(
        lambda *refs: sense_rest(*refs, total=total, own=blk_dev),
        in_specs=[smem] + [vmem] * 7,
        out_shape=(
            jax.ShapeDtypeStruct((2, subs), f32),
            jax.ShapeDtypeStruct((tiles, 2 * subs // LANES, LANES), f32),
        ),
        compiler_params=limit,
        name="sense_rest",
    )(start, foot_rows, before, after, interp_weights, phase, illumination, transform_table(SIDE))

    cm = cm_values.reshape(rowblk * positions * rb * comps, cbs)
    gathered = lax.all_to_all(words, "tile", 0, 0).reshape(-1, LANES)
    sent = pl.pallas_call(
        lambda *refs: reconstruct(*refs, rb=rb, share=1.0 / groups, mirrors=mirrors),
        in_specs=[vmem] * 4,
        out_shape=jax.ShapeDtypeStruct((groups * tiles, lines, LANES), f32),
        compiler_params=limit,
        name="reconstruct",
    )(gathered, cm, spot, state)
    got = lax.all_to_all(sent, DEVICES, 0, 0)
    tile = lax.axis_index("tile").astype(jnp.int32).reshape(1)
    commands = pl.pallas_call(
        lambda *refs: settle(*refs, groups=groups, mirrors=mirrors),
        in_specs=[smem, vmem, vmem],
        out_shape=jax.ShapeDtypeStruct((acts,), f32),
        compiler_params=limit,
        name="settle",
    )(tile, got, state)
    return (slopes, commands)


def solution(mesh):
    in_specs = (
        P(None, ("grp", "tile"), None),
        P(),
        P(("grp", "tile"), None, None),
        P(("grp", "tile"), None),
        P("tile", "grp", None, None, None),
        P("tile", "grp"),
        P("tile"),
        P("tile"),
        P(),
    )
    out_specs = (P(None, ("grp", "tile")), P("tile"))
    return jax.shard_map(
        on_device, mesh=mesh, in_specs=in_specs, out_specs=out_specs, check_vma=False
    )
```

time: 54.7 us -> 52.1 us (0.952)
  blocking collectives: 14.4 us -> 35 us
  starting transfers between devices: 13.1 us -> 2.66 us
  local copies, waits for them, and re-layouts: 7.27 us -> 1.45 us
  waiting for transfers between devices: 7.42 us -> 2.58 us
  Pallas kernels: 11.3 us -> 9.53 us
    all_to_all x0 -> x1, blocking collectives: none -> 17.7 us  [on_device(): gathered = lax.all_to_all(words, 'tile', 0, 0).reshape(-1, LANES)]
    all_to_all x1 -> x0, starting transfers between devices: 10.5 us -> none  [on_device(): gathered = lax.all_to_all(words, 'tile', 0, 0).reshape(-1, LANES)]
    all_to_all x1 -> x0, waiting for transfers between devices: 7.41 us -> none  [on_device(): gathered = lax.all_to_all(words, 'tile', 0, 0).reshape(-1, LANES)]
    all_to_all x1, blocking collectives: 14.4 us -> 17.2 us  [on_device(): got = lax.all_to_all(sent, DEVICES, 0, 0)]
    ppermute x2, waiting for transfers between devices: 0.01 us -> 2.58 us  [from_behind(): return lax.ppermute(block, axis, route)]
    slice x1 -> x0, local copies, waits for them, and re-layouts: 2.18 us -> none  [on_device(): after = from_behind(screens[:, :reach], DEVICES, -1)]
    pallas_call x4 -> x5, Pallas kernels: 11.3 us -> 9.53 us  [the longest x1 3.18 us: on_device(): pl.pallas_call(lambda *refs: sense_rest(*refs, total=total, own=blk_dev),...]
    reshape x4 -> x0, local copies, waits for them, and re-layouts: 1.61 us -> none  [the longest x1 1.5 us: on_device(): jnp.transpose(cm_values, (1, 0, 2, 3, 4))]
  transfers between devices with their start and end apart: 3 -> 2, of which waited for: 1 -> 2; matrix products, arithmetic and copies ran while one was open for 7% -> 0% of each run, Pallas kernels for 9% -> 6%
where the time goes in v2:
time: 52.1 us; the launch traced here: 51.9 us
  blocking collectives  35 us (67%)
  Pallas kernels  9.53 us (18%)
  starting transfers between devices  2.66 us (5%)
  waiting for transfers between devices  2.58 us (5%)
  local copies, waits for them, and re-layouts  1.45 us (3%)
  between operations  0.76 us (1%)
    all_to_all x1, blocking collectives, on_device(): gathered = lax.all_to_all(words, 'tile', 0, 0).reshape(-1, LANES)  17.7 us
    all_to_all x1, blocking collectives, on_device(): got = lax.all_to_all(sent, DEVICES, 0, 0)  17.2 us
    pallas_call x1, Pallas kernels, on_device(): pl.pallas_call(lambda *refs: sense_rest(*refs, total=total, own=blk_dev),...  3.18 us
    pallas_call x1, Pallas kernels, on_device(): pl.pallas_call(lambda *refs: sense_own(*refs, total=total), in_specs=[sme...  3.14 us
    ppermute x2, starting transfers between devices, from_behind(): return lax.ppermute(block, axis, route)  2.66 us
    ppermute x2, waiting for transfers between devices, from_behind(): return lax.ppermute(block, axis, route)  2.58 us
    unnamed x22, local copies, waits for them, and re-layouts  1.45 us
    pallas_call x1, Pallas kernels, on_device(): pl.pallas_call(edges, in_specs=[pl.BlockSpec(memory_space=pltpu.HBM)], ou...  1.36 us
  transfers between devices with their start and end apart: 2, of which 2 were waited for; matrix products, arithmetic and copies ran while one was open for 0% of the time, Pallas kernels for 6%

profile of v2, /device:TPU:1, one launch (start us, length us, event | category | flops | bytes accessed | tf_op | source)
XLA Modules:
  0.0 51.9 jit_solution(6889789749284137049)
XLA Ops:
  0.6 0.0 copy-start
  0.6 0.0 copy-start.6
  0.7 0.0 copy-start.10
  0.7 1.4 %edges.1 = (bf16[3,256,256]{2,1,0:T(8,128)(2,1)S(1)}, bf16[3,256,256]{2,1,0:T(8,128)(2,1)S(1)}) custom-call(bf16[3,1024,256]{2,1,0:T(8,128)(2,1)} %refs_7_.2), custom_call_target="tpu_custom_call" | custom-call | tf_op jit(solution)/shard_map/edges/pallas_call | solution.py:287
  2.1 2.7 %collective-permute-start = (bf16[3,256,256]{2,1,0:T(8,128)(2,1)S(1)}, bf16[3,256,256]{2,1,0:T(8,128)(2,1)S(1)}, u32[]{:S(2)}, u32[]{:S(2)}) collective-permute-start(bf16[3,256,256]{2,1,0:T(8,128)(2,1)S(1)} %get-tuple-element.9), channel_id=1, source_target_pairs={{127,0},{0,1},{1,2},{2,3},{3,4},{4,5},{5,6},{6,7},{7,8},{8,9},{9,1... | collective-permute-start | bytes 1179656 | tf_op jit(solution)/shard_map/ppermute | solution.py:20
  4.7 0.0 collective-permute-start.1
  4.7 0.0 copy-done.10
  4.7 0.0 copy-done.7
  4.7 0.0 copy-done.8
  4.8 0.0 copy-done.9
  4.8 0.0 copy-start.1
  4.8 1.4 %copy-done.1 = bf16[3,4,256,256]{3,2,1,0:T(8,128)(2,1)S(1)} copy-done((bf16[3,4,256,256]{3,2,1,0:T(8,128)(2,1)S(1)}, bf16[3,4,256,256]{3,2,1,0:T(8,128)(2,1)}, u32[]{:S(2)}) %copy-start.1) | copy-done | bytes 1572888
  6.2 3.1 %sense_own.1 = (f32[256,256]{1,0:T(8,128)S(1)}, s32[32,128]{1,0:T(8,128)S(1)}, f32[12,128]{1,0:T(8,128)S(1)}) custom-call(s32[1]{0:T(128)} %bitcast.refs_0_, s32[1]{0:T(128)} %bitcast.2.refs_1_, f32[3]{0:T(128)S(1)} %copy-done.10, s32[3,4,256]{2,1,0:T(4,128)S(1)} %bitcast.11, s32[4,28]{1,0:T(4,128)S(1)} %bitcast.13, s32[1,448]{1,0:T(1,128)S(1)} %bitcast.14, ...), custom_call_target="tpu_custom_call" | custom-call | tf_op jit(solution)/shard_map/sense_own/pallas_call | solution.py:302
  9.3 0.1 collective-permute-done.refs_2_
  9.4 2.5 %collective-permute-done.1.refs_3_ = bf16[3,256,256]{2,1,0:T(8,128)(2,1)S(1)} collective-permute-done((bf16[3,256,256]{2,1,0:T(8,128)(2,1)S(1)}, bf16[3,256,256]{2,1,0:T(8,128)(2,1)S(1)}, u32[]{:S(2)}, u32[]{:S(2)}) %collective-permute-start.1) | collective-permute-done | bytes 393248 | tf_op jit(solution)/shard_map/ppermute | solution.py:20
  11.9 0.0 copy-done.2
  11.9 0.0 copy-done.5
  11.9 0.0 copy-start.3
  11.9 3.2 %sense_rest.1 = (f32[2,256]{1,0:T(2,128)}, f32[32,4,128]{2,1,0:T(4,128)S(1)}) custom-call(s32[1]{0:T(128)} %bitcast.refs_0_, s32[3,4,256]{2,1,0:T(4,128)S(1)} %bitcast.12, bf16[3,256,256]{2,1,0:T(8,128)(2,1)S(1)} %collective-permute-done.refs_2_, bf16[3,256,256]{2,1,0:T(8,128)(2,1)S(1)} %collective-permute-done.1.refs_3_, ...), custom_call_target="tpu_custom_call" | custom-call | tf_op jit(solution)/shard_map/sense_rest/pallas_call | solution.py:316
  15.1 17.7 %all_to_all.10 = f32[32,4,128]{2,1,0:T(4,128)S(1)} all-to-all(f32[32,4,128]{2,1,0:T(4,128)S(1)} %get-tuple-element.13), channel_id=1, replica_groups=mesh['grp'=4,'tile'=32] {'tile'}, dimensions={0} | all-to-all | bytes 131072 | tf_op jit(solution)/shard_map/all_to_all | solution.py:328
  32.9 0.0 copy-done.3
  32.9 1.1 %reconstruct.1 = f32[128,4,128]{2,1,0:T(4,128)S(1)} custom-call(f32[128,128]{1,0:T(8,128)S(1)} %bitcast.10, bf16[3584,128]{1,0:T(8,128)(2,1)S(1)} %bitcast.9, s32[32,128]{1,0:T(8,128)S(1)} %get-tuple-element.14.refs_2_, f32[12,128]{1,0:T(8,128)S(1)} %get-tuple-element.15.refs_3_.refs_2_), custom_call_target="tpu_custom_call" | custom-call | tf_op jit(solution)/shard_map/reconstruct/pallas_call | solution.py:329
  34.0 17.2 %all_to_all.11.refs_1_ = f32[128,4,128]{2,1,0:T(4,128)S(1)} all-to-all(f32[128,4,128]{2,1,0:T(4,128)S(1)} %reconstruct.1), channel_id=1, replica_groups=mesh['grp'=4,'tile'=32] {'grp','tile'}, dimensions={0} | all-to-all | bytes 524288 | tf_op jit(solution)/shard_map/all_to_all | solution.py:336
  51.2 0.7 %settle.1 = f32[448]{0:T(512)} custom-call(s32[1]{0:T(128)} %bitcast.6.refs_0_, f32[128,4,128]{2,1,0:T(4,128)S(1)} %all_to_all.11.refs_1_, f32[12,128]{1,0:T(8,128)S(1)} %get-tuple-element.15.refs_3_.refs_2_), custom_call_target="tpu_custom_call" | custom-call | tf_op jit(solution)/shard_map/settle/pallas_call | solution.py:338
  (9 shorter events, 0.0 us)
Async XLA Ops:
  0.6 4.1 %copy-start = (bf16[3,1024,256]{2,1,0:T(8,128)(2,1)S(1)}, bf16[3,1024,256]{2,1,0:T(8,128)(2,1)}, u32[]{:S(2)}) copy-start(bf16[3,1024,256]{2,1,0:T(8,128)(2,1)} %refs_7_.2) | copy-start | bytes 4718596
  0.6 4.1 %copy-start.6 = (s32[256,3,4]{0,2,1:T(4,128)S(1)}, s32[256,3,4]{0,2,1:T(4,128)}, u32[]{:S(2)}) copy-start(s32[256,3,4]{0,2,1:T(4,128)} %param.12) | copy-start | bytes 36868
  0.7 4.1 %copy-start.10 = (f32[3]{0:T(128)S(1)}, f32[3]{0:T(128)}, u32[]{:S(2)}) copy-start(f32[3]{0:T(128)} %refs_2_.1) | copy-start | bytes 40
  0.7 4.1 %copy-start.7 = (s32[28,4]{0,1:T(4,128)S(1)}, s32[28,4]{0,1:T(4,128)}, u32[]{:S(2)}) copy-start(s32[28,4]{0,1:T(4,128)} %param.15) | copy-start | bytes 1348
  0.7 4.1 %copy-start.8 = (s32[448]{0:T(512)S(1)}, s32[448]{0:T(512)}, u32[]{:S(2)}) copy-start(s32[448]{0:T(512)} %param.17) | copy-start | bytes 5380
  0.7 4.1 %copy-start.9 = (f32[448]{0:T(512)S(1)}, f32[448]{0:T(512)}, u32[]{:S(2)}) copy-start(f32[448]{0:T(512)} %param.16) | copy-start | bytes 5380
  2.1 7.4 %collective-permute-start = (bf16[3,256,256]{2,1,0:T(8,128)(2,1)S(1)}, bf16[3,256,256]{2,1,0:T(8,128)(2,1)S(1)}, u32[]{:S(2)}, u32[]{:S(2)}) collective-permute-start(bf16[3,256,256]{2,1,0:T(8,128)(2,1)S(1)} %get-tuple-element.9), channel_id=1, source_target_pairs={{127,0},{0,1},{1,2},{2,3},{3,4},{4,5},{5,6},{6,7},{7,8},{8,9},{9,1... | collective-permute-start | bytes 1179656 | tf_op jit(solution)/shard_map/ppermute | solution.py:20
  4.7 7.2 %collective-permute-start.1 = (bf16[3,256,256]{2,1,0:T(8,128)(2,1)S(1)}, bf16[3,256,256]{2,1,0:T(8,128)(2,1)S(1)}, u32[]{:S(2)}, u32[]{:S(2)}) collective-permute-start(bf16[3,256,256]{2,1,0:T(8,128)(2,1)S(1)} %get-tuple-element.10), channel_id=1, source_target_pairs={{1,0},{2,1},{3,2},{4,3},{5,4},{6,5},{7,6},{8,7},{9,8},{10,9},{11,1... | collective-permute-start | bytes 1179656 | tf_op jit(solution)/shard_map/ppermute | solution.py:20
  4.8 1.4 %copy-start.1 = (bf16[3,4,256,256]{3,2,1,0:T(8,128)(2,1)S(1)}, bf16[3,4,256,256]{3,2,1,0:T(8,128)(2,1)}, u32[]{:S(2)}) copy-start(bf16[3,4,256,256]{3,2,1,0:T(8,128)(2,1)} %refs_4_.1) | copy-start | bytes 4718596
  6.2 5.7 %copy-start.2 = (bf16[3,4,256,256]{3,2,1,0:T(8,128)(2,1)S(1)}, bf16[3,4,256,256]{3,2,1,0:T(8,128)(2,1)}, u32[]{:S(2)}) copy-start(bf16[3,4,256,256]{3,2,1,0:T(8,128)(2,1)} %refs_4_.1) | copy-start | bytes 4718596
  6.2 5.7 %copy-start.4 = (bf16[512,512]{1,0:T(8,128)(2,1)S(1)}, bf16[512,512]{1,0:T(8,128)(2,1)}, u32[]{:S(2)}) copy-start(bf16[512,512]{1,0:T(8,128)(2,1)} %constant.17.clone.refs_7_) | copy-start | bytes 1572868
  6.2 5.7 %copy-start.5 = (f32[256,256]{1,0:T(8,128)S(1)}, f32[256,256]{1,0:T(8,128)}, u32[]{:S(2)}) copy-start(f32[256,256]{1,0:T(8,128)} %refs_6_.1) | copy-start | bytes 786436
  11.9 20.9 %copy-start.3 = (bf16[28,4,16,2,128]{4,3,2,1,0:T(2,128)(2,1)S(1)}, bf16[28,4,16,2,128]{4,3,2,1,0:T(2,128)(2,1)}, u32[]{:S(2)}) copy-start(bf16[28,4,16,2,128]{4,3,2,1,0:T(2,128)(2,1)} %param.14) | copy-start | bytes 2752516

commit v3 on v2

--- a/solution.py
+++ b/solution.py
@@ -14,10 +14,10 @@
 EDGE = 256
 
 
-def from_behind(block, axis, distance):
-    devices = range(lax.axis_size(axis))
-    route = [((i - distance) % len(devices), i) for i in devices]
-    return lax.ppermute(block, axis, route)
+def swap(block, step):
+    count = lax.axis_size(DEVICES)
+    route = [(i, (i + step if i % 2 else i - step) % count) for i in range(count)]
+    return lax.ppermute(block, DEVICES, route)
 
 
 def transform_table(side):
@@ -72,14 +72,18 @@
     return jnp.concatenate(parts, 1)
 
 
-def edges(screens_ref, tail_ref, head_ref, sems):
+def edges(odd_ref, screens_ref, outer_ref, inner_ref, sems):
     layers, blocks, _ = screens_ref.shape
+    last = (blocks // EDGE - 1) * EDGE
+    outer = pl.multiple_of(odd_ref[0] * last, EDGE)
+    inner = pl.multiple_of((1 - odd_ref[0]) * last, EDGE)
     copies = []
     for layer in range(layers):
-        tail = screens_ref.at[layer, pl.ds(blocks - EDGE, EDGE)]
-        head = screens_ref.at[layer, pl.ds(0, EDGE)]
-        copies.append(pltpu.make_async_copy(tail, tail_ref.at[layer], sems.at[2 * layer]))
-        copies.append(pltpu.make_async_copy(head, head_ref.at[layer], sems.at[2 * layer + 1]))
+        for first, ref, sem in ((outer, outer_ref, 0), (inner, inner_ref, 1)):
+            block = screens_ref.at[layer, pl.ds(first, EDGE)]
+            copies.append(
+                pltpu.make_async_copy(block, ref.at[layer], sems.at[2 * layer + sem])
+            )
     for copy in copies:
         copy.start()
     for copy in copies:
@@ -87,22 +91,26 @@
 
 
 def sense_own(
-    start_ref, base_ref, gain_ref, foot_ref, cols_ref, owner_ref, prev_ref, screens_ref,
-    weights_ref, phase_ref, spot_ref, state_ref, *, total
+    start_ref, first_ref, base_ref, gain_ref, foot_ref, cols_ref, owner_ref, prev_ref,
+    screens_ref, inner_ref, weights_ref, phase_ref, spot_ref, state_ref, *, total
 ):
     layers, foot, _ = foot_ref.shape
     blocks, pixels = screens_ref.shape[1:]
     phase = None
     for layer in range(layers):
         offsets = offsets_of(foot_ref[layer], start_ref[0], total)
-        picked = [
-            jnp.dot(
-                hits(offsets[:, k : k + 1], 0, blocks),
-                screens_ref[layer],
+        picked = []
+        for k in range(foot):
+            column = offsets[:, k : k + 1]
+            rows = jnp.dot(
+                hits(column, 0, blocks), screens_ref[layer], preferred_element_type=jnp.float32
+            )
+            rows = rows + jnp.dot(
+                hits(column - first_ref[0], 0, EDGE),
+                inner_ref[layer],
                 preferred_element_type=jnp.float32,
-            ).astype(jnp.bfloat16)
-            for k in range(foot)
-        ]
+            )
+            picked.append(rows.astype(jnp.bfloat16))
         part = jnp.dot(
             jnp.concatenate(picked, 1),
             weights_ref[layer].reshape(foot * pixels, pixels),
@@ -141,20 +149,18 @@
 
 
 def sense_rest(
-    start_ref, foot_ref, before_ref, after_ref, weights_ref, phase_ref, illum_ref, table_ref,
-    slopes_ref, words_ref, *, total, own
+    start_ref, first_ref, foot_ref, outer_ref, weights_ref, phase_ref, illum_ref, table_ref,
+    slopes_ref, words_ref, *, total
 ):
     layers, foot, subs = foot_ref.shape
     pixels = phase_ref.shape[1]
     phase = phase_ref[...]
     for layer in range(layers):
         offsets = offsets_of(foot_ref[layer], start_ref[0], total)
-        blocks = jnp.concatenate([before_ref[layer], after_ref[layer]], 0)
         picked = []
         for k in range(foot):
-            column = offsets[:, k : k + 1]
-            found = jnp.concatenate([hits(column, -EDGE, EDGE), hits(column, own, EDGE)], 1)
-            rows = jnp.dot(found, blocks, preferred_element_type=jnp.float32)
+            found = hits(offsets[:, k : k + 1] - first_ref[0], 0, EDGE)
+            rows = jnp.dot(found, outer_ref[layer], preferred_element_type=jnp.float32)
             picked.append(rows.astype(jnp.bfloat16))
         phase = phase + jnp.dot(
             jnp.concatenate(picked, 1),
@@ -284,24 +290,27 @@
     f32 = jnp.float32
 
     edge = jax.ShapeDtypeStruct((layers, EDGE, pixels), screens.dtype)
-    tail, head = pl.pallas_call(
+    odd = (lax.axis_index("tile") % 2).astype(jnp.int32).reshape(1)
+    outer, inner = pl.pallas_call(
         edges,
-        in_specs=[pl.BlockSpec(memory_space=pltpu.HBM)],
+        in_specs=[smem, pl.BlockSpec(memory_space=pltpu.HBM)],
         out_specs=[vmem, vmem],
         out_shape=[edge, edge],
         scratch_shapes=[pltpu.SemaphoreType.DMA((2 * layers,))],
         compiler_params=limit,
         name="edges",
-    )(pltpu.with_memory_space_constraint(screens, pltpu.HBM))
-    before = from_behind(tail, DEVICES, 1)
-    after = from_behind(head, DEVICES, -1)
+    )(odd, pltpu.with_memory_space_constraint(screens, pltpu.HBM))
+    outer = swap(outer, 1)
+    inner = swap(inner, -1)
+    outer_first = odd * (blk_dev + EDGE) - EDGE
+    inner_first = (1 - odd) * (blk_dev + EDGE) - EDGE
 
     start = (lax.axis_index(DEVICES) * blk_dev).astype(jnp.int32).reshape(1)
     base = (lax.axis_index("grp") * (tiles * subs // cbs)).astype(jnp.int32).reshape(1)
     foot_rows = jnp.transpose(footprint, (1, 2, 0))
     phase, spot, state = pl.pallas_call(
         lambda *refs: sense_own(*refs, total=total),
-        in_specs=[smem] * 3 + [vmem] * 6,
+        in_specs=[smem] * 4 + [vmem] * 7,
         out_shape=(
             jax.ShapeDtypeStruct((subs, pixels), f32),
             jax.ShapeDtypeStruct((height, LANES), jnp.int32),
@@ -310,19 +319,22 @@
         compiler_params=limit,
         name="sense_own",
     )(
-        start, base, dm_gain, foot_rows, cm_columns.T, owner_map.reshape(1, acts),
-        prev_commands.reshape(1, acts), screens, interp_weights,
+        start, inner_first, base, dm_gain, foot_rows, cm_columns.T, owner_map.reshape(1, acts),
+        prev_commands.reshape(1, acts), screens, inner, interp_weights,
     )
     slopes, words = pl.pallas_call(
-        lambda *refs: sense_rest(*refs, total=total, own=blk_dev),
-        in_specs=[smem] + [vmem] * 7,
+        lambda *refs: sense_rest(*refs, total=total),
+        in_specs=[smem] * 2 + [vmem] * 6,
         out_shape=(
             jax.ShapeDtypeStruct((2, subs), f32),
             jax.ShapeDtypeStruct((tiles, 2 * subs // LANES, LANES), f32),
         ),
         compiler_params=limit,
         name="sense_rest",
-    )(start, foot_rows, before, after, interp_weights, phase, illumination, transform_table(SIDE))
+    )(
+        start, outer_first, foot_rows, outer, interp_weights, phase, illumination,
+        transform_table(SIDE),
+    )
 
     cm = cm_values.reshape(rowblk * positions * rb * comps, cbs)
     gathered = lax.all_to_all(words, "tile", 0, 0).reshape(-1, LANES)

time: 52.1 us -> 52.4 us (level)
  blocking collectives: 35 us -> 36.7 us
  waiting for transfers between devices: 2.58 us -> 0.89 us
    ppermute x2, waiting for transfers between devices: 2.58 us -> 0.89 us  [swap(): return lax.ppermute(block, DEVICES, route)]
    all_to_all x1, blocking collectives: 17.7 us -> 19.2 us  [on_device(): gathered = lax.all_to_all(words, 'tile', 0, 0).reshape(-1, LANES)]
  transfers between devices with their start and end apart: 2 -> 2, of which waited for: 2 -> 1; matrix products, arithmetic and copies ran while one was open for 0% -> 0% of each run, Pallas kernels for 6% -> 7%
where the time goes in v3:
time: 52.4 us; the launch traced here: 52.2 us
  blocking collectives  36.7 us (70%)
  Pallas kernels  9.63 us (18%)
  starting transfers between devices  2.76 us (5%)
  local copies, waits for them, and re-layouts  1.45 us (3%)
  waiting for transfers between devices  0.89 us (2%)
  between operations  0.76 us (1%)
    all_to_all x1, blocking collectives, on_device(): gathered = lax.all_to_all(words, 'tile', 0, 0).reshape(-1, LANES)  19.2 us
    all_to_all x1, blocking collectives, on_device(): got = lax.all_to_all(sent, DEVICES, 0, 0)  17.5 us
    pallas_call x1, Pallas kernels, on_device(): pl.pallas_call(lambda *refs: sense_own(*refs, total=total), in_specs=[sme...  3.56 us
    pallas_call x1, Pallas kernels, on_device(): pl.pallas_call(lambda *refs: sense_rest(*refs, total=total), in_specs=[sm...  2.87 us
    ppermute x2, starting transfers between devices, swap(): return lax.ppermute(block, DEVICES, route)  2.76 us
    unnamed x22, local copies, waits for them, and re-layouts  1.45 us
    pallas_call x1, Pallas kernels, on_device(): pl.pallas_call(edges, in_specs=[smem, pl.BlockSpec(memory_space=pltpu.HBM...  1.36 us
    pallas_call x1, Pallas kernels, on_device(): pl.pallas_call(lambda *refs: reconstruct(*refs, rb=rb, share=1.0 / groups...  1.13 us
  transfers between devices with their start and end apart: 2, of which 1 were waited for; matrix products, arithmetic and copies ran while one was open for 0% of the time, Pallas kernels for 7%

profile of v3, /device:TPU:1, one launch (start us, length us, event | category | flops | bytes accessed | tf_op | source)
XLA Modules:
  0.0 52.2 jit_solution(16604707089100433115)
XLA Ops:
  0.6 0.0 copy-start
  0.6 0.0 copy-start.6
  0.7 0.0 copy-start.7
  0.7 0.0 copy-start.8
  0.7 0.0 copy-start.9
  0.7 0.0 copy-start.10
  0.7 1.4 %edges.1 = (bf16[3,256,256]{2,1,0:T(8,128)(2,1)S(1)}, bf16[3,256,256]{2,1,0:T(8,128)(2,1)S(1)}) custom-call(s32[1]{0:T(128)} %bitcast.1.odd_ref, bf16[3,1024,256]{2,1,0:T(8,128)(2,1)} %refs_8_.1), custom_call_target="tpu_custom_call" | custom-call | tf_op jit(solution)/shard_map/edges/pallas_call | solution.py:294
  2.1 1.5 %collective-permute-start.1 = (bf16[3,256,256]{2,1,0:T(8,128)(2,1)S(1)}, bf16[3,256,256]{2,1,0:T(8,128)(2,1)S(1)}, u32[]{:S(2)}, u32[]{:S(2)}) collective-permute-start(bf16[3,256,256]{2,1,0:T(8,128)(2,1)S(1)} %get-tuple-element.10), channel_id=1, source_target_pairs={{0,1},{1,0},{2,3},{3,2},{4,5},{5,4},{6,7},{7,6},{8,9},{9,8},{10,11... | collective-permute-start | bytes 1179656 | tf_op jit(solution)/shard_map/ppermute | solution.py:20
  3.5 1.3 %collective-permute-start = (bf16[3,256,256]{2,1,0:T(8,128)(2,1)S(1)}, bf16[3,256,256]{2,1,0:T(8,128)(2,1)S(1)}, u32[]{:S(2)}, u32[]{:S(2)}) collective-permute-start(bf16[3,256,256]{2,1,0:T(8,128)(2,1)S(1)} %get-tuple-element.9), channel_id=1, source_target_pairs={{0,127},{1,2},{2,1},{3,4},{4,3},{5,6},{6,5},{7,8},{8,7},{9,10},{10... | collective-permute-start | bytes 1179656 | tf_op jit(solution)/shard_map/ppermute | solution.py:20
  4.8 0.0 collective-permute-done.1.refs_9_
  4.9 0.0 copy-done
  4.9 0.0 copy-done.6
  4.9 0.0 copy-start.1
  4.9 1.4 %copy-done.1 = bf16[3,4,256,256]{3,2,1,0:T(8,128)(2,1)S(1)} copy-done((bf16[3,4,256,256]{3,2,1,0:T(8,128)(2,1)S(1)}, bf16[3,4,256,256]{3,2,1,0:T(8,128)(2,1)}, u32[]{:S(2)}) %copy-start.1) | copy-done | bytes 1572888
  6.3 3.6 %sense_own.1 = (f32[256,256]{1,0:T(8,128)S(1)}, s32[32,128]{1,0:T(8,128)S(1)}, f32[12,128]{1,0:T(8,128)S(1)}) custom-call(s32[1]{0:T(128)} %bitcast.refs_0_, s32[1]{0:T(128)S(6)} %sub.11.refs_1_, s32[1]{0:T(128)} %bitcast.3.refs_2_, f32[3]{0:T(128)S(1)} %copy-done.10, s32[3,4,256]{2,1,0:T(4,128)S(1)} %bitcast.12, s32[4,28]{1,0:T(4,128)S(1)} %bitcast.14, ...), custom_call_target="tpu_custom_call" | custom-call | tf_op jit(solution)/shard_map/sense_own/pallas_call | solution.py:311
  9.9 0.8 %collective-permute-done.refs_3_ = bf16[3,256,256]{2,1,0:T(8,128)(2,1)S(1)} collective-permute-done((bf16[3,256,256]{2,1,0:T(8,128)(2,1)S(1)}, bf16[3,256,256]{2,1,0:T(8,128)(2,1)S(1)}, u32[]{:S(2)}, u32[]{:S(2)}) %collective-permute-start) | collective-permute-done | bytes 393248 | tf_op jit(solution)/shard_map/ppermute | solution.py:20
  10.7 0.0 copy-done.2
  10.7 0.0 copy-start.3
  10.8 2.9 %sense_rest.1 = (f32[2,256]{1,0:T(2,128)}, f32[32,4,128]{2,1,0:T(4,128)S(1)}) custom-call(s32[1]{0:T(128)} %bitcast.refs_0_, s32[1]{0:T(128)S(6)} %sub.9.refs_1_, s32[3,4,256]{2,1,0:T(4,128)S(1)} %bitcast.13, bf16[3,256,256]{2,1,0:T(8,128)(2,1)S(1)} %collective-permute-done.refs_3_, bf16[3,4,256,256]{3,2,1,0:T(8,128)(2,1)S(1)} %copy-done.2, ...), custom_call_target="tpu_custom_call" | custom-call | tf_op jit(solution)/shard_map/sense_rest/pallas_call | solution.py:325
  13.6 19.2 %all_to_all.10 = f32[32,4,128]{2,1,0:T(4,128)S(1)} all-to-all(f32[32,4,128]{2,1,0:T(4,128)S(1)} %get-tuple-element.13), channel_id=1, replica_groups=mesh['grp'=4,'tile'=32] {'tile'}, dimensions={0} | all-to-all | bytes 131072 | tf_op jit(solution)/shard_map/all_to_all | solution.py:340
  32.8 0.0 copy-done.3
  32.8 1.1 %reconstruct.1 = f32[128,4,128]{2,1,0:T(4,128)S(1)} custom-call(f32[128,128]{1,0:T(8,128)S(1)} %bitcast.11, bf16[3584,128]{1,0:T(8,128)(2,1)S(1)} %bitcast.10, s32[32,128]{1,0:T(8,128)S(1)} %get-tuple-element.14.refs_2_, f32[12,128]{1,0:T(8,128)S(1)} %get-tuple-element.15.refs_3_.refs_2_), custom_call_target="tpu_custom_call" | custom-call | tf_op jit(solution)/shard_map/reconstruct/pallas_call | solution.py:341
  34.0 17.5 %all_to_all.11.refs_1_ = f32[128,4,128]{2,1,0:T(4,128)S(1)} all-to-all(f32[128,4,128]{2,1,0:T(4,128)S(1)} %reconstruct.1), channel_id=1, replica_groups=mesh['grp'=4,'tile'=32] {'grp','tile'}, dimensions={0} | all-to-all | bytes 524288 | tf_op jit(solution)/shard_map/all_to_all | solution.py:348
  51.5 0.7 %settle.1 = f32[448]{0:T(512)} custom-call(s32[1]{0:T(128)} %bitcast.7.refs_0_, f32[128,4,128]{2,1,0:T(4,128)S(1)} %all_to_all.11.refs_1_, f32[12,128]{1,0:T(8,128)S(1)} %get-tuple-element.15.refs_3_.refs_2_), custom_call_target="tpu_custom_call" | custom-call | tf_op jit(solution)/shard_map/settle/pallas_call | solution.py:350
  (9 shorter events, 0.0 us)
Async XLA Ops:
  0.6 4.2 %copy-start = (bf16[3,1024,256]{2,1,0:T(8,128)(2,1)S(1)}, bf16[3,1024,256]{2,1,0:T(8,128)(2,1)}, u32[]{:S(2)}) copy-start(bf16[3,1024,256]{2,1,0:T(8,128)(2,1)} %refs_8_.1) | copy-start | bytes 4718596
  0.6 4.2 %copy-start.6 = (s32[256,3,4]{0,2,1:T(4,128)S(1)}, s32[256,3,4]{0,2,1:T(4,128)}, u32[]{:S(2)}) copy-start(s32[256,3,4]{0,2,1:T(4,128)} %param.12) | copy-start | bytes 36868
  0.7 4.2 %copy-start.7 = (s32[28,4]{0,1:T(4,128)S(1)}, s32[28,4]{0,1:T(4,128)}, u32[]{:S(2)}) copy-start(s32[28,4]{0,1:T(4,128)} %param.15) | copy-start | bytes 1348
  0.7 4.2 %copy-start.8 = (s32[448]{0:T(512)S(1)}, s32[448]{0:T(512)}, u32[]{:S(2)}) copy-start(s32[448]{0:T(512)} %param.17) | copy-start | bytes 5380
  0.7 4.2 %copy-start.9 = (f32[448]{0:T(512)S(1)}, f32[448]{0:T(512)}, u32[]{:S(2)}) copy-start(f32[448]{0:T(512)} %param.16) | copy-start | bytes 5380
  0.7 4.2 %copy-start.10 = (f32[3]{0:T(128)S(1)}, f32[3]{0:T(128)}, u32[]{:S(2)}) copy-start(f32[3]{0:T(128)} %refs_3_.1) | copy-start | bytes 40
  2.1 2.8 %collective-permute-start.1 = (bf16[3,256,256]{2,1,0:T(8,128)(2,1)S(1)}, bf16[3,256,256]{2,1,0:T(8,128)(2,1)S(1)}, u32[]{:S(2)}, u32[]{:S(2)}) collective-permute-start(bf16[3,256,256]{2,1,0:T(8,128)(2,1)S(1)} %get-tuple-element.10), channel_id=1, source_target_pairs={{0,1},{1,0},{2,3},{3,2},{4,5},{5,4},{6,7},{7,6},{8,9},{9,8},{10,11... | collective-permute-start | bytes 1179656 | tf_op jit(solution)/shard_map/ppermute | solution.py:20
  3.5 7.2 %collective-permute-start = (bf16[3,256,256]{2,1,0:T(8,128)(2,1)S(1)}, bf16[3,256,256]{2,1,0:T(8,128)(2,1)S(1)}, u32[]{:S(2)}, u32[]{:S(2)}) collective-permute-start(bf16[3,256,256]{2,1,0:T(8,128)(2,1)S(1)} %get-tuple-element.9), channel_id=1, source_target_pairs={{0,127},{1,2},{2,1},{3,4},{4,3},{5,6},{6,5},{7,8},{8,7},{9,10},{10... | collective-permute-start | bytes 1179656 | tf_op jit(solution)/shard_map/ppermute | solution.py:20
  4.9 1.4 %copy-start.1 = (bf16[3,4,256,256]{3,2,1,0:T(8,128)(2,1)S(1)}, bf16[3,4,256,256]{3,2,1,0:T(8,128)(2,1)}, u32[]{:S(2)}) copy-start(bf16[3,4,256,256]{3,2,1,0:T(8,128)(2,1)} %refs_4_.1) | copy-start | bytes 4718596
  6.3 4.4 %copy-start.2 = (bf16[3,4,256,256]{3,2,1,0:T(8,128)(2,1)S(1)}, bf16[3,4,256,256]{3,2,1,0:T(8,128)(2,1)}, u32[]{:S(2)}) copy-start(bf16[3,4,256,256]{3,2,1,0:T(8,128)(2,1)} %refs_4_.1) | copy-start | bytes 4718596
  6.3 4.4 %copy-start.4 = (bf16[512,512]{1,0:T(8,128)(2,1)S(1)}, bf16[512,512]{1,0:T(8,128)(2,1)}, u32[]{:S(2)}) copy-start(bf16[512,512]{1,0:T(8,128)(2,1)} %constant.38.clone.refs_7_) | copy-start | bytes 1572868
  6.3 4.4 %copy-start.5 = (f32[256,256]{1,0:T(8,128)S(1)}, f32[256,256]{1,0:T(8,128)}, u32[]{:S(2)}) copy-start(f32[256,256]{1,0:T(8,128)} %refs_6_.1) | copy-start | bytes 786436
  10.7 22.1 %copy-start.3 = (bf16[28,4,16,2,128]{4,3,2,1,0:T(2,128)(2,1)S(1)}, bf16[28,4,16,2,128]{4,3,2,1,0:T(2,128)(2,1)}, u32[]{:S(2)}) copy-start(bf16[28,4,16,2,128]{4,3,2,1,0:T(2,128)(2,1)} %param.14) | copy-start | bytes 2752516

commit v4 on v3

--- a/solution.py
+++ b/solution.py
@@ -90,9 +90,74 @@
         copy.wait()
 
 
+def mirror_rows(
+    base_ref, gain_ref, cols_ref, owner_ref, prev_ref, cm_ref, sent_ref, spot_ref, state_ref
+):
+    tiles, rows_sent, _ = sent_ref.shape
+    mirrors = gain_ref.shape[0]
+    positions, rowblk = cols_ref.shape
+    acts = owner_ref.shape[1]
+    rb = acts // rowblk
+    cols = (cols_ref[...] - base_ref[0]).astype(jnp.float32)
+    lane = lax.broadcasted_iota(jnp.int32, (positions, LANES), 1)
+    place = lax.broadcasted_iota(jnp.int32, (positions, LANES), 0)
+    spread = jnp.where(lane // (2 * rb) == place, 1.0, 0.0)
+    cols = lax.dot_general(
+        cols, spread, (((0,), (0,)), ((), ())), preferred_element_type=jnp.float32
+    ).astype(jnp.int32)
+    comp = lax.broadcasted_iota(jnp.int32, cols.shape, 1) % 2
+    height = spot_ref.shape[0]
+    spot_ref[...] = jnp.concatenate(
+        [cols * 2 + comp, jnp.full((height - rowblk, LANES), -1, jnp.int32)], 0
+    )
+    owner = owner_ref[...]
+    act = lax.broadcasted_iota(jnp.int32, (rowblk, acts), 1)
+    block = lax.broadcasted_iota(jnp.int32, (rowblk, acts), 0)
+    held = jnp.where(act // rb == block, owner, 0).astype(jnp.float32).astype(jnp.bfloat16)
+    act = lax.broadcasted_iota(jnp.int32, (acts, LANES), 0)
+    wide = lax.broadcasted_iota(jnp.int32, (acts, LANES), 1)
+    spread = jnp.where(act % rb == (wide % (2 * rb)) // 2, 1.0, 0.0).astype(jnp.bfloat16)
+    owners = jnp.dot(held, spread, preferred_element_type=jnp.float32)
+    target = cols * (2 * mirrors) + comp * mirrors + owners.astype(jnp.int32)
+
+    used = 4 * mirrors
+    row = lax.broadcasted_iota(jnp.int16, (tiles * used, LANES), 0)
+    one, zero = jnp.bfloat16(1), jnp.bfloat16(0)
+    picks = [
+        jnp.where(
+            row == jnp.broadcast_to(target[i : i + 1, :], row.shape).astype(jnp.int16), one, zero
+        )
+        for i in range(rowblk)
+    ]
+    sums = jnp.dot(
+        jnp.concatenate(picks, 1), cm_ref[...], preferred_element_type=jnp.float32
+    )
+    lane = lax.broadcasted_iota(jnp.int32, (1, LANES), 1)
+    extra = jnp.zeros((1, LANES), jnp.float32)
+    gain = jnp.zeros(owner.shape, jnp.float32)
+    for m in range(mirrors):
+        mine = owner == m
+        gain = jnp.where(mine, gain_ref[m], gain)
+        prev = jnp.sum(jnp.where(mine, prev_ref[...], 0.0), axis=1, keepdims=True)
+        number = jnp.sum(jnp.where(mine, 1.0, 0.0), axis=1, keepdims=True)
+        extra = jnp.where(lane == m, prev, jnp.where(lane == mirrors + m, number, extra))
+    for t in range(tiles):
+        sent_ref[t, 0:used, :] = sums[t * used : (t + 1) * used]
+    sent_ref[:, used : used + 1, :] = jnp.broadcast_to(extra[None], (tiles, 1, LANES))
+    left = rows_sent - used - 1
+    sent_ref[:, used + 1 :, :] = jnp.zeros((tiles, left, LANES), jnp.float32)
+
+    lines = height * rb // LANES
+    missing = lines * LANES - acts
+    rows = []
+    for values, fill in ((owner.astype(jnp.float32), -1.0), (prev_ref[...], 0.0), (gain, 0.0)):
+        values = jnp.concatenate([values, jnp.full((1, missing), fill, jnp.float32)], 1)
+        rows += [values[:, i * LANES : (i + 1) * LANES] for i in range(lines)]
+    state_ref[...] = jnp.concatenate(rows, 0)
+
+
 def sense_own(
-    start_ref, first_ref, base_ref, gain_ref, foot_ref, cols_ref, owner_ref, prev_ref,
-    screens_ref, inner_ref, weights_ref, phase_ref, spot_ref, state_ref, *, total
+    start_ref, first_ref, foot_ref, screens_ref, inner_ref, weights_ref, phase_ref, *, total
 ):
     layers, foot, _ = foot_ref.shape
     blocks, pixels = screens_ref.shape[1:]
@@ -118,34 +183,6 @@
         )
         phase = part if phase is None else phase + part
     phase_ref[...] = phase
-
-    positions, rowblk = cols_ref.shape
-    acts = owner_ref.shape[1]
-    rb = acts // rowblk
-    cols = (cols_ref[...] - base_ref[0]).astype(jnp.float32)
-    lane = lax.broadcasted_iota(jnp.int32, (positions, LANES), 1)
-    place = lax.broadcasted_iota(jnp.int32, (positions, LANES), 0)
-    spread = jnp.where(lane // (2 * rb) == place, 1.0, 0.0)
-    cols = lax.dot_general(
-        cols, spread, (((0,), (0,)), ((), ())), preferred_element_type=jnp.float32
-    )
-    comp = lax.broadcasted_iota(jnp.int32, cols.shape, 1) % 2
-    spot = cols.astype(jnp.int32) * 2 + comp
-    height = spot_ref.shape[0]
-    spot_ref[...] = jnp.concatenate(
-        [spot, jnp.full((height - rowblk, LANES), -1, jnp.int32)], 0
-    )
-    lines = height * rb // LANES
-    owner = owner_ref[...]
-    gain = jnp.zeros(owner.shape, jnp.float32)
-    for m in range(gain_ref.shape[0]):
-        gain = jnp.where(owner == m, gain_ref[m], gain)
-    missing = lines * LANES - acts
-    rows = []
-    for values, fill in ((owner.astype(jnp.float32), -1.0), (prev_ref[...], 0.0), (gain, 0.0)):
-        values = jnp.concatenate([values, jnp.full((1, missing), fill, jnp.float32)], 1)
-        rows += [values[:, i * LANES : (i + 1) * LANES] for i in range(lines)]
-    state_ref[...] = jnp.concatenate(rows, 0)
 
 
 def sense_rest(
@@ -187,11 +224,34 @@
     slopes_ref[...] = slopes
     words = slopes.astype(jnp.bfloat16).astype(jnp.float32)
     words = [words[:, h * LANES : (h + 1) * LANES] for h in range(subs // LANES)]
-    words_ref[...] = jnp.broadcast_to(jnp.concatenate(words, 0)[None], words_ref.shape)
-
-
-def reconstruct(words_ref, cm_ref, spot_ref, state_ref, sent_ref, *, rb, share, mirrors):
-    words = words_ref[...].astype(jnp.bfloat16)
+    words_ref[...] = jnp.concatenate(words, 0)
+
+
+def pack(words_ref, rows_ref, sent_ref, extra_ref, *, mirrors):
+    words = words_ref[...]
+    sums = jnp.sum(rows_ref[...], axis=0)
+    lane = lax.broadcasted_iota(jnp.int32, (1, LANES), 1)
+    line = jnp.zeros((1, LANES), jnp.float32)
+    for m in range(mirrors):
+        product = jnp.zeros((1, LANES), jnp.float32)
+        for k in range(words.shape[0]):
+            at = k * mirrors + m
+            product = product + sums[at : at + 1] * words[k : k + 1]
+        line = jnp.where(lane == m, jnp.sum(product, axis=1, keepdims=True), line)
+    high = line.astype(jnp.bfloat16).astype(jnp.float32)
+    middle = (line - high).astype(jnp.bfloat16).astype(jnp.float32)
+    low = line - high - middle
+    rows = jnp.concatenate([words, high, middle, low, jnp.zeros_like(low)], 0)
+    sent_ref[...] = jnp.broadcast_to(rows.astype(jnp.bfloat16)[None], sent_ref.shape)
+    used = words.shape[0] * mirrors
+    extra_ref[...] = sums[used : used + 1]
+
+
+def reconstruct(words_ref, cm_ref, spot_ref, sent_ref, *, rb):
+    got = words_ref[...].astype(jnp.float32)
+    words = got[:, :4, :].reshape(-1, LANES).astype(jnp.bfloat16)
+    line = jnp.sum(got, axis=0)
+    line = line[4:5] + line[5:6] + line[6:7]
     rowblk = cm_ref.shape[0] // LANES
     row = lax.broadcasted_iota(jnp.int32, (words.shape[0], LANES), 0)
     parts = []
@@ -218,46 +278,29 @@
     block = lax.broadcasted_iota(jnp.int32, spread.shape, 0)
     lane = lax.broadcasted_iota(jnp.int32, spread.shape, 1)
     spread = jnp.where(lane // rb == block % per, spread, 0.0)
-    lines = height // per
-    recon = jnp.sum(spread.reshape(lines, per, LANES), axis=1)
+    recon = jnp.sum(spread.reshape(height // per, per, LANES), axis=1)
+    rest = sent_ref.shape[1] - recon.shape[0] - 1
+    rows = jnp.concatenate([recon, line, jnp.zeros((rest, LANES), jnp.float32)], 0)
+    sent_ref[...] = jnp.broadcast_to(rows[None], sent_ref.shape)
+
+
+def settle(got_ref, extra_ref, state_ref, commands_ref, *, mirrors):
+    lines = state_ref.shape[0] // 3
+    sums = jnp.sum(got_ref[...], axis=0)
+    line = sums[lines : lines + 1]
+    extra = extra_ref[...]
+    lane = lax.broadcasted_iota(jnp.int32, line.shape, 1)
+
+    def entry(values, at):
+        return jnp.sum(jnp.where(lane == at, values, 0.0), axis=1, keepdims=True)
+
     owner = state_ref[:lines]
-    updated = state_ref[lines : 2 * lines] * share - state_ref[2 * lines :] * recon
-    row = lax.broadcasted_iota(jnp.int32, recon.shape, 0)
-    lane = lax.broadcasted_iota(jnp.int32, recon.shape, 1)
-    last = row == lines - 1
-    for m in range(mirrors):
-        mine = owner == float(m)
-        recon = jnp.where(
-            last & (lane == LANES - 2 * mirrors + m),
-            jnp.sum(jnp.where(mine, updated, 0.0), keepdims=True),
-            recon,
-        )
-        recon = jnp.where(
-            last & (lane == LANES - mirrors + m),
-            jnp.sum(jnp.where(mine, share, 0.0), keepdims=True),
-            recon,
-        )
-    sent_ref[...] = jnp.broadcast_to(recon[None], sent_ref.shape)
-
-
-def settle(tile_ref, got_ref, state_ref, commands_ref, *, groups, mirrors):
-    count, lines, _ = got_ref.shape
-    tiles = count // groups
-    recon = got_ref[tile_ref[0]]
-    for g in range(1, groups):
-        recon = recon + got_ref[g * tiles + tile_ref[0]]
-    last = jnp.sum(got_ref[:, lines - 1, :], axis=0, keepdims=True)
-    lane = lax.broadcasted_iota(jnp.int32, last.shape, 1)
-
-    def entry(at):
-        return jnp.sum(jnp.where(lane == at, last, 0.0), axis=1, keepdims=True)
-
-    owner = state_ref[:lines]
+    gain = state_ref[2 * lines :]
     piston = jnp.zeros(owner.shape, jnp.float32)
     for m in range(mirrors):
-        mean = entry(LANES - 2 * mirrors + m) / entry(LANES - mirrors + m)
-        piston = jnp.where(owner == float(m), mean, piston)
-    commands = state_ref[lines : 2 * lines] - state_ref[2 * lines :] * recon - piston
+        total = entry(extra, m) - gain * entry(line, m)
+        piston = jnp.where(owner == float(m), total / entry(extra, mirrors + m), piston)
+    commands = state_ref[lines : 2 * lines] - gain * sums[:lines] - piston
     acts = commands_ref.shape[0]
     for i in range(lines):
         some = min(LANES, acts - i * LANES)
@@ -282,7 +325,7 @@
     rowblk, positions, rb, comps, cbs = cm_values.shape
     acts = rowblk * rb
     mirrors = dm_gain.shape[0]
-    height = -(-(acts + 2 * mirrors) // LANES) * LANES // rb
+    height = -(-acts // LANES) * LANES // rb
     lines = height * rb // LANES
     smem = pl.BlockSpec(memory_space=pltpu.SMEM)
     vmem = pl.BlockSpec(memory_space=pltpu.VMEM)
@@ -305,29 +348,39 @@
     outer_first = odd * (blk_dev + EDGE) - EDGE
     inner_first = (1 - odd) * (blk_dev + EDGE) - EDGE
 
-    start = (lax.axis_index(DEVICES) * blk_dev).astype(jnp.int32).reshape(1)
     base = (lax.axis_index("grp") * (tiles * subs // cbs)).astype(jnp.int32).reshape(1)
-    foot_rows = jnp.transpose(footprint, (1, 2, 0))
-    phase, spot, state = pl.pallas_call(
-        lambda *refs: sense_own(*refs, total=total),
-        in_specs=[smem] * 4 + [vmem] * 7,
+    cm = cm_values.reshape(rowblk * positions * rb * comps, cbs)
+    rows, spot, state = pl.pallas_call(
+        mirror_rows,
+        in_specs=[smem] * 2 + [vmem] * 4,
         out_shape=(
-            jax.ShapeDtypeStruct((subs, pixels), f32),
+            jax.ShapeDtypeStruct((tiles, 16, LANES), f32),
             jax.ShapeDtypeStruct((height, LANES), jnp.int32),
             jax.ShapeDtypeStruct((3 * lines, LANES), f32),
         ),
         compiler_params=limit,
+        name="mirror_rows",
+    )(
+        base, dm_gain, cm_columns.T, owner_map.reshape(1, acts), prev_commands.reshape(1, acts), cm
+    )
+    start = (lax.axis_index(DEVICES) * blk_dev).astype(jnp.int32).reshape(1)
+    foot_rows = jnp.transpose(footprint, (1, 2, 0))
+    rows, foot_rows = lax.optimization_barrier((rows, foot_rows))
+    rows = lax.all_to_all(rows, "tile", 0, 0)
+
+    phase = pl.pallas_call(
+        lambda *refs: sense_own(*refs, total=total),
+        in_specs=[smem] * 2 + [vmem] * 4,
+        out_shape=jax.ShapeDtypeStruct((subs, pixels), f32),
+        compiler_params=limit,
         name="sense_own",
-    )(
-        start, inner_first, base, dm_gain, foot_rows, cm_columns.T, owner_map.reshape(1, acts),
-        prev_commands.reshape(1, acts), screens, inner, interp_weights,
-    )
+    )(start, inner_first, foot_rows, screens, inner, interp_weights)
     slopes, words = pl.pallas_call(
         lambda *refs: sense_rest(*refs, total=total),
         in_specs=[smem] * 2 + [vmem] * 6,
         out_shape=(
             jax.ShapeDtypeStruct((2, subs), f32),
-            jax.ShapeDtypeStruct((tiles, 2 * subs // LANES, LANES), f32),
+            jax.ShapeDtypeStruct((2 * subs // LANES, LANES), f32),
         ),
         compiler_params=limit,
         name="sense_rest",
@@ -335,25 +388,33 @@
         start, outer_first, foot_rows, outer, interp_weights, phase, illumination,
         transform_table(SIDE),
     )
-
-    cm = cm_values.reshape(rowblk * positions * rb * comps, cbs)
-    gathered = lax.all_to_all(words, "tile", 0, 0).reshape(-1, LANES)
+    packed, extra = pl.pallas_call(
+        lambda *refs: pack(*refs, mirrors=mirrors),
+        in_specs=[vmem] * 2,
+        out_shape=(
+            jax.ShapeDtypeStruct((tiles, 8, LANES), jnp.bfloat16),
+            jax.ShapeDtypeStruct((1, LANES), f32),
+        ),
+        compiler_params=limit,
+        name="pack",
+    )(words, rows)
+
+    gathered = lax.all_to_all(packed, "tile", 0, 0)
     sent = pl.pallas_call(
-        lambda *refs: reconstruct(*refs, rb=rb, share=1.0 / groups, mirrors=mirrors),
-        in_specs=[vmem] * 4,
-        out_shape=jax.ShapeDtypeStruct((groups * tiles, lines, LANES), f32),
+        lambda *refs: reconstruct(*refs, rb=rb),
+        in_specs=[vmem] * 3,
+        out_shape=jax.ShapeDtypeStruct((groups, 8, LANES), f32),
         compiler_params=limit,
         name="reconstruct",
-    )(gathered, cm, spot, state)
-    got = lax.all_to_all(sent, DEVICES, 0, 0)
-    tile = lax.axis_index("tile").astype(jnp.int32).reshape(1)
+    )(gathered, cm, spot)
+    got = lax.all_to_all(sent, "grp", 0, 0)
     commands = pl.pallas_call(
-        lambda *refs: settle(*refs, groups=groups, mirrors=mirrors),
-        in_specs=[smem, vmem, vmem],
+        lambda *refs: settle(*refs, mirrors=mirrors),
+        in_specs=[vmem] * 3,
         out_shape=jax.ShapeDtypeStruct((acts,), f32),
         compiler_params=limit,
         name="settle",
-    )(tile, got, state)
+    )(got, extra, state)
     return (slopes, commands)
 
 

time: 52.4 us -> 50.3 us (0.960)
  blocking collectives: 36.7 us -> 19.6 us
  starting transfers between devices: 2.76 us -> 13.9 us
  Pallas kernels: 9.63 us -> 11.3 us
  local copies, waits for them, and re-layouts: 1.45 us -> 2.62 us
  waiting for transfers between devices: 0.89 us -> 1.58 us
    all_to_all x2, blocking collectives: 36.7 us -> 19.6 us  [the longest x1 13 us: on_device(): gathered = lax.all_to_all(packed, 'tile', 0, 0)]
    all_to_all x0 -> x1, starting transfers between devices: none -> 11.1 us  [on_device(): rows = lax.all_to_all(rows, 'tile', 0, 0)]
    pallas_call x2 -> x4, Pallas kernels: 1.85 us -> 4.07 us  [the longest x1 2.3 us: on_device(): pl.pallas_call(mirror_rows, in_specs=[smem] * 2 + [vmem] * 4, out_shape=(...]
    all_to_all x0 -> x1, waiting for transfers between devices: none -> 1.58 us  [on_device(): rows = lax.all_to_all(rows, 'tile', 0, 0)]
    unnamed x22 -> x24, local copies, waits for them, and re-layouts: 1.45 us -> 2.62 us
    ppermute x2, waiting for transfers between devices: 0.89 us -> 0.01 us  [swap(): return lax.ppermute(block, DEVICES, route)]
    pallas_call x1, Pallas kernels: 3.56 us -> 3.01 us  [on_device(): pl.pallas_call(lambda *refs: sense_own(*refs, total=total), in_specs=[sme...]
  transfers between devices with their start and end apart: 2 -> 3, of which waited for: 1 -> 1; matrix products, arithmetic and copies ran while one was open for 0% -> 0% of each run, Pallas kernels for 7% -> 16%
where the time goes in v4:
time: 50.3 us; the launch traced here: 49.8 us
  blocking collectives  19.6 us (39%)
  starting transfers between devices  13.9 us (28%)
  Pallas kernels  11.3 us (22%)
  local copies, waits for them, and re-layouts  2.62 us (5%)
  waiting for transfers between devices  1.58 us (3%)
  between operations  0.83 us (2%)
    all_to_all x1, blocking collectives, on_device(): gathered = lax.all_to_all(packed, 'tile', 0, 0)  13 us
    all_to_all x1, starting transfers between devices, on_device(): rows = lax.all_to_all(rows, 'tile', 0, 0)  11.1 us
    all_to_all x1, blocking collectives, on_device(): got = lax.all_to_all(sent, 'grp', 0, 0)  6.56 us
    pallas_call x1, Pallas kernels, on_device(): pl.pallas_call(lambda *refs: sense_own(*refs, total=total), in_specs=[sme...  3.01 us
    pallas_call x1, Pallas kernels, on_device(): pl.pallas_call(lambda *refs: sense_rest(*refs, total=total), in_specs=[sm...  2.88 us
    ppermute x2, starting transfers between devices, swap(): return lax.ppermute(block, DEVICES, route)  2.76 us
    unnamed x24, local copies, waits for them, and re-layouts  2.62 us
    pallas_call x1, Pallas kernels, on_device(): pl.pallas_call(mirror_rows, in_specs=[smem] * 2 + [vmem] * 4, out_shape=(...  2.3 us
  transfers between devices with their start and end apart: 3, of which 1 were waited for; matrix products, arithmetic and copies ran while one was open for 0% of the time, Pallas kernels for 16%

profile of v4, /device:TPU:1, one launch (start us, length us, event | category | flops | bytes accessed | tf_op | source)
XLA Modules:
  0.0 49.8 jit_solution(12520733571625367508)
XLA Ops:
  0.6 0.0 copy-start
  0.6 0.0 copy-start.8
  0.7 1.4 %edges.1 = (bf16[3,256,256]{2,1,0:T(8,128)(2,1)S(1)}, bf16[3,256,256]{2,1,0:T(8,128)(2,1)S(1)}) custom-call(s32[1]{0:T(128)} %bitcast.1.odd_ref, bf16[3,1024,256]{2,1,0:T(8,128)(2,1)} %refs_3_.1), custom_call_target="tpu_custom_call" | custom-call | tf_op jit(solution)/shard_map/edges/pallas_call | solution.py:337
  2.1 1.5 %collective-permute-start.1 = (bf16[3,256,256]{2,1,0:T(8,128)(2,1)S(1)}, bf16[3,256,256]{2,1,0:T(8,128)(2,1)S(1)}, u32[]{:S(2)}, u32[]{:S(2)}) collective-permute-start(bf16[3,256,256]{2,1,0:T(8,128)(2,1)S(1)} %get-tuple-element.16), channel_id=1, source_target_pairs={{0,1},{1,0},{2,3},{3,2},{4,5},{5,4},{6,7},{7,6},{8,9},{9,8},{10,11... | collective-permute-start | bytes 1179656 | tf_op jit(solution)/shard_map/ppermute | solution.py:20
  3.5 1.3 %collective-permute-start = (bf16[3,256,256]{2,1,0:T(8,128)(2,1)S(1)}, bf16[3,256,256]{2,1,0:T(8,128)(2,1)S(1)}, u32[]{:S(2)}, u32[]{:S(2)}) collective-permute-start(bf16[3,256,256]{2,1,0:T(8,128)(2,1)S(1)} %get-tuple-element.15), channel_id=1, source_target_pairs={{0,127},{1,2},{2,1},{3,4},{4,3},{5,6},{6,5},{7,8},{8,7},{9,10},{10... | collective-permute-start | bytes 1179656 | tf_op jit(solution)/shard_map/ppermute | solution.py:20
  4.8 0.0 copy-done.11
  4.8 0.0 copy-start.3
  4.9 1.2 %copy-done.3 = bf16[28,4,16,2,128]{4,3,2,1,0:T(2,128)(2,1)S(1)} copy-done((bf16[28,4,16,2,128]{4,3,2,1,0:T(2,128)(2,1)S(1)}, bf16[28,4,16,2,128]{4,3,2,1,0:T(2,128)(2,1)}, u32[]{:S(2)}) %copy-start.3) | copy-done | bytes 917528
  6.0 2.3 %mirror_rows.1 = (f32[32,16,128]{2,1,0:T(8,128)}, s32[32,128]{1,0:T(8,128)S(1)}, f32[12,128]{1,0:T(8,128)S(1)}) custom-call(s32[1]{0:T(128)} %bitcast.2.base_ref, f32[3]{0:T(128)S(1)} %copy-done.11, s32[4,28]{1,0:T(4,128)S(1)} %bitcast.12, s32[1,448]{1,0:T(1,128)S(1)} %bitcast.13, f32[1,448]{1,0:T(1,128)S(1)} %bitcast.14, bf16[3584,128]{1,0:T(8,128)(2,1)S(1)} %bitcast.8), custom_call_target="tpu_custom_call" | custom-call | tf_op jit(solution)/shard_map/mirror_rows/pallas_call | solution.py:353
  8.3 11.1 %all-to-all-start = ((f32[32,16,128]{2,1,0:T(8,128)}), f32[32,16,128]{2,1,0:T(8,128)S(1)}, u32[]{:S(2)}, u32[]{:S(2)}) async-start(f32[32,16,128]{2,1,0:T(8,128)} %get-tuple-element.19), calls=%async_computation | async-start | bytes 524288 | tf_op jit(solution)/shard_map/all_to_all | solution.py:369
  19.5 0.0 collective-permute-done.1.refs_4_
  19.5 0.0 copy-start.1
  19.5 1.4 %copy-done.1 = bf16[3,4,256,256]{3,2,1,0:T(8,128)(2,1)S(1)} copy-done((bf16[3,4,256,256]{3,2,1,0:T(8,128)(2,1)S(1)}, bf16[3,4,256,256]{3,2,1,0:T(8,128)(2,1)}, u32[]{:S(2)}) %copy-start.1) | copy-done | bytes 1572888
  20.9 3.0 %sense_own.1.refs_5_ = f32[256,256]{1,0:T(8,128)S(1)} custom-call(s32[1]{0:T(128)} %bitcast.refs_0_, s32[1]{0:T(128)S(6)} %sub.11.refs_1_, s32[3,4,256]{2,1,0:T(4,128)S(1)} %bitcast.10, bf16[3,1024,256]{2,1,0:T(8,128)(2,1)S(1)} %copy-done, bf16[3,256,256]{2,1,0:T(8,128)(2,1)S(1)} %collective-permute-done.1.refs_4_, bf16[3,4,256,256]{3,2,1,0:T(8,128)(2,1)S(1)} %copy-done.1), custom_call_target="tpu_custom_call" | custom-call | tf_op jit(solution)/shard_map/sense_own/pallas_call | solution.py:371
  23.9 0.0 copy-start.4
  23.9 0.0 collective-permute-done.refs_3_
  24.0 2.9 %sense_rest.1 = (f32[2,256]{1,0:T(2,128)}, f32[4,128]{1,0:T(4,128)S(1)}) custom-call(s32[1]{0:T(128)} %bitcast.refs_0_, s32[1]{0:T(128)S(6)} %sub.9.refs_1_, s32[3,4,256]{2,1,0:T(4,128)S(1)} %bitcast.11, bf16[3,256,256]{2,1,0:T(8,128)(2,1)S(1)} %collective-permute-done.refs_3_, bf16[3,4,256,256]{3,2,1,0:T(8,128)(2,1)S(1)} %copy-done.2, ...), custom_call_target="tpu_custom_call" | custom-call | tf_op jit(solution)/shard_map/sense_rest/pallas_call | solution.py:378
  26.9 1.6 %all-to-all-done.refs_1_ = f32[32,16,128]{2,1,0:T(8,128)S(1)} async-done(((f32[32,16,128]{2,1,0:T(8,128)}), f32[32,16,128]{2,1,0:T(8,128)S(1)}, u32[]{:S(2)}, u32[]{:S(2)}) %all-to-all-start) | async-done | bytes 262176 | tf_op jit(solution)/shard_map/all_to_all | solution.py:369
  28.4 0.1 pack.1
  28.6 13.0 %all_to_all.15.refs_0_ = bf16[32,8,128]{2,1,0:T(8,128)(2,1)S(1)} all-to-all(bf16[32,8,128]{2,1,0:T(8,128)(2,1)S(1)} %get-tuple-element.20), channel_id=1, replica_groups=mesh['grp'=4,'tile'=32] {'tile'}, dimensions={0} | all-to-all | bytes 131072 | tf_op jit(solution)/shard_map/all_to_all | solution.py:402
  41.6 0.0 copy-done.4
  41.6 1.0 %reconstruct.1 = f32[4,8,128]{2,1,0:T(8,128)S(1)} custom-call(bf16[32,8,128]{2,1,0:T(8,128)(2,1)S(1)} %all_to_all.15.refs_0_, bf16[3584,128]{1,0:T(8,128)(2,1)S(1)} %bitcast.9, s32[32,128]{1,0:T(8,128)S(1)} %get-tuple-element.21.refs_2_), custom_call_target="tpu_custom_call" | custom-call | tf_op jit(solution)/shard_map/reconstruct/pallas_call | solution.py:403
  42.6 6.6 %all_to_all.16.refs_0_ = f32[4,8,128]{2,1,0:T(8,128)S(1)} all-to-all(f32[4,8,128]{2,1,0:T(8,128)S(1)} %reconstruct.1), channel_id=1, replica_groups=mesh['grp'=4,'tile'=32] {'grp'}, dimensions={0} | all-to-all | bytes 32768 | tf_op jit(solution)/shard_map/all_to_all | solution.py:410
  49.2 0.7 %settle.1 = f32[448]{0:T(512)} custom-call(f32[4,8,128]{2,1,0:T(8,128)S(1)} %all_to_all.16.refs_0_, f32[1,128]{1,0:T(1,128)S(1)} %get-tuple-element.22.refs_1_, f32[12,128]{1,0:T(8,128)S(1)} %get-tuple-element.23.refs_2_), custom_call_target="tpu_custom_call" | custom-call | tf_op jit(solution)/shard_map/settle/pallas_call | solution.py:411
  (15 shorter events, 0.0 us)
Async XLA Ops:
  0.6 18.9 %copy-start = (bf16[3,1024,256]{2,1,0:T(8,128)(2,1)S(1)}, bf16[3,1024,256]{2,1,0:T(8,128)(2,1)}, u32[]{:S(2)}) copy-start(bf16[3,1024,256]{2,1,0:T(8,128)(2,1)} %refs_3_.1) | copy-start | bytes 4718596
  0.6 4.2 %copy-start.8 = (s32[28,4]{0,1:T(4,128)S(1)}, s32[28,4]{0,1:T(4,128)}, u32[]{:S(2)}) copy-start(s32[28,4]{0,1:T(4,128)} %param.15) | copy-start | bytes 1348
  0.7 4.2 %copy-start.9 = (s32[448]{0:T(512)S(1)}, s32[448]{0:T(512)}, u32[]{:S(2)}) copy-start(s32[448]{0:T(512)} %param.17) | copy-start | bytes 5380
  0.7 4.2 %copy-start.10 = (f32[448]{0:T(512)S(1)}, f32[448]{0:T(512)}, u32[]{:S(2)}) copy-start(f32[448]{0:T(512)} %param.16) | copy-start | bytes 5380
  0.7 4.2 %copy-start.11 = (f32[3]{0:T(128)S(1)}, f32[3]{0:T(128)}, u32[]{:S(2)}) copy-start(f32[3]{0:T(128)} %gain_ref.1) | copy-start | bytes 40
  0.7 18.8 %copy-start.7 = (s32[256,3,4]{0,2,1:T(4,128)S(1)}, s32[256,3,4]{0,2,1:T(4,128)}, u32[]{:S(2)}) copy-start(s32[256,3,4]{0,2,1:T(4,128)} %param.12) | copy-start | bytes 36868
  2.1 17.4 %collective-permute-start.1 = (bf16[3,256,256]{2,1,0:T(8,128)(2,1)S(1)}, bf16[3,256,256]{2,1,0:T(8,128)(2,1)S(1)}, u32[]{:S(2)}, u32[]{:S(2)}) collective-permute-start(bf16[3,256,256]{2,1,0:T(8,128)(2,1)S(1)} %get-tuple-element.16), channel_id=1, source_target_pairs={{0,1},{1,0},{2,3},{3,2},{4,5},{5,4},{6,7},{7,6},{8,9},{9,8},{10,11... | collective-permute-start | bytes 1179656 | tf_op jit(solution)/shard_map/ppermute | solution.py:20
  3.5 20.4 %collective-permute-start = (bf16[3,256,256]{2,1,0:T(8,128)(2,1)S(1)}, bf16[3,256,256]{2,1,0:T(8,128)(2,1)S(1)}, u32[]{:S(2)}, u32[]{:S(2)}) collective-permute-start(bf16[3,256,256]{2,1,0:T(8,128)(2,1)S(1)} %get-tuple-element.15), channel_id=1, source_target_pairs={{0,127},{1,2},{2,1},{3,4},{4,3},{5,6},{6,5},{7,8},{8,7},{9,10},{10... | collective-permute-start | bytes 1179656 | tf_op jit(solution)/shard_map/ppermute | solution.py:20
  4.8 1.2 %copy-start.3 = (bf16[28,4,16,2,128]{4,3,2,1,0:T(2,128)(2,1)S(1)}, bf16[28,4,16,2,128]{4,3,2,1,0:T(2,128)(2,1)}, u32[]{:S(2)}) copy-start(bf16[28,4,16,2,128]{4,3,2,1,0:T(2,128)(2,1)} %param.14) | copy-start | bytes 2752516
  8.3 20.1 %all-to-all-start = ((f32[32,16,128]{2,1,0:T(8,128)}), f32[32,16,128]{2,1,0:T(8,128)S(1)}, u32[]{:S(2)}, u32[]{:S(2)}) async-start(f32[32,16,128]{2,1,0:T(8,128)} %get-tuple-element.19), calls=%async_computation | async-start | bytes 524288 | tf_op jit(solution)/shard_map/all_to_all | solution.py:369
  19.5 1.4 %copy-start.1 = (bf16[3,4,256,256]{3,2,1,0:T(8,128)(2,1)S(1)}, bf16[3,4,256,256]{3,2,1,0:T(8,128)(2,1)}, u32[]{:S(2)}) copy-start(bf16[3,4,256,256]{3,2,1,0:T(8,128)(2,1)} %refs_4_.1) | copy-start | bytes 4718596
  20.9 3.0 %copy-start.2 = (bf16[3,4,256,256]{3,2,1,0:T(8,128)(2,1)S(1)}, bf16[3,4,256,256]{3,2,1,0:T(8,128)(2,1)}, u32[]{:S(2)}) copy-start(bf16[3,4,256,256]{3,2,1,0:T(8,128)(2,1)} %refs_4_.1) | copy-start | bytes 4718596
  20.9 3.1 %copy-start.5 = (bf16[512,512]{1,0:T(8,128)(2,1)S(1)}, bf16[512,512]{1,0:T(8,128)(2,1)}, u32[]{:S(2)}) copy-start(bf16[512,512]{1,0:T(8,128)(2,1)} %constant.38.clone.refs_7_) | copy-start | bytes 1572868
  20.9 3.1 %copy-start.6 = (f32[256,256]{1,0:T(8,128)S(1)}, f32[256,256]{1,0:T(8,128)}, u32[]{:S(2)}) copy-start(f32[256,256]{1,0:T(8,128)} %refs_6_.1) | copy-start | bytes 786436
  23.9 17.7 %copy-start.4 = (bf16[28,4,16,2,128]{4,3,2,1,0:T(2,128)(2,1)S(1)}, bf16[28,4,16,2,128]{4,3,2,1,0:T(2,128)(2,1)}, u32[]{:S(2)}) copy-start(bf16[28,4,16,2,128]{4,3,2,1,0:T(2,128)(2,1)} %param.14) | copy-start | bytes 2752516

commit v5 on v4

--- a/solution.py
+++ b/solution.py
@@ -72,11 +72,12 @@
     return jnp.concatenate(parts, 1)
 
 
-def edges(odd_ref, screens_ref, outer_ref, inner_ref, sems):
+def edges(screens_ref, matrix_ref, outer_ref, inner_ref, cm_ref, sems):
     layers, blocks, _ = screens_ref.shape
     last = (blocks // EDGE - 1) * EDGE
-    outer = pl.multiple_of(odd_ref[0] * last, EDGE)
-    inner = pl.multiple_of((1 - odd_ref[0]) * last, EDGE)
+    odd = lax.axis_index("tile") % 2
+    outer = pl.multiple_of(odd * last, EDGE)
+    inner = pl.multiple_of((1 - odd) * last, EDGE)
     copies = []
     for layer in range(layers):
         for first, ref, sem in ((outer, outer_ref, 0), (inner, inner_ref, 1)):
@@ -84,6 +85,7 @@
             copies.append(
                 pltpu.make_async_copy(block, ref.at[layer], sems.at[2 * layer + sem])
             )
+    copies.append(pltpu.make_async_copy(matrix_ref, cm_ref, sems.at[2 * layers]))
     for copy in copies:
         copy.start()
     for copy in copies:
@@ -91,14 +93,14 @@
 
 
 def mirror_rows(
-    base_ref, gain_ref, cols_ref, owner_ref, prev_ref, cm_ref, sent_ref, spot_ref, state_ref
+    gain_ref, cols_ref, owner_ref, prev_ref, cm_ref, sent_ref, spot_ref, state_ref, *, columns
 ):
     tiles, rows_sent, _ = sent_ref.shape
     mirrors = gain_ref.shape[0]
     positions, rowblk = cols_ref.shape
     acts = owner_ref.shape[1]
     rb = acts // rowblk
-    cols = (cols_ref[...] - base_ref[0]).astype(jnp.float32)
+    cols = (cols_ref[...] - lax.axis_index("grp") * columns).astype(jnp.float32)
     lane = lax.broadcasted_iota(jnp.int32, (positions, LANES), 1)
     place = lax.broadcasted_iota(jnp.int32, (positions, LANES), 0)
     spread = jnp.where(lane // (2 * rb) == place, 1.0, 0.0)
@@ -129,9 +131,6 @@
         )
         for i in range(rowblk)
     ]
-    sums = jnp.dot(
-        jnp.concatenate(picks, 1), cm_ref[...], preferred_element_type=jnp.float32
-    )
     lane = lax.broadcasted_iota(jnp.int32, (1, LANES), 1)
     extra = jnp.zeros((1, LANES), jnp.float32)
     gain = jnp.zeros(owner.shape, jnp.float32)
@@ -141,12 +140,6 @@
         prev = jnp.sum(jnp.where(mine, prev_ref[...], 0.0), axis=1, keepdims=True)
         number = jnp.sum(jnp.where(mine, 1.0, 0.0), axis=1, keepdims=True)
         extra = jnp.where(lane == m, prev, jnp.where(lane == mirrors + m, number, extra))
-    for t in range(tiles):
-        sent_ref[t, 0:used, :] = sums[t * used : (t + 1) * used]
-    sent_ref[:, used : used + 1, :] = jnp.broadcast_to(extra[None], (tiles, 1, LANES))
-    left = rows_sent - used - 1
-    sent_ref[:, used + 1 :, :] = jnp.zeros((tiles, left, LANES), jnp.float32)
-
     lines = height * rb // LANES
     missing = lines * LANES - acts
     rows = []
@@ -155,55 +148,59 @@
         rows += [values[:, i * LANES : (i + 1) * LANES] for i in range(lines)]
     state_ref[...] = jnp.concatenate(rows, 0)
 
-
-def sense_own(
-    start_ref, first_ref, foot_ref, screens_ref, inner_ref, weights_ref, phase_ref, *, total
-):
+    sums = jnp.dot(
+        jnp.concatenate(picks, 1), cm_ref[...], preferred_element_type=jnp.float32
+    )
+    for t in range(tiles):
+        sent_ref[t, 0:used, :] = sums[t * used : (t + 1) * used]
+    sent_ref[:, used : used + 1, :] = jnp.broadcast_to(extra[None], (tiles, 1, LANES))
+    left = rows_sent - used - 1
+    sent_ref[:, used + 1 :, :] = jnp.zeros((tiles, left, LANES), jnp.float32)
+
+
+def pick_own(foot_ref, screens_ref, inner_ref, picked_ref, *, total):
     layers, foot, _ = foot_ref.shape
     blocks, pixels = screens_ref.shape[1:]
-    phase = None
+    start = lax.axis_index(DEVICES) * blocks
+    first = (1 - lax.axis_index("tile") % 2) * (blocks + EDGE) - EDGE
     for layer in range(layers):
-        offsets = offsets_of(foot_ref[layer], start_ref[0], total)
-        picked = []
+        offsets = offsets_of(foot_ref[layer], start, total)
         for k in range(foot):
             column = offsets[:, k : k + 1]
             rows = jnp.dot(
                 hits(column, 0, blocks), screens_ref[layer], preferred_element_type=jnp.float32
             )
             rows = rows + jnp.dot(
-                hits(column - first_ref[0], 0, EDGE),
+                hits(column - first, 0, EDGE),
                 inner_ref[layer],
                 preferred_element_type=jnp.float32,
             )
-            picked.append(rows.astype(jnp.bfloat16))
+            picked_ref[layer, :, k * pixels : (k + 1) * pixels] = rows.astype(jnp.bfloat16)
+
+
+def sense_rest(
+    foot_ref, outer_ref, weights_ref, own_ref, illum_ref, table_ref, slopes_ref, words_ref, *,
+    total, blocks
+):
+    layers, foot, subs = foot_ref.shape
+    pixels = illum_ref.shape[1]
+    start = lax.axis_index(DEVICES) * blocks
+    first = (lax.axis_index("tile") % 2) * (blocks + EDGE) - EDGE
+    phase = None
+    for layer in range(layers):
+        offsets = offsets_of(foot_ref[layer], start, total)
+        picked = []
+        for k in range(foot):
+            found = hits(offsets[:, k : k + 1] - first, 0, EDGE)
+            rows = jnp.dot(found, outer_ref[layer], preferred_element_type=jnp.float32)
+            own = own_ref[layer, :, k * pixels : (k + 1) * pixels]
+            picked.append(rows.astype(jnp.bfloat16) + own)
         part = jnp.dot(
             jnp.concatenate(picked, 1),
             weights_ref[layer].reshape(foot * pixels, pixels),
             preferred_element_type=jnp.float32,
         )
         phase = part if phase is None else phase + part
-    phase_ref[...] = phase
-
-
-def sense_rest(
-    start_ref, first_ref, foot_ref, outer_ref, weights_ref, phase_ref, illum_ref, table_ref,
-    slopes_ref, words_ref, *, total
-):
-    layers, foot, subs = foot_ref.shape
-    pixels = phase_ref.shape[1]
-    phase = phase_ref[...]
-    for layer in range(layers):
-        offsets = offsets_of(foot_ref[layer], start_ref[0], total)
-        picked = []
-        for k in range(foot):
-            found = hits(offsets[:, k : k + 1] - first_ref[0], 0, EDGE)
-            rows = jnp.dot(found, outer_ref[layer], preferred_element_type=jnp.float32)
-            picked.append(rows.astype(jnp.bfloat16))
-        phase = phase + jnp.dot(
-            jnp.concatenate(picked, 1),
-            weights_ref[layer].reshape(foot * pixels, pixels),
-            preferred_element_type=jnp.float32,
-        )
     phase = phase.T
     illum = illum_ref[...].T
     sine, cosine = sine_cosine(phase)
@@ -333,26 +330,26 @@
     f32 = jnp.float32
 
     edge = jax.ShapeDtypeStruct((layers, EDGE, pixels), screens.dtype)
-    odd = (lax.axis_index("tile") % 2).astype(jnp.int32).reshape(1)
-    outer, inner = pl.pallas_call(
+    hbm = pl.BlockSpec(memory_space=pltpu.HBM)
+    cm = cm_values.reshape(rowblk * positions * rb * comps, cbs)
+    outer, inner, loaded = pl.pallas_call(
         edges,
-        in_specs=[smem, pl.BlockSpec(memory_space=pltpu.HBM)],
-        out_specs=[vmem, vmem],
-        out_shape=[edge, edge],
-        scratch_shapes=[pltpu.SemaphoreType.DMA((2 * layers,))],
+        in_specs=[hbm] * 2,
+        out_specs=[vmem] * 3,
+        out_shape=[edge, edge, jax.ShapeDtypeStruct(cm.shape, cm.dtype)],
+        scratch_shapes=[pltpu.SemaphoreType.DMA((2 * layers + 1,))],
         compiler_params=limit,
         name="edges",
-    )(odd, pltpu.with_memory_space_constraint(screens, pltpu.HBM))
+    )(
+        pltpu.with_memory_space_constraint(screens, pltpu.HBM),
+        pltpu.with_memory_space_constraint(cm, pltpu.HBM),
+    )
     outer = swap(outer, 1)
     inner = swap(inner, -1)
-    outer_first = odd * (blk_dev + EDGE) - EDGE
-    inner_first = (1 - odd) * (blk_dev + EDGE) - EDGE
-
-    base = (lax.axis_index("grp") * (tiles * subs // cbs)).astype(jnp.int32).reshape(1)
-    cm = cm_values.reshape(rowblk * positions * rb * comps, cbs)
+
     rows, spot, state = pl.pallas_call(
-        mirror_rows,
-        in_specs=[smem] * 2 + [vmem] * 4,
+        lambda *refs: mirror_rows(*refs, columns=tiles * subs // cbs),
+        in_specs=[smem] + [vmem] * 4,
         out_shape=(
             jax.ShapeDtypeStruct((tiles, 16, LANES), f32),
             jax.ShapeDtypeStruct((height, LANES), jnp.int32),
@@ -361,23 +358,22 @@
         compiler_params=limit,
         name="mirror_rows",
     )(
-        base, dm_gain, cm_columns.T, owner_map.reshape(1, acts), prev_commands.reshape(1, acts), cm
-    )
-    start = (lax.axis_index(DEVICES) * blk_dev).astype(jnp.int32).reshape(1)
+        dm_gain, cm_columns.T, owner_map.reshape(1, acts), prev_commands.reshape(1, acts), loaded
+    )
     foot_rows = jnp.transpose(footprint, (1, 2, 0))
     rows, foot_rows = lax.optimization_barrier((rows, foot_rows))
     rows = lax.all_to_all(rows, "tile", 0, 0)
 
-    phase = pl.pallas_call(
-        lambda *refs: sense_own(*refs, total=total),
-        in_specs=[smem] * 2 + [vmem] * 4,
-        out_shape=jax.ShapeDtypeStruct((subs, pixels), f32),
-        compiler_params=limit,
-        name="sense_own",
-    )(start, inner_first, foot_rows, screens, inner, interp_weights)
+    picked = pl.pallas_call(
+        lambda *refs: pick_own(*refs, total=total),
+        in_specs=[vmem] * 3,
+        out_shape=jax.ShapeDtypeStruct((layers, subs, foot * pixels), screens.dtype),
+        compiler_params=limit,
+        name="pick_own",
+    )(foot_rows, screens, inner)
     slopes, words = pl.pallas_call(
-        lambda *refs: sense_rest(*refs, total=total),
-        in_specs=[smem] * 2 + [vmem] * 6,
+        lambda *refs: sense_rest(*refs, total=total, blocks=blk_dev),
+        in_specs=[vmem] * 6,
         out_shape=(
             jax.ShapeDtypeStruct((2, subs), f32),
             jax.ShapeDtypeStruct((2 * subs // LANES, LANES), f32),
@@ -385,8 +381,7 @@
         compiler_params=limit,
         name="sense_rest",
     )(
-        start, outer_first, foot_rows, outer, interp_weights, phase, illumination,
-        transform_table(SIDE),
+        foot_rows, outer, interp_weights, picked, illumination, transform_table(SIDE)
     )
     packed, extra = pl.pallas_call(
         lambda *refs: pack(*refs, mirrors=mirrors),

time: 50.3 us -> 47.6 us (0.946)
  local copies, waits for them, and re-layouts: 2.62 us -> 0.05 us
  waiting for transfers between devices: 1.58 us -> 3.4 us
  blocking collectives: 19.6 us -> 17.8 us
    unnamed x24 -> x20, local copies, waits for them, and re-layouts: 2.62 us -> 0.05 us
    all_to_all x1, blocking collectives: 13 us -> 11.2 us  [on_device(): gathered = lax.all_to_all(packed, 'tile', 0, 0)]
    all_to_all x1, waiting for transfers between devices: 1.58 us -> 3.39 us  [on_device(): rows = lax.all_to_all(rows, 'tile', 0, 0)]
where the time goes in v5:
time: 47.6 us; the launch traced here: 47.2 us
  blocking collectives  17.8 us (37%)
  starting transfers between devices  13.9 us (29%)
  Pallas kernels  11.3 us (24%)
  waiting for transfers between devices  3.4 us (7%)
  between operations  0.81 us (2%)
    all_to_all x1, blocking collectives, on_device(): gathered = lax.all_to_all(packed, 'tile', 0, 0)  11.2 us
    all_to_all x1, starting transfers between devices, on_device(): rows = lax.all_to_all(rows, 'tile', 0, 0)  11.1 us
    all_to_all x1, blocking collectives, on_device(): got = lax.all_to_all(sent, 'grp', 0, 0)  6.56 us
    all_to_all x1, waiting for transfers between devices, on_device(): rows = lax.all_to_all(rows, 'tile', 0, 0)  3.39 us
    pallas_call x1, Pallas kernels, on_device(): pl.pallas_call(lambda *refs: sense_rest(*refs, total=total, blocks=blk_de...  2.92 us
    ppermute x2, starting transfers between devices, swap(): return lax.ppermute(block, DEVICES, route)  2.76 us
    pallas_call x1, Pallas kernels, on_device(): pl.pallas_call(lambda *refs: pick_own(*refs, total=total), in_specs=[vmem...  2.55 us
    pallas_call x1, Pallas kernels, on_device(): pl.pallas_call(lambda *refs: mirror_rows(*refs, columns=tiles * subs // c...  2.31 us
  transfers between devices with their start and end apart: 3, of which 1 were waited for; matrix products, arithmetic and copies ran while one was open for 0% of the time, Pallas kernels for 16%

profile of v5, /device:TPU:1, one launch (start us, length us, event | category | flops | bytes accessed | tf_op | source)
XLA Modules:
  0.0 47.2 jit_solution(12534952247896911118)
XLA Ops:
  0.6 0.0 copy-start.9
  0.6 0.0 copy-start.7
  0.7 0.0 copy-start.8
  0.7 0.0 copy-start.6
  0.7 0.0 copy-start
  0.7 1.7 %edges.1 = (bf16[3,256,256]{2,1,0:T(8,128)(2,1)S(1)}, bf16[3,256,256]{2,1,0:T(8,128)(2,1)S(1)}, bf16[3584,128]{1,0:T(8,128)(2,1)S(1)}) custom-call(bf16[3,1024,256]{2,1,0:T(8,128)(2,1)} %refs_1_.1, bf16[3584,128]{1,0:T(8,128)(2,1)} %bitcast.5), custom_call_target="tpu_custom_call" | custom-call | tf_op jit(solution)/shard_map/edges/pallas_call | solution.py:335
  2.4 1.5 %collective-permute-start.1 = (bf16[3,256,256]{2,1,0:T(8,128)(2,1)S(1)}, bf16[3,256,256]{2,1,0:T(8,128)(2,1)S(1)}, u32[]{:S(2)}, u32[]{:S(2)}) collective-permute-start(bf16[3,256,256]{2,1,0:T(8,128)(2,1)S(1)} %get-tuple-element.18), channel_id=1, source_target_pairs={{0,1},{1,0},{2,3},{3,2},{4,5},{5,4},{6,7},{7,6},{8,9},{9,8},{10,11... | collective-permute-start | bytes 1179656 | tf_op jit(solution)/shard_map/ppermute | solution.py:20
  3.9 1.3 %collective-permute-start = (bf16[3,256,256]{2,1,0:T(8,128)(2,1)S(1)}, bf16[3,256,256]{2,1,0:T(8,128)(2,1)S(1)}, u32[]{:S(2)}, u32[]{:S(2)}) collective-permute-start(bf16[3,256,256]{2,1,0:T(8,128)(2,1)S(1)} %get-tuple-element.17), channel_id=1, source_target_pairs={{0,127},{1,2},{2,1},{3,4},{4,3},{5,6},{6,5},{7,8},{8,7},{9,10},{10... | collective-permute-start | bytes 1179656 | tf_op jit(solution)/shard_map/ppermute | solution.py:20
  5.2 2.3 %mirror_rows.1 = (f32[32,16,128]{2,1,0:T(8,128)}, s32[32,128]{1,0:T(8,128)S(1)}, f32[12,128]{1,0:T(8,128)S(1)}) custom-call(f32[3]{0:T(128)S(1)} %copy-done.9, s32[4,28]{1,0:T(4,128)S(1)} %bitcast.9, s32[1,448]{1,0:T(1,128)S(1)} %bitcast.10, f32[1,448]{1,0:T(1,128)S(1)} %bitcast.11, bf16[3584,128]{1,0:T(8,128)(2,1)S(1)} %get-tuple-element.14.refs_4_), custom_call_target="tpu_custom_call" | custom-call | tf_op jit(solution)/shard_map/mirror_rows/pallas_call | solution.py:350
  7.5 11.1 %all-to-all-start = ((f32[32,16,128]{2,1,0:T(8,128)}), f32[32,16,128]{2,1,0:T(8,128)S(1)}, u32[]{:S(2)}, u32[]{:S(2)}) async-start(f32[32,16,128]{2,1,0:T(8,128)} %get-tuple-element.21), calls=%async_computation | async-start | bytes 524288 | tf_op jit(solution)/shard_map/all_to_all | solution.py:365
  18.6 0.0 copy-start.2
  18.6 0.0 copy-start.3
  18.6 0.0 copy-start.4
  18.7 0.0 collective-permute-done.1.refs_2_
  18.7 2.5 %pick_own.1.refs_3_ = bf16[3,256,1024]{2,1,0:T(8,128)(2,1)S(1)} custom-call(s32[3,4,256]{2,1,0:T(4,128)S(1)} %bitcast.7, bf16[3,1024,256]{2,1,0:T(8,128)(2,1)S(1)} %copy-done, bf16[3,256,256]{2,1,0:T(8,128)(2,1)S(1)} %collective-permute-done.1.refs_2_), custom_call_target="tpu_custom_call" | custom-call | tf_op jit(solution)/shard_map/pick_own/pallas_call | solution.py:367
  21.2 0.0 copy-start.1
  21.3 0.0 collective-permute-done.refs_1_
  21.3 2.9 %sense_rest.1 = (f32[2,256]{1,0:T(2,128)}, f32[4,128]{1,0:T(4,128)S(1)}) custom-call(s32[3,4,256]{2,1,0:T(4,128)S(1)} %bitcast.8, bf16[3,256,256]{2,1,0:T(8,128)(2,1)S(1)} %collective-permute-done.refs_1_, bf16[3,4,256,256]{3,2,1,0:T(8,128)(2,1)S(1)} %copy-done.2, bf16[3,256,1024]{2,1,0:T(8,128)(2,1)S(1)} %pick_own.1.refs_3_, f32[256,256]{1,0:T(8,128)S(1)} %copy-done.4, ...), custom_call_target="tpu_custom_call" | custom-call | tf_op jit(solution)/shard_map/sense_rest/pallas_call | solution.py:374
  24.2 3.4 %all-to-all-done.refs_1_ = f32[32,16,128]{2,1,0:T(8,128)S(1)} async-done(((f32[32,16,128]{2,1,0:T(8,128)}), f32[32,16,128]{2,1,0:T(8,128)S(1)}, u32[]{:S(2)}, u32[]{:S(2)}) %all-to-all-start) | async-done | bytes 262176 | tf_op jit(solution)/shard_map/all_to_all | solution.py:365
  27.6 0.1 pack.1
  27.7 11.2 %all_to_all.15.refs_0_ = bf16[32,8,128]{2,1,0:T(8,128)(2,1)S(1)} all-to-all(bf16[32,8,128]{2,1,0:T(8,128)(2,1)S(1)} %get-tuple-element.22), channel_id=1, replica_groups=mesh['grp'=4,'tile'=32] {'tile'}, dimensions={0} | all-to-all | bytes 131072 | tf_op jit(solution)/shard_map/all_to_all | solution.py:397
  39.0 1.0 %reconstruct.1 = f32[4,8,128]{2,1,0:T(8,128)S(1)} custom-call(bf16[32,8,128]{2,1,0:T(8,128)(2,1)S(1)} %all_to_all.15.refs_0_, bf16[3584,128]{1,0:T(8,128)(2,1)S(1)} %bitcast.6, s32[32,128]{1,0:T(8,128)S(1)} %get-tuple-element.23.refs_2_), custom_call_target="tpu_custom_call" | custom-call | tf_op jit(solution)/shard_map/reconstruct/pallas_call | solution.py:398
  39.9 6.6 %all_to_all.16.refs_0_ = f32[4,8,128]{2,1,0:T(8,128)S(1)} all-to-all(f32[4,8,128]{2,1,0:T(8,128)S(1)} %reconstruct.1), channel_id=1, replica_groups=mesh['grp'=4,'tile'=32] {'grp'}, dimensions={0} | all-to-all | bytes 32768 | tf_op jit(solution)/shard_map/all_to_all | solution.py:405
  46.5 0.7 %settle.1 = f32[448]{0:T(512)} custom-call(f32[4,8,128]{2,1,0:T(8,128)S(1)} %all_to_all.16.refs_0_, f32[1,128]{1,0:T(1,128)S(1)} %get-tuple-element.24.refs_1_, f32[12,128]{1,0:T(8,128)S(1)} %get-tuple-element.25.refs_2_), custom_call_target="tpu_custom_call" | custom-call | tf_op jit(solution)/shard_map/settle/pallas_call | solution.py:406
  (11 shorter events, 0.0 us)
Async XLA Ops:
  0.6 4.5 %copy-start.9 = (f32[3]{0:T(128)S(1)}, f32[3]{0:T(128)}, u32[]{:S(2)}) copy-start(f32[3]{0:T(128)} %refs_0_.1) | copy-start | bytes 40
  0.6 4.5 %copy-start.7 = (s32[448]{0:T(512)S(1)}, s32[448]{0:T(512)}, u32[]{:S(2)}) copy-start(s32[448]{0:T(512)} %param.17) | copy-start | bytes 5380
  0.7 4.5 %copy-start.8 = (f32[448]{0:T(512)S(1)}, f32[448]{0:T(512)}, u32[]{:S(2)}) copy-start(f32[448]{0:T(512)} %param.16) | copy-start | bytes 5380
  0.7 4.5 %copy-start.6 = (s32[28,4]{0,1:T(4,128)S(1)}, s32[28,4]{0,1:T(4,128)}, u32[]{:S(2)}) copy-start(s32[28,4]{0,1:T(4,128)} %param.15) | copy-start | bytes 1348
  0.7 18.0 %copy-start = (bf16[3,1024,256]{2,1,0:T(8,128)(2,1)S(1)}, bf16[3,1024,256]{2,1,0:T(8,128)(2,1)}, u32[]{:S(2)}) copy-start(bf16[3,1024,256]{2,1,0:T(8,128)(2,1)} %refs_1_.1) | copy-start | bytes 4718596
  0.7 18.0 %copy-start.5 = (s32[256,3,4]{0,2,1:T(4,128)S(1)}, s32[256,3,4]{0,2,1:T(4,128)}, u32[]{:S(2)}) copy-start(s32[256,3,4]{0,2,1:T(4,128)} %param.12) | copy-start | bytes 36868
  2.4 16.3 %collective-permute-start.1 = (bf16[3,256,256]{2,1,0:T(8,128)(2,1)S(1)}, bf16[3,256,256]{2,1,0:T(8,128)(2,1)S(1)}, u32[]{:S(2)}, u32[]{:S(2)}) collective-permute-start(bf16[3,256,256]{2,1,0:T(8,128)(2,1)S(1)} %get-tuple-element.18), channel_id=1, source_target_pairs={{0,1},{1,0},{2,3},{3,2},{4,5},{5,4},{6,7},{7,6},{8,9},{9,8},{10,11... | collective-permute-start | bytes 1179656 | tf_op jit(solution)/shard_map/ppermute | solution.py:20
  3.9 17.4 %collective-permute-start = (bf16[3,256,256]{2,1,0:T(8,128)(2,1)S(1)}, bf16[3,256,256]{2,1,0:T(8,128)(2,1)S(1)}, u32[]{:S(2)}, u32[]{:S(2)}) collective-permute-start(bf16[3,256,256]{2,1,0:T(8,128)(2,1)S(1)} %get-tuple-element.17), channel_id=1, source_target_pairs={{0,127},{1,2},{2,1},{3,4},{4,3},{5,6},{6,5},{7,8},{8,7},{9,10},{10... | collective-permute-start | bytes 1179656 | tf_op jit(solution)/shard_map/ppermute | solution.py:20
  7.5 20.1 %all-to-all-start = ((f32[32,16,128]{2,1,0:T(8,128)}), f32[32,16,128]{2,1,0:T(8,128)S(1)}, u32[]{:S(2)}, u32[]{:S(2)}) async-start(f32[32,16,128]{2,1,0:T(8,128)} %get-tuple-element.21), calls=%async_computation | async-start | bytes 524288 | tf_op jit(solution)/shard_map/all_to_all | solution.py:365
  18.6 2.6 %copy-start.2 = (bf16[3,4,256,256]{3,2,1,0:T(8,128)(2,1)S(1)}, bf16[3,4,256,256]{3,2,1,0:T(8,128)(2,1)}, u32[]{:S(2)}) copy-start(bf16[3,4,256,256]{3,2,1,0:T(8,128)(2,1)} %refs_2_.1) | copy-start | bytes 4718596
  18.6 2.6 %copy-start.3 = (bf16[512,512]{1,0:T(8,128)(2,1)S(1)}, bf16[512,512]{1,0:T(8,128)(2,1)}, u32[]{:S(2)}) copy-start(bf16[512,512]{1,0:T(8,128)(2,1)} %constant.2.clone.refs_5_) | copy-start | bytes 1572868
  18.6 2.6 %copy-start.4 = (f32[256,256]{1,0:T(8,128)S(1)}, f32[256,256]{1,0:T(8,128)}, u32[]{:S(2)}) copy-start(f32[256,256]{1,0:T(8,128)} %refs_4_.1) | copy-start | bytes 786436
  21.2 17.7 %copy-start.1 = (bf16[28,4,16,2,128]{4,3,2,1,0:T(2,128)(2,1)S(1)}, bf16[28,4,16,2,128]{4,3,2,1,0:T(2,128)(2,1)}, u32[]{:S(2)}) copy-start(bf16[28,4,16,2,128]{4,3,2,1,0:T(2,128)(2,1)} %param.14) | copy-start | bytes 2752516

commit v6 on v5

--- a/solution.py
+++ b/solution.py
@@ -7,6 +7,7 @@
 from jax.experimental import pallas as pl
 from jax.experimental.pallas import tpu as pltpu
 from jax.sharding import PartitionSpec as P
+
 
 SIDE = 16
 DEVICES = ("grp", "tile")
@@ -72,34 +73,35 @@
     return jnp.concatenate(parts, 1)
 
 
-def edges(screens_ref, matrix_ref, outer_ref, inner_ref, cm_ref, sems):
+def edges(
+    screens_ref, matrix_ref, cols_hbm, owner_hbm, outer_ref, inner_ref, cm_ref, picks_ref, spot_ref,
+    cols_ref, owner_ref, sems, *, columns, mirrors
+):
     layers, blocks, _ = screens_ref.shape
     last = (blocks // EDGE - 1) * EDGE
     odd = lax.axis_index("tile") % 2
     outer = pl.multiple_of(odd * last, EDGE)
     inner = pl.multiple_of((1 - odd) * last, EDGE)
     copies = []
-    for layer in range(layers):
-        for first, ref, sem in ((outer, outer_ref, 0), (inner, inner_ref, 1)):
+    for first, ref in ((outer, outer_ref), (inner, inner_ref)):
+        for layer in range(layers):
             block = screens_ref.at[layer, pl.ds(first, EDGE)]
-            copies.append(
-                pltpu.make_async_copy(block, ref.at[layer], sems.at[2 * layer + sem])
-            )
-    copies.append(pltpu.make_async_copy(matrix_ref, cm_ref, sems.at[2 * layers]))
-    for copy in copies:
+            copies.append(pltpu.make_async_copy(block, ref.at[layer], sems.at[len(copies)]))
+    copies.append(pltpu.make_async_copy(matrix_ref, cm_ref, sems.at[len(copies)]))
+    small = [
+        pltpu.make_async_copy(cols_hbm, cols_ref, sems.at[len(copies)]),
+        pltpu.make_async_copy(owner_hbm, owner_ref, sems.at[len(copies) + 1]),
+    ]
+    for copy in small + copies:
         copy.start()
-    for copy in copies:
-        copy.wait()
-
-
-def mirror_rows(
-    gain_ref, cols_ref, owner_ref, prev_ref, cm_ref, sent_ref, spot_ref, state_ref, *, columns
-):
-    tiles, rows_sent, _ = sent_ref.shape
-    mirrors = gain_ref.shape[0]
     positions, rowblk = cols_ref.shape
     acts = owner_ref.shape[1]
     rb = acts // rowblk
+    act = lax.broadcasted_iota(jnp.int32, (acts, LANES), 0)
+    wide = lax.broadcasted_iota(jnp.int32, (acts, LANES), 1)
+    over = jnp.where(act % rb == (wide % (2 * rb)) // 2, 1.0, 0.0).astype(jnp.bfloat16)
+    for copy in small:
+        copy.wait()
     cols = (cols_ref[...] - lax.axis_index("grp") * columns).astype(jnp.float32)
     lane = lax.broadcasted_iota(jnp.int32, (positions, LANES), 1)
     place = lax.broadcasted_iota(jnp.int32, (positions, LANES), 0)
@@ -112,25 +114,46 @@
     spot_ref[...] = jnp.concatenate(
         [cols * 2 + comp, jnp.full((height - rowblk, LANES), -1, jnp.int32)], 0
     )
-    owner = owner_ref[...]
     act = lax.broadcasted_iota(jnp.int32, (rowblk, acts), 1)
     block = lax.broadcasted_iota(jnp.int32, (rowblk, acts), 0)
-    held = jnp.where(act // rb == block, owner, 0).astype(jnp.float32).astype(jnp.bfloat16)
-    act = lax.broadcasted_iota(jnp.int32, (acts, LANES), 0)
-    wide = lax.broadcasted_iota(jnp.int32, (acts, LANES), 1)
-    spread = jnp.where(act % rb == (wide % (2 * rb)) // 2, 1.0, 0.0).astype(jnp.bfloat16)
-    owners = jnp.dot(held, spread, preferred_element_type=jnp.float32)
+    held = jnp.where(act // rb == block, owner_ref[...], 0)
+    held = held.astype(jnp.float32).astype(jnp.bfloat16)
+    owners = jnp.dot(held, over, preferred_element_type=jnp.float32)
     target = cols * (2 * mirrors) + comp * mirrors + owners.astype(jnp.int32)
-
-    used = 4 * mirrors
-    row = lax.broadcasted_iota(jnp.int16, (tiles * used, LANES), 0)
+    row = lax.broadcasted_iota(jnp.int16, (picks_ref.shape[0], LANES), 0)
     one, zero = jnp.bfloat16(1), jnp.bfloat16(0)
-    picks = [
-        jnp.where(
-            row == jnp.broadcast_to(target[i : i + 1, :], row.shape).astype(jnp.int16), one, zero
+    for i in range(rowblk):
+        named = jnp.broadcast_to(target[i : i + 1, :], row.shape).astype(jnp.int16)
+        picks_ref[:, i * LANES : (i + 1) * LANES] = jnp.where(row == named, one, zero)
+    for copy in copies:
+        copy.wait()
+
+
+def mirror_rows(
+    gain_ref, owner_ref, prev_ref, picks_ref, cm_ref, sent_ref, state_ref, extra_ref, half_ref, sems
+):
+    tiles, threes, fours, _ = sent_ref.shape
+    mirrors = gain_ref.shape[0]
+    acts = owner_ref.shape[1]
+    half = tiles // 2
+    rows = half * threes * fours
+    copies = []
+    for part in range(2):
+        sums = jnp.dot(
+            picks_ref[part * rows : (part + 1) * rows, :],
+            cm_ref[...],
+            preferred_element_type=jnp.float32,
         )
-        for i in range(rowblk)
-    ]
+        for t in range(half):
+            for j in range(threes):
+                at = (t * threes + j) * fours
+                half_ref[part * half + t, j] = sums[at : at + fours]
+        span = pl.ds(part * half, half)
+        copies.append(
+            pltpu.make_async_copy(half_ref.at[span], sent_ref.at[span], sems.at[part])
+        )
+        copies[part].start()
+    owner = owner_ref[...]
     lane = lax.broadcasted_iota(jnp.int32, (1, LANES), 1)
     extra = jnp.zeros((1, LANES), jnp.float32)
     gain = jnp.zeros(owner.shape, jnp.float32)
@@ -139,23 +162,18 @@
         gain = jnp.where(mine, gain_ref[m], gain)
         prev = jnp.sum(jnp.where(mine, prev_ref[...], 0.0), axis=1, keepdims=True)
         number = jnp.sum(jnp.where(mine, 1.0, 0.0), axis=1, keepdims=True)
-        extra = jnp.where(lane == m, prev, jnp.where(lane == mirrors + m, number, extra))
-    lines = height * rb // LANES
+        extra = jnp.where(lane == mirrors + m, prev, extra)
+        extra = jnp.where(lane == 2 * mirrors + m, number, extra)
+    extra_ref[...] = extra
+    lines = state_ref.shape[0] // 3
     missing = lines * LANES - acts
     rows = []
     for values, fill in ((owner.astype(jnp.float32), -1.0), (prev_ref[...], 0.0), (gain, 0.0)):
         values = jnp.concatenate([values, jnp.full((1, missing), fill, jnp.float32)], 1)
         rows += [values[:, i * LANES : (i + 1) * LANES] for i in range(lines)]
     state_ref[...] = jnp.concatenate(rows, 0)
-
-    sums = jnp.dot(
-        jnp.concatenate(picks, 1), cm_ref[...], preferred_element_type=jnp.float32
-    )
-    for t in range(tiles):
-        sent_ref[t, 0:used, :] = sums[t * used : (t + 1) * used]
-    sent_ref[:, used : used + 1, :] = jnp.broadcast_to(extra[None], (tiles, 1, LANES))
-    left = rows_sent - used - 1
-    sent_ref[:, used + 1 :, :] = jnp.zeros((tiles, left, LANES), jnp.float32)
+    for copy in copies:
+        copy.wait()
 
 
 def pick_own(foot_ref, screens_ref, inner_ref, picked_ref, *, total):
@@ -224,24 +242,23 @@
     words_ref[...] = jnp.concatenate(words, 0)
 
 
-def pack(words_ref, rows_ref, sent_ref, extra_ref, *, mirrors):
+def pack(words_ref, rows_ref, extra_ref, sent_ref, *, mirrors):
     words = words_ref[...]
     sums = jnp.sum(rows_ref[...], axis=0)
     lane = lax.broadcasted_iota(jnp.int32, (1, LANES), 1)
-    line = jnp.zeros((1, LANES), jnp.float32)
+    line = extra_ref[...]
     for m in range(mirrors):
         product = jnp.zeros((1, LANES), jnp.float32)
         for k in range(words.shape[0]):
             at = k * mirrors + m
-            product = product + sums[at : at + 1] * words[k : k + 1]
+            row = sums[at // sums.shape[1], at % sums.shape[1]][None]
+            product = product + row * words[k : k + 1]
         line = jnp.where(lane == m, jnp.sum(product, axis=1, keepdims=True), line)
     high = line.astype(jnp.bfloat16).astype(jnp.float32)
     middle = (line - high).astype(jnp.bfloat16).astype(jnp.float32)
     low = line - high - middle
     rows = jnp.concatenate([words, high, middle, low, jnp.zeros_like(low)], 0)
     sent_ref[...] = jnp.broadcast_to(rows.astype(jnp.bfloat16)[None], sent_ref.shape)
-    used = words.shape[0] * mirrors
-    extra_ref[...] = sums[used : used + 1]
 
 
 def reconstruct(words_ref, cm_ref, spot_ref, sent_ref, *, rb):
@@ -281,22 +298,24 @@
     sent_ref[...] = jnp.broadcast_to(rows[None], sent_ref.shape)
 
 
-def settle(got_ref, extra_ref, state_ref, commands_ref, *, mirrors):
+def settle(got_ref, state_ref, found_ref, slopes_ref, commands_ref, *, mirrors):
+    slopes_ref[...] = found_ref[...]
     lines = state_ref.shape[0] // 3
     sums = jnp.sum(got_ref[...], axis=0)
     line = sums[lines : lines + 1]
-    extra = extra_ref[...]
+    share = 1.0 / got_ref.shape[0]
     lane = lax.broadcasted_iota(jnp.int32, line.shape, 1)
 
-    def entry(values, at):
-        return jnp.sum(jnp.where(lane == at, values, 0.0), axis=1, keepdims=True)
+    def entry(at):
+        return jnp.sum(jnp.where(lane == at, line, 0.0), axis=1, keepdims=True)
 
     owner = state_ref[:lines]
     gain = state_ref[2 * lines :]
     piston = jnp.zeros(owner.shape, jnp.float32)
     for m in range(mirrors):
-        total = entry(extra, m) - gain * entry(line, m)
-        piston = jnp.where(owner == float(m), total / entry(extra, mirrors + m), piston)
+        total = share * entry(mirrors + m) - gain * entry(m)
+        count = share * entry(2 * mirrors + m)
+        piston = jnp.where(owner == float(m), total / count, piston)
     commands = state_ref[lines : 2 * lines] - gain * sums[:lines] - piston
     acts = commands_ref.shape[0]
     for i in range(lines):
@@ -332,34 +351,50 @@
     edge = jax.ShapeDtypeStruct((layers, EDGE, pixels), screens.dtype)
     hbm = pl.BlockSpec(memory_space=pltpu.HBM)
     cm = cm_values.reshape(rowblk * positions * rb * comps, cbs)
-    outer, inner, loaded = pl.pallas_call(
-        edges,
-        in_specs=[hbm] * 2,
-        out_specs=[vmem] * 3,
-        out_shape=[edge, edge, jax.ShapeDtypeStruct(cm.shape, cm.dtype)],
-        scratch_shapes=[pltpu.SemaphoreType.DMA((2 * layers + 1,))],
+    held = owner_map.reshape(1, acts)
+    sums = 4 * mirrors
+
+    def stay(array):
+        return pltpu.with_memory_space_constraint(array, pltpu.HBM)
+
+    outer, inner, loaded, picks, spot = pl.pallas_call(
+        lambda *refs: edges(*refs, columns=tiles * subs // cbs, mirrors=mirrors),
+        in_specs=[hbm] * 4,
+        out_specs=[vmem] * 5,
+        out_shape=[
+            edge,
+            edge,
+            jax.ShapeDtypeStruct(cm.shape, cm.dtype),
+            jax.ShapeDtypeStruct((tiles * sums, cm.shape[0]), jnp.bfloat16),
+            jax.ShapeDtypeStruct((height, LANES), jnp.int32),
+        ],
+        scratch_shapes=[
+            pltpu.VMEM((positions, rowblk), jnp.int32),
+            pltpu.VMEM((1, acts), jnp.int32),
+            pltpu.SemaphoreType.DMA((2 * layers + 3,)),
+        ],
         compiler_params=limit,
         name="edges",
-    )(
-        pltpu.with_memory_space_constraint(screens, pltpu.HBM),
-        pltpu.with_memory_space_constraint(cm, pltpu.HBM),
-    )
+    )(stay(screens), stay(cm), stay(cm_columns.T), stay(held))
     outer = swap(outer, 1)
     inner = swap(inner, -1)
 
-    rows, spot, state = pl.pallas_call(
-        lambda *refs: mirror_rows(*refs, columns=tiles * subs // cbs),
+    rows, state, extra = pl.pallas_call(
+        mirror_rows,
         in_specs=[smem] + [vmem] * 4,
+        out_specs=[hbm, vmem, vmem],
         out_shape=(
-            jax.ShapeDtypeStruct((tiles, 16, LANES), f32),
-            jax.ShapeDtypeStruct((height, LANES), jnp.int32),
+            jax.ShapeDtypeStruct((tiles, sums // 4, 4, LANES), f32),
             jax.ShapeDtypeStruct((3 * lines, LANES), f32),
+            jax.ShapeDtypeStruct((1, LANES), f32),
         ),
+        scratch_shapes=[
+            pltpu.VMEM((tiles, sums // 4, 4, LANES), f32),
+            pltpu.SemaphoreType.DMA((2,)),
+        ],
         compiler_params=limit,
         name="mirror_rows",
-    )(
-        dm_gain, cm_columns.T, owner_map.reshape(1, acts), prev_commands.reshape(1, acts), loaded
-    )
+    )(dm_gain, held, prev_commands.reshape(1, acts), picks, loaded)
     foot_rows = jnp.transpose(footprint, (1, 2, 0))
     rows, foot_rows = lax.optimization_barrier((rows, foot_rows))
     rows = lax.all_to_all(rows, "tile", 0, 0)
@@ -383,16 +418,13 @@
     )(
         foot_rows, outer, interp_weights, picked, illumination, transform_table(SIDE)
     )
-    packed, extra = pl.pallas_call(
+    packed = pl.pallas_call(
         lambda *refs: pack(*refs, mirrors=mirrors),
-        in_specs=[vmem] * 2,
-        out_shape=(
-            jax.ShapeDtypeStruct((tiles, 8, LANES), jnp.bfloat16),
-            jax.ShapeDtypeStruct((1, LANES), f32),
-        ),
+        in_specs=[vmem] * 3,
+        out_shape=jax.ShapeDtypeStruct((tiles, 8, LANES), jnp.bfloat16),
         compiler_params=limit,
         name="pack",
-    )(words, rows)
+    )(words, rows, extra)
 
     gathered = lax.all_to_all(packed, "tile", 0, 0)
     sent = pl.pallas_call(
@@ -403,14 +435,16 @@
         name="reconstruct",
     )(gathered, cm, spot)
     got = lax.all_to_all(sent, "grp", 0, 0)
-    commands = pl.pallas_call(
+    return pl.pallas_call(
         lambda *refs: settle(*refs, mirrors=mirrors),
         in_specs=[vmem] * 3,
-        out_shape=jax.ShapeDtypeStruct((acts,), f32),
+        out_shape=(
+            jax.ShapeDtypeStruct((2, subs), f32),
+            jax.ShapeDtypeStruct((acts,), f32),
+        ),
         compiler_params=limit,
         name="settle",
-    )(got, extra, state)
-    return (slopes, commands)
+    )(got, state, slopes)
 
 
 def solution(mesh):

time: 47.6 us -> 46.8 us (0.983)
  Pallas kernels: 11.3 us -> 10.4 us
    pallas_call x1, Pallas kernels: 2.92 us -> 2.37 us  [on_device(): pl.pallas_call(lambda *refs: sense_rest(*refs, total=total, blocks=blk_de...]
  transfers between devices with their start and end apart: 3 -> 3, of which waited for: 1 -> 1; matrix products, arithmetic and copies ran while one was open for 0% -> 0% of each run, Pallas kernels for 16% -> 15%
where the time goes in v6:
time: 46.8 us; the launch traced here: 46.4 us
  blocking collectives  17.9 us (38%)
  starting transfers between devices  13.9 us (30%)
  Pallas kernels  10.4 us (22%)
  waiting for transfers between devices  3.31 us (7%)
  between operations  0.81 us (2%)
    all_to_all x1, blocking collectives, on_device(): gathered = lax.all_to_all(packed, 'tile', 0, 0)  11.3 us
    all_to_all x1, starting transfers between devices, on_device(): rows = lax.all_to_all(rows, 'tile', 0, 0)  11.1 us
    all_to_all x1, blocking collectives, on_device(): got = lax.all_to_all(sent, 'grp', 0, 0)  6.56 us
    all_to_all x1, waiting for transfers between devices, on_device(): rows = lax.all_to_all(rows, 'tile', 0, 0)  3.3 us
    ppermute x2, starting transfers between devices, swap(): return lax.ppermute(block, DEVICES, route)  2.76 us
    pallas_call x1, Pallas kernels, on_device(): pl.pallas_call(lambda *refs: pick_own(*refs, total=total), in_specs=[vmem...  2.54 us
    pallas_call x1, Pallas kernels, on_device(): pl.pallas_call(lambda *refs: sense_rest(*refs, total=total, blocks=blk_de...  2.37 us
    pallas_call x1, Pallas kernels, on_device(): pl.pallas_call(mirror_rows, in_specs=[smem] + [vmem] * 4, out_specs=[hbm,...  2.07 us
  transfers between devices with their start and end apart: 3, of which 1 were waited for; matrix products, arithmetic and copies ran while one was open for 0% of the time, Pallas kernels for 15%

profile of v6, /device:TPU:1, one launch (start us, length us, event | category | flops | bytes accessed | tf_op | source)
XLA Modules:
  0.0 46.4 jit_solution(1352281509504154493)
XLA Ops:
  0.6 0.0 copy-start.6
  0.6 0.0 copy-start.8
  0.7 0.0 copy-start.7
  0.7 1.6 %edges.1 = (bf16[3,256,256]{2,1,0:T(8,128)(2,1)S(1)}, bf16[3,256,256]{2,1,0:T(8,128)(2,1)S(1)}, bf16[3584,128]{1,0:T(8,128)(2,1)S(1)}, bf16[384,3584]{1,0:T(8,128)(2,1)S(1)}, s32[32,128]{1,0:T(8,128)S(1)}) custom-call(bf16[3,1024,256]{2,1,0:T(8,128)(2,1)} %refs_1_.1, bf16[3584,128]{1,0:T(8,128)(2,1)} %bitcast.5, s32[4,28]{1,0:T(4,128)} %bitcast.12, ...), custom_call_target="tpu_custom_call" | custom-call | tf_op jit(solution)/shard_map/edges/pallas_call | solution.py:360
  2.3 1.5 %collective-permute-start.1 = (bf16[3,256,256]{2,1,0:T(8,128)(2,1)S(1)}, bf16[3,256,256]{2,1,0:T(8,128)(2,1)S(1)}, u32[]{:S(2)}, u32[]{:S(2)}) collective-permute-start(bf16[3,256,256]{2,1,0:T(8,128)(2,1)S(1)} %get-tuple-element.19), channel_id=1, source_target_pairs={{0,1},{1,0},{2,3},{3,2},{4,5},{5,4},{6,7},{7,6},{8,9},{9,8},{10,11... | collective-permute-start | bytes 1179656 | tf_op jit(solution)/shard_map/ppermute | solution.py:21
  3.8 1.3 %collective-permute-start = (bf16[3,256,256]{2,1,0:T(8,128)(2,1)S(1)}, bf16[3,256,256]{2,1,0:T(8,128)(2,1)S(1)}, u32[]{:S(2)}, u32[]{:S(2)}) collective-permute-start(bf16[3,256,256]{2,1,0:T(8,128)(2,1)S(1)} %get-tuple-element.18), channel_id=1, source_target_pairs={{0,127},{1,2},{2,1},{3,4},{4,3},{5,6},{6,5},{7,8},{8,7},{9,10},{10... | collective-permute-start | bytes 1179656 | tf_op jit(solution)/shard_map/ppermute | solution.py:21
  5.1 0.0 copy-start.5
  5.1 2.1 %mirror_rows.1 = (f32[32,3,4,128]{3,2,1,0:T(4,128)}, f32[12,128]{1,0:T(8,128)S(1)}, f32[1,128]{1,0:T(1,128)S(1)}) custom-call(f32[3]{0:T(128)S(1)} %copy-done.8, s32[1,448]{1,0:T(1,128)S(1)} %bitcast.10, f32[1,448]{1,0:T(1,128)S(1)} %bitcast.11, bf16[384,3584]{1,0:T(8,128)(2,1)S(1)} %get-tuple-element.14.picks_ref, ...), custom_call_target="tpu_custom_call" | custom-call | tf_op jit(solution)/shard_map/mirror_rows/pallas_call | solution.py:382
  7.2 11.1 %all-to-all-start = ((f32[32,3,4,128]{3,2,1,0:T(4,128)}), f32[32,3,4,128]{3,2,1,0:T(4,128)S(1)}, u32[]{:S(2)}, u32[]{:S(2)}) async-start(f32[32,3,4,128]{3,2,1,0:T(4,128)} %get-tuple-element.21), calls=%async_computation | async-start | bytes 393216 | tf_op jit(solution)/shard_map/all_to_all | solution.py:400
  18.3 0.0 copy-start.2
  18.3 0.0 copy-start.3
  18.3 0.0 copy-start.4
  18.4 0.0 collective-permute-done.1.refs_2_
  18.4 2.5 %pick_own.1.refs_3_ = bf16[3,256,1024]{2,1,0:T(8,128)(2,1)S(1)} custom-call(s32[3,4,256]{2,1,0:T(4,128)S(1)} %bitcast.7, bf16[3,1024,256]{2,1,0:T(8,128)(2,1)S(1)} %copy-done, bf16[3,256,256]{2,1,0:T(8,128)(2,1)S(1)} %collective-permute-done.1.refs_2_), custom_call_target="tpu_custom_call" | custom-call | tf_op jit(solution)/shard_map/pick_own/pallas_call | solution.py:402
  20.9 0.0 copy-start.1
  21.0 0.0 collective-permute-done.refs_1_
  21.0 2.4 %sense_rest.1 = (f32[2,256]{1,0:T(2,128)S(1)}, f32[4,128]{1,0:T(4,128)S(1)}) custom-call(s32[3,4,256]{2,1,0:T(4,128)S(1)} %bitcast.8, bf16[3,256,256]{2,1,0:T(8,128)(2,1)S(1)} %collective-permute-done.refs_1_, bf16[3,4,256,256]{3,2,1,0:T(8,128)(2,1)S(1)} %copy-done.2, bf16[3,256,1024]{2,1,0:T(8,128)(2,1)S(1)} %pick_own.1.refs_3_, f32[256,256]{1,0:T(8,128)S(1)} %copy-done.4, ...), custom_call_target="tpu_custom_call" | custom-call | tf_op jit(solution)/shard_map/sense_rest/pallas_call | solution.py:409
  23.4 3.3 %all-to-all-done.refs_1_ = f32[32,3,4,128]{3,2,1,0:T(4,128)S(1)} async-done(((f32[32,3,4,128]{3,2,1,0:T(4,128)}), f32[32,3,4,128]{3,2,1,0:T(4,128)S(1)}, u32[]{:S(2)}, u32[]{:S(2)}) %all-to-all-start) | async-done | bytes 196640 | tf_op jit(solution)/shard_map/all_to_all | solution.py:400
  26.7 0.1 pack.1
  26.8 11.3 %all_to_all.15.refs_0_ = bf16[32,8,128]{2,1,0:T(8,128)(2,1)S(1)} all-to-all(bf16[32,8,128]{2,1,0:T(8,128)(2,1)S(1)} %pack.1), channel_id=1, replica_groups=mesh['grp'=4,'tile'=32] {'tile'}, dimensions={0} | all-to-all | bytes 131072 | tf_op jit(solution)/shard_map/all_to_all | solution.py:429
  38.1 0.0 copy-done.1
  38.1 1.0 %reconstruct.1 = f32[4,8,128]{2,1,0:T(8,128)S(1)} custom-call(bf16[32,8,128]{2,1,0:T(8,128)(2,1)S(1)} %all_to_all.15.refs_0_, bf16[3584,128]{1,0:T(8,128)(2,1)S(1)} %bitcast.6, s32[32,128]{1,0:T(8,128)S(1)} %get-tuple-element.23.refs_2_), custom_call_target="tpu_custom_call" | custom-call | tf_op jit(solution)/shard_map/reconstruct/pallas_call | solution.py:430
  39.1 6.6 %all_to_all.16.refs_0_ = f32[4,8,128]{2,1,0:T(8,128)S(1)} all-to-all(f32[4,8,128]{2,1,0:T(8,128)S(1)} %reconstruct.1), channel_id=1, replica_groups=mesh['grp'=4,'tile'=32] {'grp'}, dimensions={0} | all-to-all | bytes 32768 | tf_op jit(solution)/shard_map/all_to_all | solution.py:437
  45.7 0.7 %settle.1 = (f32[2,256]{1,0:T(2,128)}, f32[448]{0:T(512)}) custom-call(f32[4,8,128]{2,1,0:T(8,128)S(1)} %all_to_all.16.refs_0_, f32[12,128]{1,0:T(8,128)S(1)} %get-tuple-element.24.refs_1_, f32[2,256]{1,0:T(2,128)S(1)} %get-tuple-element.25.refs_2_), custom_call_target="tpu_custom_call" | custom-call | tf_op jit(solution)/shard_map/settle/pallas_call | solution.py:438
  (9 shorter events, 0.0 us)
Async XLA Ops:
  0.6 4.4 %copy-start.6 = (s32[448]{0:T(512)S(1)}, s32[448]{0:T(512)}, u32[]{:S(2)}) copy-start(s32[448]{0:T(512)} %param.17) | copy-start | bytes 5380
  0.6 4.4 %copy-start.8 = (f32[3]{0:T(128)S(1)}, f32[3]{0:T(128)}, u32[]{:S(2)}) copy-start(f32[3]{0:T(128)} %gain_ref.1) | copy-start | bytes 40
  0.7 4.4 %copy-start.7 = (f32[448]{0:T(512)S(1)}, f32[448]{0:T(512)}, u32[]{:S(2)}) copy-start(f32[448]{0:T(512)} %param.16) | copy-start | bytes 5380
  2.3 16.0 %collective-permute-start.1 = (bf16[3,256,256]{2,1,0:T(8,128)(2,1)S(1)}, bf16[3,256,256]{2,1,0:T(8,128)(2,1)S(1)}, u32[]{:S(2)}, u32[]{:S(2)}) collective-permute-start(bf16[3,256,256]{2,1,0:T(8,128)(2,1)S(1)} %get-tuple-element.19), channel_id=1, source_target_pairs={{0,1},{1,0},{2,3},{3,2},{4,5},{5,4},{6,7},{7,6},{8,9},{9,8},{10,11... | collective-permute-start | bytes 1179656 | tf_op jit(solution)/shard_map/ppermute | solution.py:21
  3.8 17.2 %collective-permute-start = (bf16[3,256,256]{2,1,0:T(8,128)(2,1)S(1)}, bf16[3,256,256]{2,1,0:T(8,128)(2,1)S(1)}, u32[]{:S(2)}, u32[]{:S(2)}) collective-permute-start(bf16[3,256,256]{2,1,0:T(8,128)(2,1)S(1)} %get-tuple-element.18), channel_id=1, source_target_pairs={{0,127},{1,2},{2,1},{3,4},{4,3},{5,6},{6,5},{7,8},{8,7},{9,10},{10... | collective-permute-start | bytes 1179656 | tf_op jit(solution)/shard_map/ppermute | solution.py:21
  5.1 13.3 %copy-start = (bf16[3,1024,256]{2,1,0:T(8,128)(2,1)S(1)}, bf16[3,1024,256]{2,1,0:T(8,128)(2,1)}, u32[]{:S(2)}) copy-start(bf16[3,1024,256]{2,1,0:T(8,128)(2,1)} %refs_1_.1) | copy-start | bytes 4718596
  5.1 13.3 %copy-start.5 = (s32[256,3,4]{0,2,1:T(4,128)S(1)}, s32[256,3,4]{0,2,1:T(4,128)}, u32[]{:S(2)}) copy-start(s32[256,3,4]{0,2,1:T(4,128)} %param.12) | copy-start | bytes 36868
  7.2 19.5 %all-to-all-start = ((f32[32,3,4,128]{3,2,1,0:T(4,128)}), f32[32,3,4,128]{3,2,1,0:T(4,128)S(1)}, u32[]{:S(2)}, u32[]{:S(2)}) async-start(f32[32,3,4,128]{3,2,1,0:T(4,128)} %get-tuple-element.21), calls=%async_computation | async-start | bytes 393216 | tf_op jit(solution)/shard_map/all_to_all | solution.py:400
  18.3 2.6 %copy-start.2 = (bf16[3,4,256,256]{3,2,1,0:T(8,128)(2,1)S(1)}, bf16[3,4,256,256]{3,2,1,0:T(8,128)(2,1)}, u32[]{:S(2)}) copy-start(bf16[3,4,256,256]{3,2,1,0:T(8,128)(2,1)} %refs_2_.1) | copy-start | bytes 4718596
  18.3 2.6 %copy-start.3 = (bf16[512,512]{1,0:T(8,128)(2,1)S(1)}, bf16[512,512]{1,0:T(8,128)(2,1)}, u32[]{:S(2)}) copy-start(bf16[512,512]{1,0:T(8,128)(2,1)} %constant.2.clone.refs_5_) | copy-start | bytes 1572868
  18.3 2.6 %copy-start.4 = (f32[256,256]{1,0:T(8,128)S(1)}, f32[256,256]{1,0:T(8,128)}, u32[]{:S(2)}) copy-start(f32[256,256]{1,0:T(8,128)} %refs_4_.1) | copy-start | bytes 786436
  20.9 17.2 %copy-start.1 = (bf16[28,4,16,2,128]{4,3,2,1,0:T(2,128)(2,1)S(1)}, bf16[28,4,16,2,128]{4,3,2,1,0:T(2,128)(2,1)}, u32[]{:S(2)}) copy-start(bf16[28,4,16,2,128]{4,3,2,1,0:T(2,128)(2,1)} %param.14) | copy-start | bytes 2752516

commit v7 on v6

--- a/solution.py
+++ b/solution.py
@@ -207,18 +207,12 @@
     phase = None
     for layer in range(layers):
         offsets = offsets_of(foot_ref[layer], start, total)
-        picked = []
         for k in range(foot):
             found = hits(offsets[:, k : k + 1] - first, 0, EDGE)
             rows = jnp.dot(found, outer_ref[layer], preferred_element_type=jnp.float32)
-            own = own_ref[layer, :, k * pixels : (k + 1) * pixels]
-            picked.append(rows.astype(jnp.bfloat16) + own)
-        part = jnp.dot(
-            jnp.concatenate(picked, 1),
-            weights_ref[layer].reshape(foot * pixels, pixels),
-            preferred_element_type=jnp.float32,
-        )
-        phase = part if phase is None else phase + part
+            rows = rows.astype(jnp.bfloat16) + own_ref[layer, :, k * pixels : (k + 1) * pixels]
+            part = jnp.dot(rows, weights_ref[layer, k], preferred_element_type=jnp.float32)
+            phase = part if phase is None else phase + part
     phase = phase.T
     illum = illum_ref[...].T
     sine, cosine = sine_cosine(phase)
@@ -269,15 +263,18 @@
     rowblk = cm_ref.shape[0] // LANES
     row = lax.broadcasted_iota(jnp.int32, (words.shape[0], LANES), 0)
     parts = []
-    for i in range(rowblk):
+    step = math.gcd(rowblk, 4)
+    for first in range(0, rowblk, step):
         product = lax.dot_general(
             words,
-            cm_ref[i * LANES : (i + 1) * LANES, :],
+            cm_ref[first * LANES : (first + step) * LANES, :],
             (((1,), (1,)), ((), ())),
             preferred_element_type=jnp.float32,
         )
-        chosen = jnp.where(row == spot_ref[i : i + 1, :], product, 0.0)
-        parts.append(jnp.sum(chosen, axis=0, keepdims=True))
+        for i in range(step):
+            spot = spot_ref[first + i : first + i + 1, :]
+            chosen = jnp.where(row == spot, product[:, i * LANES : (i + 1) * LANES], 0.0)
+            parts.append(jnp.sum(chosen, axis=0, keepdims=True))
     height = spot_ref.shape[0]
     if height > rowblk:
         parts.append(jnp.zeros((height - rowblk, LANES), jnp.float32))
@@ -346,6 +343,7 @@
     smem = pl.BlockSpec(memory_space=pltpu.SMEM)
     vmem = pl.BlockSpec(memory_space=pltpu.VMEM)
     limit = pltpu.CompilerParams(vmem_limit_bytes=24 * 2**20)
+    tight = pltpu.CompilerParams(vmem_limit_bytes=24 * 2**20)
     f32 = jnp.float32
 
     edge = jax.ShapeDtypeStruct((layers, EDGE, pixels), screens.dtype)
@@ -403,7 +401,7 @@
         lambda *refs: pick_own(*refs, total=total),
         in_specs=[vmem] * 3,
         out_shape=jax.ShapeDtypeStruct((layers, subs, foot * pixels), screens.dtype),
-        compiler_params=limit,
+        compiler_params=tight,
         name="pick_own",
     )(foot_rows, screens, inner)
     slopes, words = pl.pallas_call(

time: 46.8 us -> 46.4 us (level)
  no operation moved by 1% of the time
where the time goes in v7:
time: 46.4 us; the launch traced here: 46 us
  blocking collectives  17.8 us (38%)
  starting transfers between devices  13.9 us (30%)
  Pallas kernels  10 us (22%)
  waiting for transfers between devices  3.37 us (7%)
  between operations  0.81 us (2%)
    all_to_all x1, blocking collectives, on_device(): gathered = lax.all_to_all(packed, 'tile', 0, 0)  11.3 us
    all_to_all x1, starting transfers between devices, on_device(): rows = lax.all_to_all(rows, 'tile', 0, 0)  11.1 us
    all_to_all x1, blocking collectives, on_device(): got = lax.all_to_all(sent, 'grp', 0, 0)  6.56 us
    all_to_all x1, waiting for transfers between devices, on_device(): rows = lax.all_to_all(rows, 'tile', 0, 0)  3.36 us
    ppermute x2, starting transfers between devices, swap(): return lax.ppermute(block, DEVICES, route)  2.76 us
    pallas_call x1, Pallas kernels, on_device(): pl.pallas_call(lambda *refs: pick_own(*refs, total=total), in_specs=[vmem...  2.54 us
    pallas_call x1, Pallas kernels, on_device(): pl.pallas_call(lambda *refs: sense_rest(*refs, total=total, blocks=blk_de...  2.31 us
    pallas_call x1, Pallas kernels, on_device(): pl.pallas_call(mirror_rows, in_specs=[smem] + [vmem] * 4, out_specs=[hbm,...  2.07 us
  transfers between devices with their start and end apart: 3, of which 1 were waited for; matrix products, arithmetic and copies ran while one was open for 0% of the time, Pallas kernels for 15%

profile of v7, /device:TPU:1, one launch (start us, length us, event | category | flops | bytes accessed | tf_op | source)
XLA Modules:
  0.0 46.0 jit_solution(13434302842203722287)
XLA Ops:
  0.6 0.0 copy-start.6
  0.6 0.0 copy-start.8
  0.7 0.0 copy-start.7
  0.7 1.6 %edges.1 = (bf16[3,256,256]{2,1,0:T(8,128)(2,1)S(1)}, bf16[3,256,256]{2,1,0:T(8,128)(2,1)S(1)}, bf16[3584,128]{1,0:T(8,128)(2,1)S(1)}, bf16[384,3584]{1,0:T(8,128)(2,1)S(1)}, s32[32,128]{1,0:T(8,128)S(1)}) custom-call(bf16[3,1024,256]{2,1,0:T(8,128)(2,1)} %refs_1_.1, bf16[3584,128]{1,0:T(8,128)(2,1)} %bitcast.5, s32[4,28]{1,0:T(4,128)} %bitcast.12, ...), custom_call_target="tpu_custom_call" | custom-call | tf_op jit(solution)/shard_map/edges/pallas_call | solution.py:358
  2.3 1.5 %collective-permute-start.1 = (bf16[3,256,256]{2,1,0:T(8,128)(2,1)S(1)}, bf16[3,256,256]{2,1,0:T(8,128)(2,1)S(1)}, u32[]{:S(2)}, u32[]{:S(2)}) collective-permute-start(bf16[3,256,256]{2,1,0:T(8,128)(2,1)S(1)} %get-tuple-element.19), channel_id=1, source_target_pairs={{0,1},{1,0},{2,3},{3,2},{4,5},{5,4},{6,7},{7,6},{8,9},{9,8},{10,11... | collective-permute-start | bytes 1179656 | tf_op jit(solution)/shard_map/ppermute | solution.py:21
  3.8 1.3 %collective-permute-start = (bf16[3,256,256]{2,1,0:T(8,128)(2,1)S(1)}, bf16[3,256,256]{2,1,0:T(8,128)(2,1)S(1)}, u32[]{:S(2)}, u32[]{:S(2)}) collective-permute-start(bf16[3,256,256]{2,1,0:T(8,128)(2,1)S(1)} %get-tuple-element.18), channel_id=1, source_target_pairs={{0,127},{1,2},{2,1},{3,4},{4,3},{5,6},{6,5},{7,8},{8,7},{9,10},{10... | collective-permute-start | bytes 1179656 | tf_op jit(solution)/shard_map/ppermute | solution.py:21
  5.1 0.0 copy-done.6
  5.1 0.0 copy-start.5
  5.1 2.1 %mirror_rows.1 = (f32[32,3,4,128]{3,2,1,0:T(4,128)}, f32[12,128]{1,0:T(8,128)S(1)}, f32[1,128]{1,0:T(1,128)S(1)}) custom-call(f32[3]{0:T(128)S(1)} %copy-done.8, s32[1,448]{1,0:T(1,128)S(1)} %bitcast.10, f32[1,448]{1,0:T(1,128)S(1)} %bitcast.11, bf16[384,3584]{1,0:T(8,128)(2,1)S(1)} %get-tuple-element.14.picks_ref, ...), custom_call_target="tpu_custom_call" | custom-call | tf_op jit(solution)/shard_map/mirror_rows/pallas_call | solution.py:380
  7.2 11.1 %all-to-all-start = ((f32[32,3,4,128]{3,2,1,0:T(4,128)}), f32[32,3,4,128]{3,2,1,0:T(4,128)S(1)}, u32[]{:S(2)}, u32[]{:S(2)}) async-start(f32[32,3,4,128]{3,2,1,0:T(4,128)} %get-tuple-element.21), calls=%async_computation | async-start | bytes 393216 | tf_op jit(solution)/shard_map/all_to_all | solution.py:398
  18.3 0.0 copy-start.2
  18.3 0.0 copy-start.3
  18.3 0.0 copy-start.4
  18.4 0.0 collective-permute-done.1.refs_2_
  18.4 2.5 %pick_own.1.refs_3_ = bf16[3,256,1024]{2,1,0:T(8,128)(2,1)S(1)} custom-call(s32[3,4,256]{2,1,0:T(4,128)S(1)} %bitcast.7, bf16[3,1024,256]{2,1,0:T(8,128)(2,1)S(1)} %copy-done, bf16[3,256,256]{2,1,0:T(8,128)(2,1)S(1)} %collective-permute-done.1.refs_2_), custom_call_target="tpu_custom_call" | custom-call | tf_op jit(solution)/shard_map/pick_own/pallas_call | solution.py:400
  20.9 0.0 copy-start.1
  21.0 0.0 collective-permute-done.refs_1_
  21.0 2.3 %sense_rest.1 = (f32[2,256]{1,0:T(2,128)S(1)}, f32[4,128]{1,0:T(4,128)S(1)}) custom-call(s32[3,4,256]{2,1,0:T(4,128)S(1)} %bitcast.8, bf16[3,256,256]{2,1,0:T(8,128)(2,1)S(1)} %collective-permute-done.refs_1_, bf16[3,4,256,256]{3,2,1,0:T(8,128)(2,1)S(1)} %copy-done.2, bf16[3,256,1024]{2,1,0:T(8,128)(2,1)S(1)} %pick_own.1.refs_3_, f32[256,256]{1,0:T(8,128)S(1)} %copy-done.4, ...), custom_call_target="tpu_custom_call" | custom-call | tf_op jit(solution)/shard_map/sense_rest/pallas_call | solution.py:407
  23.3 3.4 %all-to-all-done.refs_1_ = f32[32,3,4,128]{3,2,1,0:T(4,128)S(1)} async-done(((f32[32,3,4,128]{3,2,1,0:T(4,128)}), f32[32,3,4,128]{3,2,1,0:T(4,128)S(1)}, u32[]{:S(2)}, u32[]{:S(2)}) %all-to-all-start) | async-done | bytes 196640 | tf_op jit(solution)/shard_map/all_to_all | solution.py:398
  26.7 0.1 pack.1
  26.8 11.3 %all_to_all.15.refs_0_ = bf16[32,8,128]{2,1,0:T(8,128)(2,1)S(1)} all-to-all(bf16[32,8,128]{2,1,0:T(8,128)(2,1)S(1)} %pack.1), channel_id=1, replica_groups=mesh['grp'=4,'tile'=32] {'tile'}, dimensions={0} | all-to-all | bytes 131072 | tf_op jit(solution)/shard_map/all_to_all | solution.py:427
  38.1 0.6 %reconstruct.1 = f32[4,8,128]{2,1,0:T(8,128)S(1)} custom-call(bf16[32,8,128]{2,1,0:T(8,128)(2,1)S(1)} %all_to_all.15.refs_0_, bf16[3584,128]{1,0:T(8,128)(2,1)S(1)} %bitcast.6, s32[32,128]{1,0:T(8,128)S(1)} %get-tuple-element.23.refs_2_), custom_call_target="tpu_custom_call" | custom-call | tf_op jit(solution)/shard_map/reconstruct/pallas_call | solution.py:428
  38.7 6.6 %all_to_all.16.refs_0_ = f32[4,8,128]{2,1,0:T(8,128)S(1)} all-to-all(f32[4,8,128]{2,1,0:T(8,128)S(1)} %reconstruct.1), channel_id=1, replica_groups=mesh['grp'=4,'tile'=32] {'grp'}, dimensions={0} | all-to-all | bytes 32768 | tf_op jit(solution)/shard_map/all_to_all | solution.py:435
  45.3 0.7 %settle.1 = (f32[2,256]{1,0:T(2,128)}, f32[448]{0:T(512)}) custom-call(f32[4,8,128]{2,1,0:T(8,128)S(1)} %all_to_all.16.refs_0_, f32[12,128]{1,0:T(8,128)S(1)} %get-tuple-element.24.refs_1_, f32[2,256]{1,0:T(2,128)S(1)} %get-tuple-element.25.refs_2_), custom_call_target="tpu_custom_call" | custom-call | tf_op jit(solution)/shard_map/settle/pallas_call | solution.py:436
  (9 shorter events, 0.0 us)
Async XLA Ops:
  0.6 4.4 %copy-start.6 = (s32[448]{0:T(512)S(1)}, s32[448]{0:T(512)}, u32[]{:S(2)}) copy-start(s32[448]{0:T(512)} %param.17) | copy-start | bytes 5380
  0.6 4.4 %copy-start.8 = (f32[3]{0:T(128)S(1)}, f32[3]{0:T(128)}, u32[]{:S(2)}) copy-start(f32[3]{0:T(128)} %gain_ref.1) | copy-start | bytes 40
  0.7 4.4 %copy-start.7 = (f32[448]{0:T(512)S(1)}, f32[448]{0:T(512)}, u32[]{:S(2)}) copy-start(f32[448]{0:T(512)} %param.16) | copy-start | bytes 5380
  2.3 16.0 %collective-permute-start.1 = (bf16[3,256,256]{2,1,0:T(8,128)(2,1)S(1)}, bf16[3,256,256]{2,1,0:T(8,128)(2,1)S(1)}, u32[]{:S(2)}, u32[]{:S(2)}) collective-permute-start(bf16[3,256,256]{2,1,0:T(8,128)(2,1)S(1)} %get-tuple-element.19), channel_id=1, source_target_pairs={{0,1},{1,0},{2,3},{3,2},{4,5},{5,4},{6,7},{7,6},{8,9},{9,8},{10,11... | collective-permute-start | bytes 1179656 | tf_op jit(solution)/shard_map/ppermute | solution.py:21
  3.8 17.2 %collective-permute-start = (bf16[3,256,256]{2,1,0:T(8,128)(2,1)S(1)}, bf16[3,256,256]{2,1,0:T(8,128)(2,1)S(1)}, u32[]{:S(2)}, u32[]{:S(2)}) collective-permute-start(bf16[3,256,256]{2,1,0:T(8,128)(2,1)S(1)} %get-tuple-element.18), channel_id=1, source_target_pairs={{0,127},{1,2},{2,1},{3,4},{4,3},{5,6},{6,5},{7,8},{8,7},{9,10},{10... | collective-permute-start | bytes 1179656 | tf_op jit(solution)/shard_map/ppermute | solution.py:21
  5.1 13.3 %copy-start = (bf16[3,1024,256]{2,1,0:T(8,128)(2,1)S(1)}, bf16[3,1024,256]{2,1,0:T(8,128)(2,1)}, u32[]{:S(2)}) copy-start(bf16[3,1024,256]{2,1,0:T(8,128)(2,1)} %refs_1_.1) | copy-start | bytes 4718596
  5.1 13.3 %copy-start.5 = (s32[256,3,4]{0,2,1:T(4,128)S(1)}, s32[256,3,4]{0,2,1:T(4,128)}, u32[]{:S(2)}) copy-start(s32[256,3,4]{0,2,1:T(4,128)} %param.12) | copy-start | bytes 36868
  7.2 19.5 %all-to-all-start = ((f32[32,3,4,128]{3,2,1,0:T(4,128)}), f32[32,3,4,128]{3,2,1,0:T(4,128)S(1)}, u32[]{:S(2)}, u32[]{:S(2)}) async-start(f32[32,3,4,128]{3,2,1,0:T(4,128)} %get-tuple-element.21), calls=%async_computation | async-start | bytes 393216 | tf_op jit(solution)/shard_map/all_to_all | solution.py:398
  18.3 2.6 %copy-start.2 = (bf16[3,4,256,256]{3,2,1,0:T(8,128)(2,1)S(1)}, bf16[3,4,256,256]{3,2,1,0:T(8,128)(2,1)}, u32[]{:S(2)}) copy-start(bf16[3,4,256,256]{3,2,1,0:T(8,128)(2,1)} %refs_2_.1) | copy-start | bytes 4718596
  18.3 2.6 %copy-start.3 = (bf16[512,512]{1,0:T(8,128)(2,1)S(1)}, bf16[512,512]{1,0:T(8,128)(2,1)}, u32[]{:S(2)}) copy-start(bf16[512,512]{1,0:T(8,128)(2,1)} %constant.2.clone.refs_5_) | copy-start | bytes 1572868
  18.3 2.6 %copy-start.4 = (f32[256,256]{1,0:T(8,128)S(1)}, f32[256,256]{1,0:T(8,128)}, u32[]{:S(2)}) copy-start(f32[256,256]{1,0:T(8,128)} %refs_4_.1) | copy-start | bytes 786436
  20.9 17.1 %copy-start.1 = (bf16[28,4,16,2,128]{4,3,2,1,0:T(2,128)(2,1)S(1)}, bf16[28,4,16,2,128]{4,3,2,1,0:T(2,128)(2,1)}, u32[]{:S(2)}) copy-start(bf16[28,4,16,2,128]{4,3,2,1,0:T(2,128)(2,1)} %param.14) | copy-start | bytes 2752516
